TPU v7x, 256 devices: a whole 4x4x8 slice. The times are simulated.
256 devices in a mesh: gr: 8 (over y, core), gc: 32 (over x, z).
Axes of the slice: x: 4, y: 4, z: 8, core: 2. Of those that a mesh axis runs over, the one named last changes fastest.
Arguments:
- below_factor: bfloat16 [31, 8, 64, 2, 32, 128], P(None, 'gr', None, None, 'gc'), may hold values from -0.046875 to 0.046875
- panel_factor: bfloat16 [31, 8, 64, 512], P(None, 'gr', 'gc'), may hold values from -0.046875 to 0.046875
- prior_factor: bfloat16 [512, 2, 32, 128], P('gr', None, 'gc'), may hold values from -0.25 to 0.25
- diag_factor: float32 [512, 512], replicated, may hold values from -1 to 3, as said below
- diag_inverse: float32 [512, 512], replicated, may hold values from -2 to 1, as said below
- below_adjoint: bfloat16 [31, 8, 64, 2, 32, 128], P(None, 'gr', None, None, 'gc'), may hold values from -6 to 6
- panel_adjoint: bfloat16 [31, 8, 64, 512], P(None, 'gr', 'gc'), may hold values from -6 to 6
- prior_adjoint: bfloat16 [512, 2, 32, 128], P('gr', None, 'gc'), may hold values from -6 to 6
- diag_adjoint: float32 [512, 512], replicated, may hold values from -6 to 6
Outputs:
- below_update: bfloat16 [31, 8, 64, 2, 32, 128], P(None, 'gr', None, None, 'gc')
- panel_gradient: bfloat16 [31, 8, 64, 512], P(None, 'gr', 'gc')
- prior_update: bfloat16 [512, 2, 32, 128], P('gr', None, 'gc')
- diag_gradient: float32 [512, 512], replicated
Inputs may be any that keep to these rules, and one draw needn't show every extreme that they name: `diag_factor`: lower triangular, diagonal entries positive. `diag_inverse`: the inverse of diag_factor.
All inputs are finite; a program needn't handle non-finite values.
Results may differ from a plain program's by a relative error of at most 0.015.
Values may be sent and summed in bfloat16 or wider, within the bound.
A program may use at most 64 MiB of HBM per device.

v0:
```python
import jax
import jax.numpy as jnp
from jax import lax
from jax.sharding import PartitionSpec as P


def row_product(left_rows, right_rows):
    return lax.dot_general(
        left_rows, right_rows, (((0,), (0,)), ((), ())), preferred_element_type=jnp.float32
    )


def diag_solve(diag_factor, diag_inverse, diag_reduced):
    highest = lax.Precision.HIGHEST
    chol_proj = jnp.dot(diag_factor.T, diag_reduced, precision=highest)
    phi_lower = jnp.tril(chol_proj) - 0.5 * jnp.diag(jnp.diagonal(chol_proj))
    symmetric = 0.5 * (phi_lower + phi_lower.T)
    left_side = jnp.dot(diag_inverse.T, symmetric, precision=highest)
    return jnp.dot(left_side, diag_inverse, precision=highest)


def local(
    below_factor,
    panel_factor,
    prior_factor,
    diag_factor,
    diag_inverse,
    below_adjoint,
    panel_adjoint,
    prior_adjoint,
    diag_adjoint,
):
    tile_count = below_factor.shape[0]
    tile_rows = below_factor.shape[2]
    local_rows = tile_count * tile_rows
    local_cols = below_factor.shape[3] * below_factor.shape[5]
    own_rows = panel_factor.shape[2]
    width = panel_factor.shape[3]
    prior_local = prior_factor.shape[0]
    below_mat = below_factor.reshape(local_rows, local_cols)
    below_bar = below_adjoint.reshape(local_rows, local_cols)
    inverse_bf = diag_inverse.astype(jnp.bfloat16)
    whole_bar, whole_factor = (
        lax.all_gather(panel_adjoint, "gc", axis=2, tiled=True),
        lax.all_gather(panel_factor, "gc", axis=2, tiled=True),
    )
    grad_rows = jnp.dot(
        whole_bar.reshape(local_rows, width), inverse_bf, preferred_element_type=jnp.float32
    ).astype(jnp.bfloat16)
    summed = lax.psum(
        row_product(grad_rows, whole_factor.reshape(local_rows, width)).astype(jnp.bfloat16), "gr"
    ).astype(jnp.float32)
    grid_col = lax.axis_index("gc")
    panel_grad = lax.dynamic_slice_in_dim(
        grad_rows.reshape(tile_count, 1, tile_rows, width), grid_col * own_rows, own_rows, 2
    )
    diag_reduced = jnp.tril(diag_adjoint - summed)
    diag_gradient = diag_solve(diag_factor, diag_inverse, diag_reduced)
    prior_here = prior_factor.reshape(prior_local, local_cols)
    prior_whole = lax.all_gather(prior_here, "gr", axis=0, tiled=True)
    below_new = (
        below_bar.astype(jnp.float32)
        - jnp.dot(grad_rows, prior_whole, preferred_element_type=jnp.float32)
    ).astype(jnp.bfloat16)
    crossing = lax.psum_scatter(
        row_product(grad_rows, below_mat).astype(jnp.bfloat16),
        "gr",
        scatter_dimension=0,
        tiled=True,
    ).astype(jnp.float32)
    grid_row = lax.axis_index("gr")
    twice_rows = lax.dynamic_slice_in_dim(
        2.0 * diag_gradient, grid_row * prior_local, prior_local, 0
    ).astype(jnp.bfloat16)
    curvature = jnp.dot(twice_rows, prior_whole, preferred_element_type=jnp.float32)
    prior_bar = prior_adjoint.reshape(prior_local, local_cols).astype(jnp.float32)
    prior_new = (prior_bar - crossing - curvature).astype(jnp.bfloat16)
    return (
        below_new.reshape(below_adjoint.shape),
        panel_grad,
        prior_new.reshape(prior_adjoint.shape),
        diag_gradient,
    )


def solution(mesh):
    in_specs = (
        P(None, "gr", None, None, "gc", None),
        P(None, "gr", "gc", None),
        P("gr", None, "gc", None),
        P(),
        P(),
        P(None, "gr", None, None, "gc", None),
        P(None, "gr", "gc", None),
        P("gr", None, "gc", None),
        P(),
    )
    out_specs = (
        P(None, "gr", None, None, "gc", None),
        P(None, "gr", "gc", None),
        P("gr", None, "gc", None),
        P(),
    )
    return jax.shard_map(local, mesh=mesh, in_specs=in_specs, out_specs=out_specs, check_vma=False)
```

profile of v0, /device:TPU:1, one launch (start us, length us, event | category | flops | bytes accessed | tf_op | source)
XLA Modules:
  0.0 280.0 jit_solution(9528895017282973600)
XLA Ops:
  7.2 0.0 all-gather.3.cloned.1.call-start
  7.2 1.6 copy.27
  8.8 0.0 all-gather.3.cloned.1.call-update
  8.8 0.0 all-gather.5.cloned.1.call-start
  8.9 1.5 copy.30
  10.3 0.0 all-gather.5.cloned.1.call-update
  10.4 0.0 all-reduce.2.cloned.1.call-start
  10.4 0.8 copy.46
  11.2 0.8 convert.3
  12.0 3.2 %convert.2 = f32[248,8,2,128]{3,2,1,0:T(2,128)} convert(bf16[248,8,2,128]{3,2,1,0:T(2,128)(2,1)} %bitcast.55) | non-fusion elementwise | flops 507904 | bytes 3047424
  15.2 15.9 %all_gather.10 = bf16[512,256]{1,0:T(8,128)(2,1)S(1)} all-gather(bf16[64,256]{1,0:T(8,128)(2,1)S(1)} %bitcast.57), channel_id=1, replica_groups=mesh['gr'=8,'gc'=32] {'gr'}, dimensions={0}, use_global_device_ids=true | all-gather | bytes 294912 | tf_op jit(solution)/shard_map/all_gather | solution.py:60
  31.1 57.9 %all-gather.3.cloned.1.call-done = bf16[31,1,64,512]{3,0,1,2:T(8,128)(2,1)} async-done(((bf16[31,1,2,512]{3,0,1,2:T(8,128)(2,1)}), bf16[31,1,64,512]{3,0,1,2:T(8,128)(2,1)}) %all-gather.3.cloned.1.call-update) | async-done | bytes 2031632 | tf_op jit(solution)/shard_map/all_gather | solution.py:44
  89.0 2.8 %copy.28 = bf16[31,1,64,512]{3,2,0,1:T(8,128)(2,1)S(1)} copy(bf16[31,1,64,512]{3,0,1,2:T(8,128)(2,1)} %all-gather.3.cloned.1.call-done) | data formatting | bytes 4063232 | tf_op jit(solution)/shard_map/all_gather | solution.py:44
  91.9 1.2 convolution_convert_fusion
  93.1 74.2 %all-gather.5.cloned.1.call-done = bf16[31,1,64,512]{3,0,1,2:T(8,128)(2,1)} async-done(((bf16[31,1,2,512]{3,0,1,2:T(8,128)(2,1)}), bf16[31,1,64,512]{3,0,1,2:T(8,128)(2,1)}) %all-gather.5.cloned.1.call-update) | async-done | bytes 2031632 | tf_op jit(solution)/shard_map/all_gather | solution.py:45
  167.3 2.7 copy.31
  170.1 2.1 convolution_convert_fusion.1
  172.1 0.0 all-reduce.2.cloned.1.call-update
  172.2 0.2 reduce-scatter.2.cloned.1.call-start
  172.4 3.2 %fusion = bf16[1984,256]{1,0:T(8,128)(2,1)} fusion(bf16[1984,512]{1,0:T(8,128)(2,1)S(1)} %convolution_convert_fusion, bf16[512,256]{1,0:T(8,128)(2,1)S(1)} %all_gather.10, f32[248,8,2,128]{3,2,1,0:T(2,128)} %convert.2), kind=kOutput, calls=%fused_computation.3 | convolution fusion | flops 521109504 | bytes 5341184 | tf_op jit(solution)/shard_map/dot_general | solution.py:63
  175.6 3.0 %reshape.38 = bf16[31,1,64,2,1,128]{5,3,2,0,4,1:T(2,128)(2,1)} reshape(bf16[1984,256]{1,0:T(8,128)(2,1)} %fusion) | data formatting | bytes 2031616 | tf_op jit(solution)/shard_map/reshape | solution.py:79
  178.7 0.7 constant_dynamic-slice_fusion
  179.4 2.7 convolution_convert_fusion.2
  182.1 55.2 %all-reduce.2.cloned.1.call-done = bf16[512,512]{1,0:T(8,128)(2,1)} async-done(((bf16[512,512]{1,0:T(8,128)(2,1)}), bf16[512,512]{1,0:T(8,128)(2,1)}) %all-reduce.2.cloned.1.call-update) | async-done | bytes 524304 | tf_op jit(solution)/shard_map/psum | solution.py:50
  237.3 3.2 %fusion.13 = f32[512,512]{1,0:T(8,128)S(1)} fusion(f32[512,512]{1,0:T(8,128)S(1)} %copy-done, f32[512,512]{1,0:T(8,128)} %param.17, bf16[512,512]{1,0:T(8,128)(2,1)} %all-reduce.2.cloned.1.call-done), kind=kOutput, calls=%fused_computation.22 | convolution fusion | flops 1611661312 | bytes 3670016 | tf_op jit(solution)/shard_map/dot_general | solution.py:15
  240.6 0.3 copy.32
  240.9 4.5 %gather_fusion = f32[512]{0:T(512)S(1)} fusion(f32[512,512]{1,0:T(8,128)S(1)} %bitcast.51, s32[512]{0:T(512)S(1)} %bitcast.50), kind=kCustom, calls=%fused_computation | custom fusion | bytes 8192 | tf_op jit(solution)/shard_map/jit(diagonal)/cond/branch_0_fun/gather | solution.py:16
  245.5 3.4 %fusion.2 = f32[512,512]{1,0:T(8,128)S(1)} fusion(f32[512,512]{1,0:T(8,128)} %param.13, f32[512,512]{1,0:T(8,128)S(1)} %fusion.13, f32[512]{0:T(512)S(1)} %gather_fusion, f32[512,512]{0,1:T(8,128)S(1)} %copy.32), kind=kOutput, calls=%fused_computation.8 | convolution fusion | flops 1614282752 | bytes 4196352 | tf_op jit(solution)/shard_map/dot_general | solution.py:18
  248.8 1.9 fusion.34
  250.8 21.1 %reduce-scatter.2.cloned.1.call-done = bf16[64,256]{1,0:T(8,128)(2,1)} async-done(((bf16[512,256]{1,0:T(8,128)(2,1)}), bf16[64,256]{1,0:T(8,128)(2,1)}) %reduce-scatter.2.cloned.1.call-update) | async-done | bytes 32784 | tf_op jit(solution)/shard_map/reduce_scatter | solution.py:65
  271.9 0.9 fusion.1
  272.8 0.6 reshape.42
  (10 shorter events, 0.0 us)
Async XLA Ops:
  7.2 230.2 %copy-start = (f32[512,512]{1,0:T(8,128)S(1)}, f32[512,512]{1,0:T(8,128)}, u32[]{:S(2)}) copy-start(f32[512,512]{1,0:T(8,128)} %param.12) | copy-start | bytes 3145732
  7.2 81.8 %all-gather.3.cloned.1.call-start = ((), (), s32[]{:S(2)}) async-start(), calls=%async_computation.1 | async-start | bytes 2162688 | tf_op jit(solution)/shard_map/all_gather | solution.py:44
  8.8 158.5 %all-gather.5.cloned.1.call-start = ((), (), s32[]{:S(2)}) async-start(), calls=%async_computation.3 | async-start | bytes 2162688 | tf_op jit(solution)/shard_map/all_gather | solution.py:45
  10.4 227.0 %all-reduce.2.cloned.1.call-start = ((), (), s32[]{:S(2)}) async-start(), calls=%async_computation.4 | async-start | bytes 1048576 | tf_op jit(solution)/shard_map/psum | solution.py:50
  89.0 2.8 %copy-start.2 = (f32[512,512]{1,0:T(8,128)S(1)}, f32[512,512]{1,0:T(8,128)}, u32[]{:S(2)}) copy-start(f32[512,512]{1,0:T(8,128)} %param.13) | copy-start | bytes 3145732
  172.2 99.7 %reduce-scatter.2.cloned.1.call-start = ((), (), s32[]{:S(2)}) async-start(), calls=%async_computation.2 | async-start | bytes 294912 | tf_op jit(solution)/shard_map/reduce_scatter | solution.py:65
  245.4 3.4 %copy-start.3 = (f32[512,512]{1,0:T(8,128)S(1)}, f32[512,512]{1,0:T(8,128)}, u32[]{:S(2)}) copy-start(f32[512,512]{1,0:T(8,128)} %param.13) | copy-start | bytes 3145732
  250.7 22.7 %copy-start.1 = (f32[512,512]{1,0:T(8,128)}, f32[512,512]{1,0:T(8,128)S(1)}, u32[]{:S(2)}) copy-start(f32[512,512]{1,0:T(8,128)S(1)} %fusion.34) | copy-start | bytes 3145732
Sparse Core Ops, SparseCore 0:
  11.2 77.7 all-gather.2
  92.2 75.1 all-gather.4
  172.3 64.9 all-reduce.1
  239.8 31.9 reduce-scatter.1
where the time goes:
time: 282 us; the launch traced here: 280 us
  waiting for transfers between devices  209 us (74%)
  local copies, waits for them, and re-layouts  18.6 us (7%)
  matrix products  18.6 us (7%)
  blocking collectives  15.9 us (6%)
  between operations  13.9 us (5%)
  other arithmetic  3.99 us (1%)
    all_gather x1, waiting for transfers between devices, local(): lax.all_gather(panel_factor, 'gc', axis=2, tiled=True)  74.2 us
    all_gather x1, waiting for transfers between devices, local(): lax.all_gather(panel_adjoint, 'gc', axis=2, tiled=True)  57.9 us
    psum x1, waiting for transfers between devices, local(): lax.psum(row_product(grad_rows, whole_factor.reshape(local_rows, width))....  55.2 us
    reduce_scatter x1, waiting for transfers between devices, local(): lax.psum_scatter(row_product(grad_rows, below_mat).astype(jnp.bfloat16),...  21.1 us
    all_gather x1, blocking collectives, local(): prior_whole = lax.all_gather(prior_here, 'gr', axis=0, tiled=True)  15.9 us
  transfers between devices with their start and end apart: 4, of which 4 were waited for; matrix products, arithmetic and copies ran while one was open for 12% of the time, Pallas kernels for 0%

commit v1 on v0

--- a/solution.py
+++ b/solution.py
@@ -1,7 +1,13 @@
+import functools
+
 import jax
 import jax.numpy as jnp
 from jax import lax
+from jax.experimental import pallas as pl
+from jax.experimental.pallas import tpu as pltpu
 from jax.sharding import PartitionSpec as P
+
+MESH_ID = pl.DeviceIdType.MESH
 
 
 def row_product(left_rows, right_rows):
@@ -19,7 +25,68 @@
     return jnp.dot(left_side, diag_inverse, precision=highest)
 
 
+def gather_kernel(n, x_ref, out_ref, send_sem, recv_sem, local_sem):
+    me = lax.axis_index("gc")
+    row = lax.axis_index("gr")
+    rows = x_ref.shape[1]
+
+    barrier = pltpu.get_barrier_semaphore()
+
+    def greet(k, carry):
+        peer = lax.rem(me + k, n)
+        pl.semaphore_signal(barrier, inc=1, device_id=(row, peer), device_id_type=MESH_ID)
+        return carry
+
+    lax.fori_loop(1, n, greet, 0)
+    pl.semaphore_wait(barrier, n - 1)
+
+    own = pltpu.make_async_copy(x_ref, out_ref.at[:, pl.ds(me * rows, rows), :], local_sem)
+    own.start()
+
+    def remote(k, sender):
+        peer = lax.rem(me + k, n)
+        return pltpu.make_async_remote_copy(
+            src_ref=x_ref,
+            dst_ref=out_ref.at[:, pl.ds(sender * rows, rows), :],
+            send_sem=send_sem.at[k],
+            recv_sem=recv_sem.at[sender],
+            device_id=(row, peer),
+            device_id_type=MESH_ID,
+        )
+
+    def send(k, carry):
+        remote(k, me).start()
+        return carry
+
+    lax.fori_loop(1, n, send, 0)
+
+    def wait(k, carry):
+        remote(k, me).wait_send()
+        remote(k, lax.rem(me + n - k, n)).wait_recv()
+        return carry
+
+    lax.fori_loop(1, n, wait, 0)
+    own.wait()
+
+
+def gather_gc(block, n):
+    tiles, rows, width = block.shape
+    return pl.pallas_call(
+        functools.partial(gather_kernel, n),
+        out_shape=jax.ShapeDtypeStruct((tiles, rows * n, width), block.dtype),
+        in_specs=[pl.BlockSpec(memory_space=pl.ANY)],
+        out_specs=pl.BlockSpec(memory_space=pl.ANY),
+        scratch_shapes=[
+            pltpu.SemaphoreType.DMA((n,)),
+            pltpu.SemaphoreType.DMA((n,)),
+            pltpu.SemaphoreType.DMA,
+        ],
+        compiler_params=pltpu.CompilerParams(collective_id=0, has_side_effects=True),
+    )(block)
+
+
 def local(
+    n_gc,
     below_factor,
     panel_factor,
     prior_factor,
@@ -40,19 +107,21 @@
     below_mat = below_factor.reshape(local_rows, local_cols)
     below_bar = below_adjoint.reshape(local_rows, local_cols)
     inverse_bf = diag_inverse.astype(jnp.bfloat16)
-    whole_bar, whole_factor = (
-        lax.all_gather(panel_adjoint, "gc", axis=2, tiled=True),
-        lax.all_gather(panel_factor, "gc", axis=2, tiled=True),
+    own_grad = jnp.dot(
+        panel_adjoint.reshape(tile_count * own_rows, width),
+        inverse_bf,
+        preferred_element_type=jnp.float32,
+    ).astype(jnp.bfloat16)
+    panel_grad = own_grad.reshape(panel_adjoint.shape)
+    both = jnp.concatenate(
+        [own_grad.reshape(tile_count, own_rows, width), panel_factor.reshape(tile_count, own_rows, width)],
+        axis=2,
     )
-    grad_rows = jnp.dot(
-        whole_bar.reshape(local_rows, width), inverse_bf, preferred_element_type=jnp.float32
-    ).astype(jnp.bfloat16)
-    summed = lax.psum(
-        row_product(grad_rows, whole_factor.reshape(local_rows, width)).astype(jnp.bfloat16), "gr"
-    ).astype(jnp.float32)
-    grid_col = lax.axis_index("gc")
-    panel_grad = lax.dynamic_slice_in_dim(
-        grad_rows.reshape(tile_count, 1, tile_rows, width), grid_col * own_rows, own_rows, 2
+    whole = gather_gc(both, n_gc)
+    grad_rows = whole[:, :, :width].reshape(local_rows, width)
+    whole_factor = whole[:, :, width:].reshape(local_rows, width)
+    summed = lax.psum(row_product(grad_rows, whole_factor).astype(jnp.bfloat16), "gr").astype(
+        jnp.float32
     )
     diag_reduced = jnp.tril(diag_adjoint - summed)
     diag_gradient = diag_solve(diag_factor, diag_inverse, diag_reduced)
@@ -101,4 +170,10 @@
         P("gr", None, "gc", None),
         P(),
     )
-    return jax.shard_map(local, mesh=mesh, in_specs=in_specs, out_specs=out_specs, check_vma=False)
+    return jax.shard_map(
+        functools.partial(local, mesh.shape["gc"]),
+        mesh=mesh,
+        in_specs=in_specs,
+        out_specs=out_specs,
+        check_vma=False,
+    )

time: 282 us -> 227 us (0.80)
  waiting for transfers between devices: 209 us -> 57.7 us
  Pallas kernels: 0 us -> 103 us
  local copies, waits for them, and re-layouts: 18.6 us -> 13.4 us
    all_gather x2 -> x0, waiting for transfers between devices: 132 us -> none  [the longest x1 74.2 us: local(): lax.all_gather(panel_factor, 'gc', axis=2, tiled=True)]
    pallas_call x0 -> x1, Pallas kernels: none -> 103 us  [gather_gc(): pl.pallas_call(functools.partial(gather_kernel, n), out_shape=jax.ShapeDt...]
    psum x1, waiting for transfers between devices: 55.2 us -> 38.3 us  [local(): lax.psum(row_product(grad_rows, whole_factor).astype(jnp.bfloat16), 'gr')]
    all_gather x2 -> x0, local copies, waits for them, and re-layouts: 5.59 us -> none  [the longest x1 2.84 us: local(): lax.all_gather(panel_adjoint, 'gc', axis=2, tiled=True)]
    unnamed x11 -> x15, local copies, waits for them, and re-layouts: 3.82 us -> 0.07 us
  transfers between devices with their start and end apart: 4 -> 2, of which waited for: 4 -> 2; matrix products, arithmetic and copies ran while one was open for 12% -> 12% of each run, Pallas kernels for 0% -> 0%
where the time goes in v1:
time: 227 us; the launch traced here: 225 us
  Pallas kernels  103 us (45%)
  waiting for transfers between devices  57.7 us (25%)
  matrix products  18.9 us (8%)
  blocking collectives  14.4 us (6%)
  between operations  14.2 us (6%)
  local copies, waits for them, and re-layouts  13.4 us (6%)
  other arithmetic  3.55 us (2%)
    pallas_call x1, Pallas kernels, gather_gc(): pl.pallas_call(functools.partial(gather_kernel, n), out_shape=jax.ShapeDt...  103 us
    psum x1, waiting for transfers between devices, local(): lax.psum(row_product(grad_rows, whole_factor).astype(jnp.bfloat16), 'gr')  38.3 us
    reduce_scatter x1, waiting for transfers between devices, local(): lax.psum_scatter(row_product(grad_rows, below_mat).astype(jnp.bfloat16),...  19.3 us
    all_gather x1, blocking collectives, local(): prior_whole = lax.all_gather(prior_here, 'gr', axis=0, tiled=True)  14.4 us
    dot_general x2, matrix products, row_product(): lax.dot_general(left_rows, right_rows, (((0,), (0,)), ((), ())), preferre...  5.77 us
  transfers between devices with their start and end apart: 2, of which 2 were waited for; matrix products, arithmetic and copies ran while one was open for 12% of the time, Pallas kernels for 0%

profile of v1, /device:TPU:1, one launch (start us, length us, event | category | flops | bytes accessed | tf_op | source)
XLA Modules:
  0.0 224.8 jit_solution(16987240041778669863)
XLA Ops:
  7.2 0.0 copy-start
  7.2 0.0 all-reduce.2.cloned.1.call-start
  7.2 0.9 reshape.43
  8.2 1.4 convolution_convert_fusion.1
  9.7 1.6 pad_maximum_fusion.x_ref
  11.3 102.6 %shard_map.120 = bf16[31,64,1024]{2,1,0:T(8,128)(2,1)} custom-call(bf16[31,2,1024]{2,1,0:T(2,128)(2,1)} %pad_maximum_fusion.x_ref), custom_call_target="tpu_custom_call" | custom-call | tf_op jit(solution)/shard_map/pallas_call | solution.py:74
  113.8 4.3 %fusion.6 = bf16[512,512]{1,0:T(8,128)(2,1)} fusion(bf16[31,64,1024]{2,1,0:T(8,128)(2,1)} %shard_map.120), kind=kOutput, calls=%fused_computation.6 | convolution fusion | flops 1040449536 | bytes 4587520 | tf_op jit(solution)/shard_map/dot_general | solution.py:14
  118.1 0.0 all-reduce.2.cloned.1.call-update
  118.1 0.0 reduce-scatter.2.cloned.1.call-start
  118.2 0.0 copy-start.6
  118.2 1.8 slice.6
  120.0 0.0 copy-done.6
  120.0 1.5 convolution_convert_fusion
  121.5 0.0 reduce-scatter.2.cloned.1.call-update
  121.5 0.7 reshape.49
  122.2 0.0 copy-done.5
  122.2 14.4 %all_gather.3 = bf16[512,256]{1,0:T(8,128)(2,1)S(1)} all-gather(bf16[64,256]{1,0:T(8,128)(2,1)S(1)} %bitcast.56), channel_id=1, replica_groups=mesh['gr'=8,'gc'=32] {'gr'}, dimensions={0}, use_global_device_ids=true | all-gather | bytes 294912 | tf_op jit(solution)/shard_map/all_gather | solution.py:129
  136.6 0.0 copy-done.4
  136.6 1.9 convert.2
  138.6 1.6 fusion
  140.2 3.1 %reshape.48 = bf16[31,1,64,2,1,128]{5,3,2,0,4,1:T(2,128)(2,1)} reshape(bf16[1984,256]{1,0:T(8,128)(2,1)} %fusion) | data formatting | bytes 2031616 | tf_op jit(solution)/shard_map/reshape | solution.py:148
  143.4 38.3 %all-reduce.2.cloned.1.call-done = bf16[512,512]{1,0:T(8,128)(2,1)} async-done(((bf16[512,512]{1,0:T(8,128)(2,1)}), bf16[512,512]{1,0:T(8,128)(2,1)}) %all-reduce.2.cloned.1.call-update) | async-done | bytes 524304 | tf_op jit(solution)/shard_map/psum | solution.py:123
  181.7 3.9 %fusion.21 = f32[512,512]{1,0:T(8,128)} fusion(f32[512,512]{1,0:T(8,128)S(1)} %copy-done, f32[512,512]{1,0:T(8,128)S(1)} %copy-done.3, bf16[512,512]{1,0:T(8,128)(2,1)} %all-reduce.2.cloned.1.call-done), kind=kOutput, calls=%fused_computation.25 | convolution fusion | flops 1611661312 | bytes 3670016 | tf_op jit(solution)/shard_map/dot_general | solution.py:21
  185.6 1.6 copy.17
  187.3 4.5 %gather_fusion = f32[512]{0:T(512)S(1)} fusion(f32[512,512]{1,0:T(8,128)S(1)} %bitcast.51, s32[512]{0:T(512)S(1)} %bitcast.50), kind=kCustom, calls=%fused_computation | custom fusion | bytes 8192 | tf_op jit(solution)/shard_map/jit(diagonal)/cond/branch_0_fun/gather | solution.py:22
  191.8 0.0 copy-done.1
  191.8 3.3 %fusion.10 = f32[512,512]{1,0:T(8,128)S(1)} fusion(f32[512,512]{1,0:T(8,128)S(1)} %copy-done.1, f32[512,512]{1,0:T(8,128)} %fusion.21, f32[512]{0:T(512)S(1)} %gather_fusion, f32[512,512]{0,1:T(8,128)S(1)} %copy.17), kind=kOutput, calls=%fused_computation.11 | convolution fusion | flops 1614282752 | bytes 4196352 | tf_op jit(solution)/shard_map/dot_general | solution.py:24
  195.1 1.9 fusion.43
  197.0 0.0 copy-start.2
  197.0 19.3 %reduce-scatter.2.cloned.1.call-done = bf16[64,256]{1,0:T(8,128)(2,1)} async-done(((bf16[512,256]{1,0:T(8,128)(2,1)}), bf16[64,256]{1,0:T(8,128)(2,1)}) %reduce-scatter.2.cloned.1.call-update) | async-done | bytes 32784 | tf_op jit(solution)/shard_map/reduce_scatter | solution.py:134
  216.4 0.9 fusion.9
  217.3 0.6 reshape.51
  (11 shorter events, 0.1 us)
Async XLA Ops:
  7.2 174.5 %copy-start = (f32[512,512]{1,0:T(8,128)S(1)}, f32[512,512]{1,0:T(8,128)}, u32[]{:S(2)}) copy-start(f32[512,512]{1,0:T(8,128)} %param.12) | copy-start | bytes 3145732
  7.2 174.5 %all-reduce.2.cloned.1.call-start = ((), (), s32[]{:S(2)}) async-start(), calls=%async_computation.2 | async-start | bytes 1048576 | tf_op jit(solution)/shard_map/psum | solution.py:123
  118.1 98.2 %reduce-scatter.2.cloned.1.call-start = ((), (), s32[]{:S(2)}) async-start(), calls=%async_computation.1 | async-start | bytes 294912 | tf_op jit(solution)/shard_map/reduce_scatter | solution.py:134
  118.2 1.8 copy-start.6
  120.0 2.2 copy-start.5
  120.0 16.6 %copy-start.4 = (bf16[64,2,1,128]{3,1,2,0:T(2,128)(2,1)S(1)}, bf16[64,2,1,128]{3,1,2,0:T(2,128)(2,1)}, u32[]{:S(2)}) copy-start(bf16[64,2,1,128]{3,1,2,0:T(2,128)(2,1)} %param.16) | copy-start | bytes 98308
  140.2 41.5 %copy-start.3 = (f32[512,512]{1,0:T(8,128)S(1)}, f32[512,512]{1,0:T(8,128)}, u32[]{:S(2)}) copy-start(f32[512,512]{1,0:T(8,128)} %param.17) | copy-start | bytes 3145732
  185.6 6.2 %copy-start.1 = (f32[512,512]{1,0:T(8,128)S(1)}, f32[512,512]{1,0:T(8,128)}, u32[]{:S(2)}) copy-start(f32[512,512]{1,0:T(8,128)} %param.13) | copy-start | bytes 3145732
  197.0 20.9 %copy-start.2 = (f32[512,512]{1,0:T(8,128)}, f32[512,512]{1,0:T(8,128)S(1)}, u32[]{:S(2)}) copy-start(f32[512,512]{1,0:T(8,128)S(1)} %fusion.43) | copy-start | bytes 3145732
Sparse Core Ops, SparseCore 0:
  118.2 63.3 all-reduce.1
  184.3 31.9 reduce-scatter.1

commit v2 on v1

--- a/solution.py
+++ b/solution.py
@@ -85,8 +85,119 @@
     )(block)
 
 
+def reduce_kernel(n, part_ref, prior_ref, cross_out, prior_out, crossing_out,
+                  recv_part, cross_slots, prior_slots, sems):
+    me = lax.axis_index("gr")
+    col = lax.axis_index("gc")
+    rows = prior_ref.shape[0]
+    wide = cross_out.shape[2]
+
+    barrier = pltpu.get_barrier_semaphore()
+
+    def greet(k, carry):
+        peer = lax.rem(me + k, n)
+        pl.semaphore_signal(barrier, inc=1, device_id=(peer, col), device_id_type=MESH_ID)
+        return carry
+
+    lax.fori_loop(1, n, greet, 0)
+    pl.semaphore_wait(barrier, n - 1)
+
+    def prior_copy(k, sender):
+        return pltpu.make_async_remote_copy(
+            src_ref=prior_ref,
+            dst_ref=prior_slots.at[sender],
+            send_sem=sems.at[0, k],
+            recv_sem=sems.at[1, sender],
+            device_id=(lax.rem(me + k, n), col),
+            device_id_type=MESH_ID,
+        )
+
+    def part_copy(k, sender):
+        peer = lax.rem(me + k, n)
+        return pltpu.make_async_remote_copy(
+            src_ref=part_ref.at[pl.ds(pl.multiple_of(peer * rows, rows), rows), :],
+            dst_ref=recv_part.at[sender],
+            send_sem=sems.at[2, k],
+            recv_sem=sems.at[3, sender],
+            device_id=(peer, col),
+            device_id_type=MESH_ID,
+        )
+
+    def cross_copy(k, sender):
+        return pltpu.make_async_remote_copy(
+            src_ref=cross_slots.at[me],
+            dst_ref=cross_slots.at[sender],
+            send_sem=sems.at[4, k],
+            recv_sem=sems.at[5, sender],
+            device_id=(lax.rem(me + k, n), col),
+            device_id_type=MESH_ID,
+        )
+
+    def send_first(k, carry):
+        prior_copy(k, me).start()
+        part_copy(k, me).start()
+        return carry
+
+    lax.fori_loop(1, n, send_first, 0)
+    prior_slots[me] = prior_ref[...]
+
+    acc = part_ref[pl.ds(pl.multiple_of(me * rows, rows), rows), :].astype(jnp.float32)
+
+    def add(k, total):
+        sender = lax.rem(me + n - k, n)
+        part_copy(k, me).wait_send()
+        part_copy(k, sender).wait_recv()
+        return total + recv_part[sender].astype(jnp.float32)
+
+    acc = lax.fori_loop(1, n, add, acc)
+    crossing_out[...] = acc[:, wide:]
+    cross_slots[me] = acc[:, :wide].astype(cross_slots.dtype)
+
+    def send_second(k, carry):
+        cross_copy(k, me).start()
+        return carry
+
+    lax.fori_loop(1, n, send_second, 0)
+
+    def wait_second(k, carry):
+        sender = lax.rem(me + n - k, n)
+        cross_copy(k, me).wait_send()
+        cross_copy(k, sender).wait_recv()
+        prior_copy(k, me).wait_send()
+        prior_copy(k, sender).wait_recv()
+        return carry
+
+    lax.fori_loop(1, n, wait_second, 0)
+    cross_out[...] = cross_slots[...]
+    prior_out[...] = prior_slots[...]
+
+
+def reduce_gr(part, prior_rows, n):
+    rows, cols = prior_rows.shape
+    wide = part.shape[1] - cols
+    vmem = pl.BlockSpec(memory_space=pltpu.VMEM)
+    return pl.pallas_call(
+        functools.partial(reduce_kernel, n),
+        out_shape=(
+            jax.ShapeDtypeStruct((n, rows, wide), part.dtype),
+            jax.ShapeDtypeStruct((n, rows, cols), prior_rows.dtype),
+            jax.ShapeDtypeStruct((rows, cols), jnp.float32),
+        ),
+        in_specs=[vmem, vmem],
+        out_specs=(vmem, vmem, vmem),
+        scratch_shapes=[
+            pltpu.VMEM((n, rows, part.shape[1]), part.dtype),
+            pltpu.VMEM((n, rows, wide), part.dtype),
+            pltpu.VMEM((n, rows, cols), prior_rows.dtype),
+            pltpu.SemaphoreType.DMA((6, n)),
+        ],
+        compiler_params=pltpu.CompilerParams(collective_id=1, has_side_effects=True),
+    )(part, prior_rows)
+
+
 def local(
     n_gc,
+    n_gr,
     below_factor,
     panel_factor,
     prior_factor,
@@ -120,23 +231,19 @@
     whole = gather_gc(both, n_gc)
     grad_rows = whole[:, :, :width].reshape(local_rows, width)
     whole_factor = whole[:, :, width:].reshape(local_rows, width)
-    summed = lax.psum(row_product(grad_rows, whole_factor).astype(jnp.bfloat16), "gr").astype(
-        jnp.float32
-    )
+    prior_here = prior_factor.reshape(prior_local, local_cols)
+    part = jnp.concatenate(
+        [row_product(grad_rows, whole_factor), row_product(grad_rows, below_mat)], axis=1
+    ).astype(jnp.bfloat16)
+    cross_rows, prior_rows, crossing = reduce_gr(part, prior_here, n_gr)
+    summed = cross_rows.reshape(width, width).astype(jnp.float32)
+    prior_whole = prior_rows.reshape(width, local_cols)
     diag_reduced = jnp.tril(diag_adjoint - summed)
     diag_gradient = diag_solve(diag_factor, diag_inverse, diag_reduced)
-    prior_here = prior_factor.reshape(prior_local, local_cols)
-    prior_whole = lax.all_gather(prior_here, "gr", axis=0, tiled=True)
     below_new = (
         below_bar.astype(jnp.float32)
         - jnp.dot(grad_rows, prior_whole, preferred_element_type=jnp.float32)
     ).astype(jnp.bfloat16)
-    crossing = lax.psum_scatter(
-        row_product(grad_rows, below_mat).astype(jnp.bfloat16),
-        "gr",
-        scatter_dimension=0,
-        tiled=True,
-    ).astype(jnp.float32)
     grid_row = lax.axis_index("gr")
     twice_rows = lax.dynamic_slice_in_dim(
         2.0 * diag_gradient, grid_row * prior_local, prior_local, 0
@@ -171,7 +278,7 @@
         P(),
     )
     return jax.shard_map(
-        functools.partial(local, mesh.shape["gc"]),
+        functools.partial(local, mesh.shape["gc"], mesh.shape["gr"]),
         mesh=mesh,
         in_specs=in_specs,
         out_specs=out_specs,

time: 227 us -> 168 us (0.74)
  waiting for transfers between devices: 57.7 us -> 0 us
  Pallas kernels: 103 us -> 129 us
  blocking collectives: 14.4 us -> 0 us
  between operations: 14.2 us -> 0.85 us
  local copies, waits for them, and re-layouts: 13.4 us -> 16.1 us
  matrix products: 18.9 us -> 16.4 us
    psum x1 -> x0, waiting for transfers between devices: 38.3 us -> none  [local(): lax.psum(row_product(grad_rows, whole_factor).astype(jnp.bfloat16), 'gr')]
    pallas_call x0 -> x1, Pallas kernels: none -> 26.8 us  [reduce_gr(): pl.pallas_call(functools.partial(reduce_kernel, n), out_shape=(jax.ShapeD...]
    reduce_scatter x1 -> x0, waiting for transfers between devices: 19.3 us -> none  [local(): lax.psum_scatter(row_product(grad_rows, below_mat).astype(jnp.bfloat16),...]
    all_gather x1 -> x0, blocking collectives: 14.4 us -> none  [local(): prior_whole = lax.all_gather(prior_here, 'gr', axis=0, tiled=True)]
    dot_general x2, matrix products: 5.77 us -> 2.03 us  [row_product(): lax.dot_general(left_rows, right_rows, (((0,), (0,)), ((), ())), preferre...]
    unnamed x15 -> x23, local copies, waits for them, and re-layouts: 0.07 us -> 2.78 us
  transfers between devices with their start and end apart: 2 -> 0, of which waited for: 2 -> 0; matrix products, arithmetic and copies ran while one was open for 12% -> 0% of each run, Pallas kernels for 0% -> 0%
where the time goes in v2:
time: 168 us; the launch traced here: 167 us
  Pallas kernels  129 us (77%)
  matrix products  16.4 us (10%)
  local copies, waits for them, and re-layouts  16.1 us (10%)
  other arithmetic  4.47 us (3%)
    pallas_call x1, Pallas kernels, gather_gc(): pl.pallas_call(functools.partial(gather_kernel, n), out_shape=jax.ShapeDt...  103 us
    pallas_call x1, Pallas kernels, reduce_gr(): pl.pallas_call(functools.partial(reduce_kernel, n), out_shape=(jax.ShapeD...  26.8 us
    gather x1, local copies, waits for them, and re-layouts, diag_solve(): phi_lower = jnp.tril(chol_proj) - 0.5 * jnp.diag(jnp.diagonal(chol_proj))  4.52 us
    dot_general x1, matrix products, diag_solve(): chol_proj = jnp.dot(diag_factor.T, diag_reduced, precision=highest)  3.9 us

profile of v2, /device:TPU:1, one launch (start us, length us, event | category | flops | bytes accessed | tf_op | source)
XLA Modules:
  0.0 167.2 jit_solution(13835443683003393287)
XLA Ops:
  0.6 0.0 copy-start
  0.6 1.0 reshape.49
  1.6 1.4 convolution_convert_fusion.1
  3.1 1.6 pad_maximum_fusion.1.x_ref
  4.7 102.5 %shard_map.120 = bf16[31,64,1024]{2,1,0:T(8,128)(2,1)} custom-call(bf16[31,2,1024]{2,1,0:T(2,128)(2,1)} %pad_maximum_fusion.1.x_ref), custom_call_target="tpu_custom_call" | custom-call | tf_op jit(solution)/shard_map/pallas_call | solution.py:74
  107.2 0.0 copy-start.10
  107.2 1.9 %slice.6 = bf16[31,64,512]{2,1,0:T(8,128)(2,1)S(1)} slice(bf16[31,64,1024]{2,1,0:T(8,128)(2,1)} %shard_map.120), slice={[0:31], [0:64], [0:512]} | slice | bytes 4063232 | tf_op jit(solution)/shard_map/slice | solution.py:232
  109.1 0.0 copy-start.2
  109.1 0.0 copy-done.10
  109.1 0.0 copy-start.1
  109.1 0.8 convolution_convert_fusion
  109.9 0.5 copy-done.2
  110.4 1.6 copy-done.1
  112.0 1.3 fusion.6
  113.3 0.0 copy-start.5
  113.3 0.9 pad_maximum_fusion.part_ref
  114.2 0.0 copy-done.9
  114.2 0.6 copy.39
  114.9 26.8 %shard_map.121 = (bf16[8,64,512]{2,1,0:T(8,128)(2,1)}, bf16[8,64,256]{2,1,0:T(8,128)(2,1)}, f32[64,256]{1,0:T(8,128)}) custom-call(bf16[512,768]{1,0:T(8,128)(2,1)} %pad_maximum_fusion.part_ref, bf16[64,256]{1,0:T(8,128)(2,1)} %bitcast.62), custom_call_target="tpu_custom_call" | custom-call | tf_op jit(solution)/shard_map/pallas_call | solution.py:179
  141.7 0.0 copy-done
  141.7 3.9 %fusion.11 = f32[512,512]{1,0:T(8,128)} fusion(f32[512,512]{1,0:T(8,128)S(1)} %copy-done, f32[512,512]{1,0:T(8,128)S(1)} %copy-done.5, bf16[512,512]{1,0:T(8,128)(2,1)} %bitcast.61), kind=kOutput, calls=%fused_computation.13 | convolution fusion | flops 1611661312 | bytes 3670016 | tf_op jit(solution)/shard_map/dot_general | solution.py:21
  145.6 1.6 copy.21
  147.3 4.5 %gather_fusion = f32[512]{0:T(512)S(1)} fusion(f32[512,512]{1,0:T(8,128)S(1)} %bitcast.54, s32[512]{0:T(512)S(1)} %bitcast.53), kind=kCustom, calls=%fused_computation | custom fusion | bytes 8192 | tf_op jit(solution)/shard_map/jit(diagonal)/cond/branch_0_fun/gather | solution.py:22
  151.8 3.3 %fusion.13 = f32[512,512]{1,0:T(8,128)S(1)} fusion(f32[512,512]{1,0:T(8,128)S(1)} %copy-done.4, f32[512,512]{1,0:T(8,128)} %fusion.11, f32[512]{0:T(512)S(1)} %gather_fusion, f32[512,512]{0,1:T(8,128)S(1)} %copy.21), kind=kOutput, calls=%fused_computation.14 | convolution fusion | flops 1614282752 | bytes 4196352 | tf_op jit(solution)/shard_map/dot_general | solution.py:24
  155.1 0.0 copy-start.8
  155.1 2.9 %fusion.42 = f32[512,512]{1,0:T(8,128)} fusion(f32[512,512]{1,0:T(8,128)S(1)} %fusion.13, f32[512,512]{1,0:T(8,128)S(1)} %copy-done.4), kind=kOutput, calls=%fused_computation.52 | convolution fusion | flops 1610612736 | bytes 3145728 | tf_op jit(solution)/shard_map/dot_general | solution.py:25
  158.1 1.2 fusion.9
  159.3 0.6 reshape.58
  159.9 1.9 %convert.18 = f32[248,8,2,128]{3,2,1,0:T(2,128)S(1)} convert(bf16[248,8,2,128]{3,2,1,0:T(2,128)(2,1)} %bitcast.59) | non-fusion elementwise | flops 507904 | bytes 3047424
  161.8 1.6 fusion
  163.5 3.0 %reshape.56 = bf16[31,1,64,2,1,128]{5,3,2,0,4,1:T(2,128)(2,1)} reshape(bf16[1984,256]{1,0:T(8,128)(2,1)} %fusion) | data formatting | bytes 2031616 | tf_op jit(solution)/shard_map/reshape | solution.py:255
  166.5 0.7 reshape.57
  (14 shorter events, 0.1 us)
Async XLA Ops:
  0.6 141.1 %copy-start = (f32[512,512]{1,0:T(8,128)S(1)}, f32[512,512]{1,0:T(8,128)}, u32[]{:S(2)}) copy-start(f32[512,512]{1,0:T(8,128)} %param.12) | copy-start | bytes 3145732
  107.2 1.9 %copy-start.10 = (bf16[31,1,64,2,1,128]{5,3,4,2,1,0:T(2,128)(2,1)S(1)}, bf16[31,1,64,2,1,128]{5,3,4,2,1,0:T(2,128)(2,1)}, u32[]{:S(2)}) copy-start(bf16[31,1,64,2,1,128]{5,3,4,2,1,0:T(2,128)(2,1)} %param.9) | copy-start | bytes 3047428
  109.1 1.3 copy-start.2
  109.1 2.9 %copy-start.1 = (bf16[31,64,1024]{2,1,0:T(8,128)(2,1)S(1)}, bf16[31,64,1024]{2,1,0:T(8,128)(2,1)}, u32[]{:S(2)}) copy-start(bf16[31,64,1024]{2,1,0:T(8,128)(2,1)} %shard_map.120) | copy-start | bytes 12189700
  112.0 2.2 %copy-start.9 = (bf16[64,2,1,128]{3,1,2,0:T(2,128)(2,1)S(1)}, bf16[64,2,1,128]{3,1,2,0:T(2,128)(2,1)}, u32[]{:S(2)}) copy-start(bf16[64,2,1,128]{3,1,2,0:T(2,128)(2,1)} %param.11) | copy-start | bytes 98308
  113.3 28.4 %copy-start.5 = (f32[512,512]{1,0:T(8,128)S(1)}, f32[512,512]{1,0:T(8,128)}, u32[]{:S(2)}) copy-start(f32[512,512]{1,0:T(8,128)} %param.17) | copy-start | bytes 3145732
  145.6 6.2 %copy-start.4 = (f32[512,512]{1,0:T(8,128)S(1)}, f32[512,512]{1,0:T(8,128)}, u32[]{:S(2)}) copy-start(f32[512,512]{1,0:T(8,128)} %param.13) | copy-start | bytes 3145732
  155.1 2.9 %copy-start.8 = (bf16[64,2,1,128]{3,1,2,0:T(2,128)(2,1)S(1)}, bf16[64,2,1,128]{3,1,2,0:T(2,128)(2,1)}, u32[]{:S(2)}) copy-start(bf16[64,2,1,128]{3,1,2,0:T(2,128)(2,1)} %param.16) | copy-start | bytes 98308
  155.1 2.9 %copy-start.6 = (bf16[8,64,256]{2,1,0:T(8,128)(2,1)S(1)}, bf16[8,64,256]{2,1,0:T(8,128)(2,1)}, u32[]{:S(2)}) copy-start(bf16[8,64,256]{2,1,0:T(8,128)(2,1)} %get-tuple-element.7) | copy-start | bytes 786436
  155.1 2.9 %copy-start.7 = (f32[64,256]{1,0:T(8,128)S(1)}, f32[64,256]{1,0:T(8,128)}, u32[]{:S(2)}) copy-start(f32[64,256]{1,0:T(8,128)} %get-tuple-element.8) | copy-start | bytes 196612
  158.0 3.8 %copy-start.3 = (bf16[31,64,512]{2,1,0:T(8,128)(2,1)S(1)}, bf16[31,64,512]{2,1,0:T(8,128)(2,1)}, u32[]{:S(2)}) copy-start(bf16[31,64,512]{2,1,0:T(8,128)(2,1)} %copy-done.2) | copy-start | bytes 6094852

commit v3 on v2

--- a/solution.py
+++ b/solution.py
@@ -25,60 +25,97 @@
     return jnp.dot(left_side, diag_inverse, precision=highest)
 
 
-def gather_kernel(n, x_ref, out_ref, send_sem, recv_sem, local_sem):
+def gather_kernel(n, line, x_ref, out_ref, sems, local_sem):
     me = lax.axis_index("gc")
     row = lax.axis_index("gr")
     rows = x_ref.shape[1]
+    lines = n // line
+    pos = lax.rem(me, line)
+    grp = me // line
+    base = grp * line
+
+    def line_peer(k):
+        return base + lax.rem(pos + k, line)
+
+    def cross_peer(k):
+        return lax.rem(grp + k, lines) * line + pos
 
     barrier = pltpu.get_barrier_semaphore()
 
-    def greet(k, carry):
-        peer = lax.rem(me + k, n)
-        pl.semaphore_signal(barrier, inc=1, device_id=(row, peer), device_id_type=MESH_ID)
-        return carry
-
-    lax.fori_loop(1, n, greet, 0)
-    pl.semaphore_wait(barrier, n - 1)
+    def greet_line(k, carry):
+        pl.semaphore_signal(barrier, inc=1, device_id=(row, line_peer(k)), device_id_type=MESH_ID)
+        return carry
+
+    def greet_cross(k, carry):
+        pl.semaphore_signal(barrier, inc=1, device_id=(row, cross_peer(k)), device_id_type=MESH_ID)
+        return carry
+
+    lax.fori_loop(1, line, greet_line, 0)
+    lax.fori_loop(1, lines, greet_cross, 0)
+    pl.semaphore_wait(barrier, line + lines - 2)
 
     own = pltpu.make_async_copy(x_ref, out_ref.at[:, pl.ds(me * rows, rows), :], local_sem)
     own.start()
 
-    def remote(k, sender):
-        peer = lax.rem(me + k, n)
+    def first(k, sender_pos):
         return pltpu.make_async_remote_copy(
             src_ref=x_ref,
-            dst_ref=out_ref.at[:, pl.ds(sender * rows, rows), :],
-            send_sem=send_sem.at[k],
-            recv_sem=recv_sem.at[sender],
-            device_id=(row, peer),
-            device_id_type=MESH_ID,
-        )
-
-    def send(k, carry):
-        remote(k, me).start()
-        return carry
-
-    lax.fori_loop(1, n, send, 0)
-
-    def wait(k, carry):
-        remote(k, me).wait_send()
-        remote(k, lax.rem(me + n - k, n)).wait_recv()
-        return carry
-
-    lax.fori_loop(1, n, wait, 0)
+            dst_ref=out_ref.at[:, pl.ds((base + sender_pos) * rows, rows), :],
+            send_sem=sems.at[0, k],
+            recv_sem=sems.at[1, sender_pos],
+            device_id=(row, line_peer(k)),
+            device_id_type=MESH_ID,
+        )
+
+    def send_first(k, carry):
+        first(k, pos).start()
+        return carry
+
+    lax.fori_loop(1, line, send_first, 0)
+
+    def wait_first(k, carry):
+        first(k, pos).wait_send()
+        first(k, lax.rem(pos + line - k, line)).wait_recv()
+        return carry
+
+    lax.fori_loop(1, line, wait_first, 0)
     own.wait()
 
-
-def gather_gc(block, n):
+    span = line * rows
+
+    def second(k, sender_grp):
+        return pltpu.make_async_remote_copy(
+            src_ref=out_ref.at[:, pl.ds(base * rows, span), :],
+            dst_ref=out_ref.at[:, pl.ds(sender_grp * span, span), :],
+            send_sem=sems.at[2, k],
+            recv_sem=sems.at[3, sender_grp],
+            device_id=(row, cross_peer(k)),
+            device_id_type=MESH_ID,
+        )
+
+    def send_second(k, carry):
+        second(k, grp).start()
+        return carry
+
+    lax.fori_loop(1, lines, send_second, 0)
+
+    def wait_second(k, carry):
+        second(k, grp).wait_send()
+        second(k, lax.rem(grp + lines - k, lines)).wait_recv()
+        return carry
+
+    lax.fori_loop(1, lines, wait_second, 0)
+
+
+def gather_gc(block, n, line):
     tiles, rows, width = block.shape
     return pl.pallas_call(
-        functools.partial(gather_kernel, n),
+        functools.partial(gather_kernel, n, line),
         out_shape=jax.ShapeDtypeStruct((tiles, rows * n, width), block.dtype),
         in_specs=[pl.BlockSpec(memory_space=pl.ANY)],
         out_specs=pl.BlockSpec(memory_space=pl.ANY),
         scratch_shapes=[
-            pltpu.SemaphoreType.DMA((n,)),
-            pltpu.SemaphoreType.DMA((n,)),
+            pltpu.SemaphoreType.DMA((4, max(line, n // line))),
             pltpu.SemaphoreType.DMA,
         ],
         compiler_params=pltpu.CompilerParams(collective_id=0, has_side_effects=True),
@@ -198,6 +235,7 @@
 def local(
     n_gc,
     n_gr,
+    line,
     below_factor,
     panel_factor,
     prior_factor,
@@ -228,7 +266,7 @@
         [own_grad.reshape(tile_count, own_rows, width), panel_factor.reshape(tile_count, own_rows, width)],
         axis=2,
     )
-    whole = gather_gc(both, n_gc)
+    whole = gather_gc(both, n_gc, line)
     grad_rows = whole[:, :, :width].reshape(local_rows, width)
     whole_factor = whole[:, :, width:].reshape(local_rows, width)
     prior_here = prior_factor.reshape(prior_local, local_cols)
@@ -259,6 +297,20 @@
     )
 
 
+def line_length(mesh):
+    column = list(mesh.devices[0])
+    coords = [getattr(d, "coords", None) for d in column]
+    if any(c is None for c in coords):
+        return 8 if len(column) % 8 == 0 else len(column)
+    first = coords[0][0]
+    count = 0
+    for c in coords:
+        if c[0] != first:
+            break
+        count += 1
+    return count if len(column) % count == 0 else len(column)
+
+
 def solution(mesh):
     in_specs = (
         P(None, "gr", None, None, "gc", None),
@@ -278,7 +330,7 @@
         P(),
     )
     return jax.shard_map(
-        functools.partial(local, mesh.shape["gc"], mesh.shape["gr"]),
+        functools.partial(local, mesh.shape["gc"], mesh.shape["gr"], line_length(mesh)),
         mesh=mesh,
         in_specs=in_specs,
         out_specs=out_specs,

time: 168 us -> 144 us (0.86)
  Pallas kernels: 129 us -> 106 us
    pallas_call x1, Pallas kernels: 103 us -> 78.3 us  [gather_gc(): pl.pallas_call(functools.partial(gather_kernel, n, line), out_shape=jax.S...]
where the time goes in v3:
time: 144 us; the launch traced here: 143 us
  Pallas kernels  106 us (74%)
  matrix products  16.4 us (11%)
  local copies, waits for them, and re-layouts  16.1 us (11%)
  other arithmetic  4.47 us (3%)
    pallas_call x1, Pallas kernels, gather_gc(): pl.pallas_call(functools.partial(gather_kernel, n, line), out_shape=jax.S...  78.3 us
    pallas_call x1, Pallas kernels, reduce_gr(): pl.pallas_call(functools.partial(reduce_kernel, n), out_shape=(jax.ShapeD...  27.4 us
    gather x1, local copies, waits for them, and re-layouts, diag_solve(): phi_lower = jnp.tril(chol_proj) - 0.5 * jnp.diag(jnp.diagonal(chol_proj))  4.52 us
    dot_general x1, matrix products, diag_solve(): chol_proj = jnp.dot(diag_factor.T, diag_reduced, precision=highest)  3.9 us
    dot_general x1, matrix products, diag_solve(): left_side = jnp.dot(diag_inverse.T, symmetric, precision=highest)  3.27 us
    reshape x1, local copies, waits for them, and re-layouts, local(): below_new.reshape(below_adjoint.shape)  3.05 us
    dot_general x1, matrix products, diag_solve(): return jnp.dot(left_side, diag_inverse, precision=highest)  2.88 us

profile of v3, /device:TPU:1, one launch (start us, length us, event | category | flops | bytes accessed | tf_op | source)
XLA Modules:
  0.0 143.5 jit_solution(16970600648711840211)
XLA Ops:
  0.6 0.0 copy-start
  0.6 1.0 reshape.49
  1.6 1.4 convolution_convert_fusion.1
  3.1 1.6 %pad_maximum_fusion.1.x_ref = bf16[31,2,1024]{2,1,0:T(2,128)(2,1)} fusion(bf16[31,2,512]{2,1,0:T(2,128)(2,1)} %bitcast.64, bf16[31,2,512]{2,1,0:T(2,128)(2,1)S(1)} %reshape.50), kind=kLoop, calls=%fused_computation.40 | loop fusion | flops 253952 | bytes 253952 | tf_op jit(solution)/shard_map/concatenate | solution.py:265
  4.7 78.3 %shard_map.120 = bf16[31,64,1024]{2,1,0:T(8,128)(2,1)} custom-call(bf16[31,2,1024]{2,1,0:T(2,128)(2,1)} %pad_maximum_fusion.1.x_ref), custom_call_target="tpu_custom_call" | custom-call | tf_op jit(solution)/shard_map/pallas_call | solution.py:112
  83.0 0.0 copy-start.10
  83.0 1.9 %slice.6 = bf16[31,64,512]{2,1,0:T(8,128)(2,1)S(1)} slice(bf16[31,64,1024]{2,1,0:T(8,128)(2,1)} %shard_map.120), slice={[0:31], [0:64], [0:512]} | slice | bytes 4063232 | tf_op jit(solution)/shard_map/slice | solution.py:270
  84.9 0.0 copy-start.2
  84.9 0.0 copy-done.10
  84.9 0.0 copy-start.1
  84.9 0.8 convolution_convert_fusion
  85.6 0.5 copy-done.2
  86.2 1.6 %copy-done.1 = bf16[31,64,1024]{2,1,0:T(8,128)(2,1)S(1)} copy-done((bf16[31,64,1024]{2,1,0:T(8,128)(2,1)S(1)}, bf16[31,64,1024]{2,1,0:T(8,128)(2,1)}, u32[]{:S(2)}) %copy-start.1) | copy-done | bytes 4063256
  87.8 1.3 fusion.6
  89.0 0.0 copy-start.5
  89.1 0.9 pad_maximum_fusion.part_ref
  90.0 0.0 copy-done.9
  90.0 0.6 copy.39
  90.6 27.4 %shard_map.121 = (bf16[8,64,512]{2,1,0:T(8,128)(2,1)}, bf16[8,64,256]{2,1,0:T(8,128)(2,1)}, f32[64,256]{1,0:T(8,128)}) custom-call(bf16[512,768]{1,0:T(8,128)(2,1)} %pad_maximum_fusion.part_ref, bf16[64,256]{1,0:T(8,128)(2,1)} %bitcast.62), custom_call_target="tpu_custom_call" | custom-call | tf_op jit(solution)/shard_map/pallas_call | solution.py:216
  118.0 3.9 %fusion.11 = f32[512,512]{1,0:T(8,128)} fusion(f32[512,512]{1,0:T(8,128)S(1)} %copy-done, f32[512,512]{1,0:T(8,128)S(1)} %copy-done.5, bf16[512,512]{1,0:T(8,128)(2,1)} %bitcast.61), kind=kOutput, calls=%fused_computation.13 | convolution fusion | flops 1611661312 | bytes 3670016 | tf_op jit(solution)/shard_map/dot_general | solution.py:21
  121.9 1.6 %copy.21 = f32[512,512]{0,1:T(8,128)S(1)} copy(f32[512,512]{1,0:T(8,128)} %fusion.11) | data formatting | bytes 2097152 | tf_op jit(solution)/shard_map/dot_general | solution.py:21
  123.6 4.5 %gather_fusion = f32[512]{0:T(512)S(1)} fusion(f32[512,512]{1,0:T(8,128)S(1)} %bitcast.54, s32[512]{0:T(512)S(1)} %bitcast.53), kind=kCustom, calls=%fused_computation | custom fusion | bytes 8192 | tf_op jit(solution)/shard_map/jit(diagonal)/cond/branch_0_fun/gather | solution.py:22
  128.1 0.0 copy-done.4
  128.1 3.3 %fusion.13 = f32[512,512]{1,0:T(8,128)S(1)} fusion(f32[512,512]{1,0:T(8,128)S(1)} %copy-done.4, f32[512,512]{1,0:T(8,128)} %fusion.11, f32[512]{0:T(512)S(1)} %gather_fusion, f32[512,512]{0,1:T(8,128)S(1)} %copy.21), kind=kOutput, calls=%fused_computation.14 | convolution fusion | flops 1614282752 | bytes 4196352 | tf_op jit(solution)/shard_map/dot_general | solution.py:24
  131.4 0.0 copy-start.8
  131.4 2.9 %fusion.42 = f32[512,512]{1,0:T(8,128)} fusion(f32[512,512]{1,0:T(8,128)S(1)} %fusion.13, f32[512,512]{1,0:T(8,128)S(1)} %copy-done.4), kind=kOutput, calls=%fused_computation.52 | convolution fusion | flops 1610612736 | bytes 3145728 | tf_op jit(solution)/shard_map/dot_general | solution.py:25
  134.4 1.2 fusion.9
  135.6 0.6 reshape.58
  136.2 1.9 %convert.18 = f32[248,8,2,128]{3,2,1,0:T(2,128)S(1)} convert(bf16[248,8,2,128]{3,2,1,0:T(2,128)(2,1)} %bitcast.59) | non-fusion elementwise | flops 507904 | bytes 3047424
  138.1 1.6 %fusion = bf16[1984,256]{1,0:T(8,128)(2,1)} fusion(bf16[1984,512]{1,0:T(8,128)(2,1)S(1)} %bitcast.56, bf16[512,256]{1,0:T(8,128)(2,1)S(1)} %bitcast.58, f32[248,8,2,128]{3,2,1,0:T(2,128)S(1)} %convert.18), kind=kOutput, calls=%fused_computation.2 | convolution fusion | flops 521109504 | bytes 5341184 | tf_op jit(solution)/shard_map/dot_general | solution.py:283
  139.8 3.0 %reshape.56 = bf16[31,1,64,2,1,128]{5,3,2,0,4,1:T(2,128)(2,1)} reshape(bf16[1984,256]{1,0:T(8,128)(2,1)} %fusion) | data formatting | bytes 2031616 | tf_op jit(solution)/shard_map/reshape | solution.py:293
  142.8 0.7 reshape.57
  (14 shorter events, 0.1 us)
Async XLA Ops:
  0.6 117.4 %copy-start = (f32[512,512]{1,0:T(8,128)S(1)}, f32[512,512]{1,0:T(8,128)}, u32[]{:S(2)}) copy-start(f32[512,512]{1,0:T(8,128)} %param.12) | copy-start | bytes 3145732
  83.0 1.9 %copy-start.10 = (bf16[31,1,64,2,1,128]{5,3,4,2,1,0:T(2,128)(2,1)S(1)}, bf16[31,1,64,2,1,128]{5,3,4,2,1,0:T(2,128)(2,1)}, u32[]{:S(2)}) copy-start(bf16[31,1,64,2,1,128]{5,3,4,2,1,0:T(2,128)(2,1)} %param.9) | copy-start | bytes 3047428
  84.9 1.3 copy-start.2
  84.9 2.9 %copy-start.1 = (bf16[31,64,1024]{2,1,0:T(8,128)(2,1)S(1)}, bf16[31,64,1024]{2,1,0:T(8,128)(2,1)}, u32[]{:S(2)}) copy-start(bf16[31,64,1024]{2,1,0:T(8,128)(2,1)} %shard_map.120) | copy-start | bytes 12189700
  87.8 2.2 %copy-start.9 = (bf16[64,2,1,128]{3,1,2,0:T(2,128)(2,1)S(1)}, bf16[64,2,1,128]{3,1,2,0:T(2,128)(2,1)}, u32[]{:S(2)}) copy-start(bf16[64,2,1,128]{3,1,2,0:T(2,128)(2,1)} %param.11) | copy-start | bytes 98308
  89.0 29.0 %copy-start.5 = (f32[512,512]{1,0:T(8,128)S(1)}, f32[512,512]{1,0:T(8,128)}, u32[]{:S(2)}) copy-start(f32[512,512]{1,0:T(8,128)} %param.17) | copy-start | bytes 3145732
  121.9 6.2 %copy-start.4 = (f32[512,512]{1,0:T(8,128)S(1)}, f32[512,512]{1,0:T(8,128)}, u32[]{:S(2)}) copy-start(f32[512,512]{1,0:T(8,128)} %param.13) | copy-start | bytes 3145732
  131.4 2.9 %copy-start.8 = (bf16[64,2,1,128]{3,1,2,0:T(2,128)(2,1)S(1)}, bf16[64,2,1,128]{3,1,2,0:T(2,128)(2,1)}, u32[]{:S(2)}) copy-start(bf16[64,2,1,128]{3,1,2,0:T(2,128)(2,1)} %param.16) | copy-start | bytes 98308
  131.4 2.9 %copy-start.6 = (bf16[8,64,256]{2,1,0:T(8,128)(2,1)S(1)}, bf16[8,64,256]{2,1,0:T(8,128)(2,1)}, u32[]{:S(2)}) copy-start(bf16[8,64,256]{2,1,0:T(8,128)(2,1)} %get-tuple-element.7) | copy-start | bytes 786436
  131.4 2.9 %copy-start.7 = (f32[64,256]{1,0:T(8,128)S(1)}, f32[64,256]{1,0:T(8,128)}, u32[]{:S(2)}) copy-start(f32[64,256]{1,0:T(8,128)} %get-tuple-element.8) | copy-start | bytes 196612
  134.3 3.8 %copy-start.3 = (bf16[31,64,512]{2,1,0:T(8,128)(2,1)S(1)}, bf16[31,64,512]{2,1,0:T(8,128)(2,1)}, u32[]{:S(2)}) copy-start(bf16[31,64,512]{2,1,0:T(8,128)(2,1)} %copy-done.2) | copy-start | bytes 6094852

commit v4 on v3

--- a/solution.py
+++ b/solution.py
@@ -73,38 +73,69 @@
 
     lax.fori_loop(1, line, send_first, 0)
 
+    span = line * rows
+
+    def forward(k, block_pos, sender_grp):
+        slot = pl.ds((grp * line + block_pos) * rows, rows)
+        return pltpu.make_async_remote_copy(
+            src_ref=out_ref.at[:, slot, :],
+            dst_ref=out_ref.at[:, slot, :],
+            send_sem=sems.at[2 + block_pos, k],
+            recv_sem=sems.at[1, line + sender_grp],
+            device_id=(row, cross_peer(k)),
+            device_id_type=MESH_ID,
+        )
+
+    def whole_line(sender_grp):
+        return pltpu.make_async_remote_copy(
+            src_ref=out_ref.at[:, pl.ds(sender_grp * span, span), :],
+            dst_ref=out_ref.at[:, pl.ds(sender_grp * span, span), :],
+            send_sem=sems.at[0, 0],
+            recv_sem=sems.at[1, line + sender_grp],
+            device_id=(row, cross_peer(1)),
+            device_id_type=MESH_ID,
+        )
+
+    own.wait()
+
+    def send_own(k, carry):
+        forward(k, pos, grp).start()
+        return carry
+
+    lax.fori_loop(1, lines, send_own, 0)
+
+    def relay(k, carry):
+        sender_pos = lax.rem(pos + line - k, line)
+        first(k, sender_pos).wait_recv()
+
+        def out(j, inner):
+            forward(j, sender_pos, grp).start()
+            return inner
+
+        return lax.fori_loop(1, lines, out, carry)
+
+    lax.fori_loop(1, line, relay, 0)
+
     def wait_first(k, carry):
         first(k, pos).wait_send()
-        first(k, lax.rem(pos + line - k, line)).wait_recv()
         return carry
 
     lax.fori_loop(1, line, wait_first, 0)
-    own.wait()
-
-    span = line * rows
-
-    def second(k, sender_grp):
-        return pltpu.make_async_remote_copy(
-            src_ref=out_ref.at[:, pl.ds(base * rows, span), :],
-            dst_ref=out_ref.at[:, pl.ds(sender_grp * span, span), :],
-            send_sem=sems.at[2, k],
-            recv_sem=sems.at[3, sender_grp],
-            device_id=(row, cross_peer(k)),
-            device_id_type=MESH_ID,
-        )
-
-    def send_second(k, carry):
-        second(k, grp).start()
-        return carry
-
-    lax.fori_loop(1, lines, send_second, 0)
-
-    def wait_second(k, carry):
-        second(k, grp).wait_send()
-        second(k, lax.rem(grp + lines - k, lines)).wait_recv()
-        return carry
-
-    lax.fori_loop(1, lines, wait_second, 0)
+
+    def wait_sent(k, carry):
+        def done(j, inner):
+            forward(j, k, grp).wait_send()
+            return inner
+
+        return lax.fori_loop(1, lines, done, carry)
+
+    lax.fori_loop(0, line, wait_sent, 0)
+
+    def wait_lines(k, carry):
+        whole_line(lax.rem(grp + lines - k, lines)).wait_recv()
+        return carry
+
+    lax.fori_loop(1, lines, wait_lines, 0)
 
 
 def gather_gc(block, n, line):
@@ -115,7 +146,7 @@
         in_specs=[pl.BlockSpec(memory_space=pl.ANY)],
         out_specs=pl.BlockSpec(memory_space=pl.ANY),
         scratch_shapes=[
-            pltpu.SemaphoreType.DMA((4, max(line, n // line))),
+            pltpu.SemaphoreType.DMA((2 + line, line + n // line)),
             pltpu.SemaphoreType.DMA,
         ],
         compiler_params=pltpu.CompilerParams(collective_id=0, has_side_effects=True),

time: 144 us -> 126 us (0.88)
  Pallas kernels: 106 us -> 87.8 us
    pallas_call x1, Pallas kernels: 78.3 us -> 60.4 us  [gather_gc(): pl.pallas_call(functools.partial(gather_kernel, n, line), out_shape=jax.S...]
where the time goes in v4:
time: 126 us
  Pallas kernels  87.8 us (70%)
  matrix products  16.4 us (13%)
  local copies, waits for them, and re-layouts  16.1 us (13%)
  other arithmetic  4.47 us (4%)
    pallas_call x1, Pallas kernels, gather_gc(): pl.pallas_call(functools.partial(gather_kernel, n, line), out_shape=jax.S...  60.4 us
    pallas_call x1, Pallas kernels, reduce_gr(): pl.pallas_call(functools.partial(reduce_kernel, n), out_shape=(jax.ShapeD...  27.3 us
    gather x1, local copies, waits for them, and re-layouts, diag_solve(): phi_lower = jnp.tril(chol_proj) - 0.5 * jnp.diag(jnp.diagonal(chol_proj))  4.52 us
    dot_general x1, matrix products, diag_solve(): chol_proj = jnp.dot(diag_factor.T, diag_reduced, precision=highest)  3.9 us
    dot_general x1, matrix products, diag_solve(): left_side = jnp.dot(diag_inverse.T, symmetric, precision=highest)  3.27 us
    reshape x1, local copies, waits for them, and re-layouts, local(): below_new.reshape(below_adjoint.shape)  3.05 us
    dot_general x1, matrix products, diag_solve(): return jnp.dot(left_side, diag_inverse, precision=highest)  2.89 us
    unnamed x23, local copies, waits for them, and re-layouts  2.78 us

profile of v4, /device:TPU:1, one launch (start us, length us, event | category | flops | bytes accessed | tf_op | source)
XLA Modules:
  0.0 125.6 jit_solution(9604376761878153917)
XLA Ops:
  0.6 0.0 copy-start
  0.6 1.0 reshape.49
  1.6 1.4 %convolution_convert_fusion.1 = bf16[62,512]{1,0:T(8,128)(2,1)S(1)} fusion(bf16[62,512]{1,0:T(8,128)(2,1)S(1)} %reshape.49, f32[512,512]{1,0:T(8,128)} %param.13), kind=kOutput, calls=%fused_computation.8 | convolution fusion | flops 32799744 | bytes 1175552 | tf_op jit(solution)/shard_map/dot_general | solution.py:290
  3.1 1.6 %pad_maximum_fusion.1.x_ref = bf16[31,2,1024]{2,1,0:T(2,128)(2,1)} fusion(bf16[31,2,512]{2,1,0:T(2,128)(2,1)} %bitcast.64, bf16[31,2,512]{2,1,0:T(2,128)(2,1)S(1)} %reshape.50), kind=kLoop, calls=%fused_computation.40 | loop fusion | flops 253952 | bytes 253952 | tf_op jit(solution)/shard_map/concatenate | solution.py:296
  4.7 60.4 %shard_map.120 = bf16[31,64,1024]{2,1,0:T(8,128)(2,1)} custom-call(bf16[31,2,1024]{2,1,0:T(2,128)(2,1)} %pad_maximum_fusion.1.x_ref), custom_call_target="tpu_custom_call" | custom-call | tf_op jit(solution)/shard_map/pallas_call | solution.py:143
  65.1 0.0 copy-start.10
  65.2 1.9 %slice.6 = bf16[31,64,512]{2,1,0:T(8,128)(2,1)S(1)} slice(bf16[31,64,1024]{2,1,0:T(8,128)(2,1)} %shard_map.120), slice={[0:31], [0:64], [0:512]} | slice | bytes 4063232 | tf_op jit(solution)/shard_map/slice | solution.py:301
  67.0 0.0 copy-start.2
  67.0 0.0 copy-done.10
  67.1 0.8 convolution_convert_fusion
  67.8 0.5 copy-done.2
  68.3 1.6 %copy-done.1 = bf16[31,64,1024]{2,1,0:T(8,128)(2,1)S(1)} copy-done((bf16[31,64,1024]{2,1,0:T(8,128)(2,1)S(1)}, bf16[31,64,1024]{2,1,0:T(8,128)(2,1)}, u32[]{:S(2)}) %copy-start.1) | copy-done | bytes 4063256
  69.9 1.3 %fusion.6 = bf16[512,512]{1,0:T(8,128)(2,1)S(1)} fusion(bf16[31,64,1024]{2,1,0:T(8,128)(2,1)S(1)} %copy-done.1), kind=kOutput, calls=%fused_computation.6 | convolution fusion | flops 1040449536 | bytes 4587520 | tf_op jit(solution)/shard_map/dot_general | solution.py:14
  71.2 0.0 copy-start.5
  71.2 0.9 pad_maximum_fusion.part_ref
  72.2 0.0 copy-done.9
  72.2 0.6 copy.39
  72.8 27.3 %shard_map.121 = (bf16[8,64,512]{2,1,0:T(8,128)(2,1)}, bf16[8,64,256]{2,1,0:T(8,128)(2,1)}, f32[64,256]{1,0:T(8,128)}) custom-call(bf16[512,768]{1,0:T(8,128)(2,1)} %pad_maximum_fusion.part_ref, bf16[64,256]{1,0:T(8,128)(2,1)} %bitcast.62), custom_call_target="tpu_custom_call" | custom-call | tf_op jit(solution)/shard_map/pallas_call | solution.py:247
  100.1 3.9 %fusion.11 = f32[512,512]{1,0:T(8,128)} fusion(f32[512,512]{1,0:T(8,128)S(1)} %copy-done, f32[512,512]{1,0:T(8,128)S(1)} %copy-done.5, bf16[512,512]{1,0:T(8,128)(2,1)} %bitcast.61), kind=kOutput, calls=%fused_computation.13 | convolution fusion | flops 1611661312 | bytes 3670016 | tf_op jit(solution)/shard_map/dot_general | solution.py:21
  104.0 1.6 %copy.21 = f32[512,512]{0,1:T(8,128)S(1)} copy(f32[512,512]{1,0:T(8,128)} %fusion.11) | data formatting | bytes 2097152 | tf_op jit(solution)/shard_map/dot_general | solution.py:21
  105.7 4.5 %gather_fusion = f32[512]{0:T(512)S(1)} fusion(f32[512,512]{1,0:T(8,128)S(1)} %bitcast.54, s32[512]{0:T(512)S(1)} %bitcast.53), kind=kCustom, calls=%fused_computation | custom fusion | bytes 8192 | tf_op jit(solution)/shard_map/jit(diagonal)/cond/branch_0_fun/gather | solution.py:22
  110.2 3.3 %fusion.13 = f32[512,512]{1,0:T(8,128)S(1)} fusion(f32[512,512]{1,0:T(8,128)S(1)} %copy-done.4, f32[512,512]{1,0:T(8,128)} %fusion.11, f32[512]{0:T(512)S(1)} %gather_fusion, f32[512,512]{0,1:T(8,128)S(1)} %copy.21), kind=kOutput, calls=%fused_computation.14 | convolution fusion | flops 1614282752 | bytes 4196352 | tf_op jit(solution)/shard_map/dot_general | solution.py:24
  113.5 0.0 copy-start.8
  113.5 0.0 copy-start.6
  113.5 0.0 copy-start.7
  113.5 2.9 %fusion.42 = f32[512,512]{1,0:T(8,128)} fusion(f32[512,512]{1,0:T(8,128)S(1)} %fusion.13, f32[512,512]{1,0:T(8,128)S(1)} %copy-done.4), kind=kOutput, calls=%fused_computation.52 | convolution fusion | flops 1610612736 | bytes 3145728 | tf_op jit(solution)/shard_map/dot_general | solution.py:25
  116.5 1.2 fusion.9
  117.7 0.6 reshape.58
  118.3 1.9 %convert.18 = f32[248,8,2,128]{3,2,1,0:T(2,128)S(1)} convert(bf16[248,8,2,128]{3,2,1,0:T(2,128)(2,1)} %bitcast.59) | non-fusion elementwise | flops 507904 | bytes 3047424
  120.3 1.6 %fusion = bf16[1984,256]{1,0:T(8,128)(2,1)} fusion(bf16[1984,512]{1,0:T(8,128)(2,1)S(1)} %bitcast.56, bf16[512,256]{1,0:T(8,128)(2,1)S(1)} %bitcast.58, f32[248,8,2,128]{3,2,1,0:T(2,128)S(1)} %convert.18), kind=kOutput, calls=%fused_computation.2 | convolution fusion | flops 521109504 | bytes 5341184 | tf_op jit(solution)/shard_map/dot_general | solution.py:314
  121.9 3.0 %reshape.56 = bf16[31,1,64,2,1,128]{5,3,2,0,4,1:T(2,128)(2,1)} reshape(bf16[1984,256]{1,0:T(8,128)(2,1)} %fusion) | data formatting | bytes 2031616 | tf_op jit(solution)/shard_map/reshape | solution.py:324
  125.0 0.7 reshape.57
  (14 shorter events, 0.1 us)
Async XLA Ops:
  0.6 99.5 %copy-start = (f32[512,512]{1,0:T(8,128)S(1)}, f32[512,512]{1,0:T(8,128)}, u32[]{:S(2)}) copy-start(f32[512,512]{1,0:T(8,128)} %param.12) | copy-start | bytes 3145732
  65.1 1.9 %copy-start.10 = (bf16[31,1,64,2,1,128]{5,3,4,2,1,0:T(2,128)(2,1)S(1)}, bf16[31,1,64,2,1,128]{5,3,4,2,1,0:T(2,128)(2,1)}, u32[]{:S(2)}) copy-start(bf16[31,1,64,2,1,128]{5,3,4,2,1,0:T(2,128)(2,1)} %param.9) | copy-start | bytes 3047428
  67.0 1.3 %copy-start.2 = (bf16[31,64,512]{2,1,0:T(8,128)(2,1)}, bf16[31,64,512]{2,1,0:T(8,128)(2,1)S(1)}, u32[]{:S(2)}) copy-start(bf16[31,64,512]{2,1,0:T(8,128)(2,1)S(1)} %slice.6) | copy-start | bytes 6094852
  67.0 2.9 %copy-start.1 = (bf16[31,64,1024]{2,1,0:T(8,128)(2,1)S(1)}, bf16[31,64,1024]{2,1,0:T(8,128)(2,1)}, u32[]{:S(2)}) copy-start(bf16[31,64,1024]{2,1,0:T(8,128)(2,1)} %shard_map.120) | copy-start | bytes 12189700
  69.9 2.2 %copy-start.9 = (bf16[64,2,1,128]{3,1,2,0:T(2,128)(2,1)S(1)}, bf16[64,2,1,128]{3,1,2,0:T(2,128)(2,1)}, u32[]{:S(2)}) copy-start(bf16[64,2,1,128]{3,1,2,0:T(2,128)(2,1)} %param.11) | copy-start | bytes 98308
  71.2 28.9 %copy-start.5 = (f32[512,512]{1,0:T(8,128)S(1)}, f32[512,512]{1,0:T(8,128)}, u32[]{:S(2)}) copy-start(f32[512,512]{1,0:T(8,128)} %param.17) | copy-start | bytes 3145732
  104.0 6.2 %copy-start.4 = (f32[512,512]{1,0:T(8,128)S(1)}, f32[512,512]{1,0:T(8,128)}, u32[]{:S(2)}) copy-start(f32[512,512]{1,0:T(8,128)} %param.13) | copy-start | bytes 3145732
  113.5 2.9 %copy-start.8 = (bf16[64,2,1,128]{3,1,2,0:T(2,128)(2,1)S(1)}, bf16[64,2,1,128]{3,1,2,0:T(2,128)(2,1)}, u32[]{:S(2)}) copy-start(bf16[64,2,1,128]{3,1,2,0:T(2,128)(2,1)} %param.16) | copy-start | bytes 98308
  113.5 2.9 %copy-start.6 = (bf16[8,64,256]{2,1,0:T(8,128)(2,1)S(1)}, bf16[8,64,256]{2,1,0:T(8,128)(2,1)}, u32[]{:S(2)}) copy-start(bf16[8,64,256]{2,1,0:T(8,128)(2,1)} %get-tuple-element.7) | copy-start | bytes 786436
  113.5 2.9 %copy-start.7 = (f32[64,256]{1,0:T(8,128)S(1)}, f32[64,256]{1,0:T(8,128)}, u32[]{:S(2)}) copy-start(f32[64,256]{1,0:T(8,128)} %get-tuple-element.8) | copy-start | bytes 196612
  116.4 3.8 %copy-start.3 = (bf16[31,64,512]{2,1,0:T(8,128)(2,1)S(1)}, bf16[31,64,512]{2,1,0:T(8,128)(2,1)}, u32[]{:S(2)}) copy-start(bf16[31,64,512]{2,1,0:T(8,128)(2,1)} %copy-done.2) | copy-start | bytes 6094852

commit v5 on v4

--- a/solution.py
+++ b/solution.py
@@ -19,7 +19,13 @@
 def diag_solve(diag_factor, diag_inverse, diag_reduced):
     highest = lax.Precision.HIGHEST
     chol_proj = jnp.dot(diag_factor.T, diag_reduced, precision=highest)
-    phi_lower = jnp.tril(chol_proj) - 0.5 * jnp.diag(jnp.diagonal(chol_proj))
+    index_row = lax.broadcasted_iota(jnp.int32, chol_proj.shape, 0)
+    index_col = lax.broadcasted_iota(jnp.int32, chol_proj.shape, 1)
+    phi_lower = jnp.where(
+        index_row > index_col,
+        chol_proj,
+        jnp.where(index_row == index_col, chol_proj - 0.5 * chol_proj, 0.0),
+    )
     symmetric = 0.5 * (phi_lower + phi_lower.T)
     left_side = jnp.dot(diag_inverse.T, symmetric, precision=highest)
     return jnp.dot(left_side, diag_inverse, precision=highest)
@@ -261,6 +267,10 @@
         ],
         compiler_params=pltpu.CompilerParams(collective_id=1, has_side_effects=True),
     )(part, prior_rows)
+
+
+def prior_factor_rows(prior_rows, below_shape):
+    return prior_rows.reshape(-1, below_shape[3], below_shape[5])
 
 
 def local(
@@ -309,10 +319,13 @@
     prior_whole = prior_rows.reshape(width, local_cols)
     diag_reduced = jnp.tril(diag_adjoint - summed)
     diag_gradient = diag_solve(diag_factor, diag_inverse, diag_reduced)
-    below_new = (
-        below_bar.astype(jnp.float32)
-        - jnp.dot(grad_rows, prior_whole, preferred_element_type=jnp.float32)
-    ).astype(jnp.bfloat16)
+    below_prod = lax.dot_general(
+        grad_rows.reshape(tile_count, tile_rows, width),
+        prior_factor_rows(prior_rows, below_factor.shape),
+        (((2,), (0,)), ((), ())),
+        preferred_element_type=jnp.float32,
+    ).reshape(below_adjoint.shape)
+    below_new = (below_adjoint.astype(jnp.float32) - below_prod).astype(jnp.bfloat16)
     grid_row = lax.axis_index("gr")
     twice_rows = lax.dynamic_slice_in_dim(
         2.0 * diag_gradient, grid_row * prior_local, prior_local, 0
@@ -321,7 +334,7 @@
     prior_bar = prior_adjoint.reshape(prior_local, local_cols).astype(jnp.float32)
     prior_new = (prior_bar - crossing - curvature).astype(jnp.bfloat16)
     return (
-        below_new.reshape(below_adjoint.shape),
+        below_new,
         panel_grad,
         prior_new.reshape(prior_adjoint.shape),
         diag_gradient,

time: 126 us -> 116 us (0.921)
  local copies, waits for them, and re-layouts: 16.1 us -> 10.6 us
  matrix products: 16.4 us -> 14.3 us
  other arithmetic: 4.47 us -> 2.56 us
    gather x1 -> x0, local copies, waits for them, and re-layouts: 4.52 us -> none  [diag_solve(): phi_lower = jnp.tril(chol_proj) - 0.5 * jnp.diag(jnp.diagonal(chol_proj))]
    reshape x1, local copies, waits for them, and re-layouts: 3.05 us -> 1.02 us  [prior_factor_rows(): return prior_rows.reshape(-1, below_shape[3], below_shape[5])]
    unnamed x2 -> x1, other arithmetic: 1.93 us -> 0.02 us
    unnamed x23 -> x22, local copies, waits for them, and re-layouts: 2.78 us -> 4.07 us
where the time goes in v5:
time: 116 us
  Pallas kernels  87.8 us (76%)
  matrix products  14.3 us (12%)
  local copies, waits for them, and re-layouts  10.6 us (9%)
  other arithmetic  2.56 us (2%)
    pallas_call x1, Pallas kernels, gather_gc(): pl.pallas_call(functools.partial(gather_kernel, n, line), out_shape=jax.S...  60.4 us
    pallas_call x1, Pallas kernels, reduce_gr(): pl.pallas_call(functools.partial(reduce_kernel, n), out_shape=(jax.ShapeD...  27.3 us
    unnamed x22, local copies, waits for them, and re-layouts  4.07 us
    dot_general x1, matrix products, diag_solve(): chol_proj = jnp.dot(diag_factor.T, diag_reduced, precision=highest)  3.33 us
    dot_general x1, matrix products, diag_solve(): left_side = jnp.dot(diag_inverse.T, symmetric, precision=highest)  3.22 us

profile of v5, /device:TPU:1, one launch (start us, length us, event | category | flops | bytes accessed | tf_op | source)
XLA Modules:
  0.0 116.0 jit_solution(2969855381540424373)
XLA Ops:
  0.6 0.0 copy-start
  0.6 1.0 reshape.48
  1.6 1.4 %convolution_convert_fusion.1 = bf16[62,512]{1,0:T(8,128)(2,1)S(1)} fusion(bf16[62,512]{1,0:T(8,128)(2,1)S(1)} %reshape.48, f32[512,512]{1,0:T(8,128)} %param.13), kind=kOutput, calls=%fused_computation.11 | convolution fusion | flops 32799744 | bytes 1175552 | tf_op jit(solution)/shard_map/dot_general | solution.py:300
  3.1 1.6 %pad_maximum_fusion.1.x_ref = bf16[31,2,1024]{2,1,0:T(2,128)(2,1)} fusion(bf16[31,2,512]{2,1,0:T(2,128)(2,1)} %bitcast.62, bf16[31,2,512]{2,1,0:T(2,128)(2,1)S(1)} %reshape.49), kind=kLoop, calls=%fused_computation.41 | loop fusion | flops 253952 | bytes 253952 | tf_op jit(solution)/shard_map/concatenate | solution.py:306
  4.7 60.4 %shard_map.120 = bf16[31,64,1024]{2,1,0:T(8,128)(2,1)} custom-call(bf16[31,2,1024]{2,1,0:T(2,128)(2,1)} %pad_maximum_fusion.1.x_ref), custom_call_target="tpu_custom_call" | custom-call | tf_op jit(solution)/shard_map/pallas_call | solution.py:149
  65.1 0.0 slice-start
  65.2 0.0 copy-start.8
  65.2 1.9 %slice-done = bf16[31,64,512]{2,1,0:T(8,128)(2,1)S(1)} async-done(((bf16[31,64,1024]{2,1,0:T(8,128)(2,1)}), bf16[31,64,512]{2,1,0:T(8,128)(2,1)S(1)}, s32[]{:S(2)}) %slice-start) | async-done | bytes 2031640 | tf_op jit(solution)/shard_map/slice | solution.py:311
  67.0 0.0 copy-done.8
  67.0 0.8 convolution_convert_fusion
  67.8 1.4 %copy-done.1 = bf16[31,64,1024]{2,1,0:T(8,128)(2,1)S(1)} copy-done((bf16[31,64,1024]{2,1,0:T(8,128)(2,1)S(1)}, bf16[31,64,1024]{2,1,0:T(8,128)(2,1)}, u32[]{:S(2)}) %copy-start.1) | copy-done | bytes 4063256
  69.2 1.3 %fusion.10 = bf16[512,512]{1,0:T(8,128)(2,1)S(1)} fusion(bf16[31,64,1024]{2,1,0:T(8,128)(2,1)S(1)} %copy-done.1), kind=kOutput, calls=%fused_computation.9 | convolution fusion | flops 1040449536 | bytes 4587520 | tf_op jit(solution)/shard_map/dot_general | solution.py:14
  70.5 0.0 copy-start.9
  70.5 0.9 pad_maximum_fusion.part_ref
  71.4 0.0 copy-done.7
  71.4 0.6 copy.39
  72.0 27.3 %shard_map.121 = (bf16[8,64,512]{2,1,0:T(8,128)(2,1)}, bf16[8,64,256]{2,1,0:T(8,128)(2,1)}, f32[64,256]{1,0:T(8,128)}) custom-call(bf16[512,768]{1,0:T(8,128)(2,1)} %pad_maximum_fusion.part_ref, bf16[64,256]{1,0:T(8,128)(2,1)} %bitcast.60), custom_call_target="tpu_custom_call" | custom-call | tf_op jit(solution)/shard_map/pallas_call | solution.py:253
  99.4 1.0 reshape.54
  100.4 0.0 copy-done.9
  100.4 2.3 %fusion.2 = bf16[31,1,64,2,1,128]{5,2,3,0,4,1:T(8,128)(2,1)S(1)} fusion(bf16[31,1,64,2,1,128]{5,3,4,2,1,0:T(2,128)(2,1)S(1)} %copy-done.9, bf16[512,2,128]{2,1,0:T(2,128)(2,1)S(1)} %reshape.54, bf16[31,64,1024]{2,1,0:T(8,128)(2,1)} %shard_map.120), kind=kOutput, calls=%fused_computation.3 | convolution fusion | flops 521617408 | bytes 4325376 | tf_op jit(solution)/shard_map/dot_general | solution.py:322
  102.6 2.0 %copy.18 = bf16[31,1,64,2,1,128]{5,3,4,2,1,0:T(2,128)(2,1)} copy(bf16[31,1,64,2,1,128]{5,2,3,0,4,1:T(8,128)(2,1)S(1)} %fusion.2) | data formatting | bytes 2031616
  104.7 0.7 reshape.56
  105.3 0.0 copy-done
  105.3 3.3 %fusion.24 = f32[512,512]{1,0:T(8,128)S(1)} fusion(f32[512,512]{1,0:T(8,128)S(1)} %copy-done, f32[512,512]{1,0:T(8,128)} %param.17, bf16[512,512]{1,0:T(8,128)(2,1)} %bitcast.59), kind=kOutput, calls=%fused_computation.23 | convolution fusion | flops 1611661312 | bytes 3670016 | tf_op jit(solution)/shard_map/dot_general | solution.py:21
  108.6 1.3 %copy.17 = f32[512,512]{0,1:T(8,128)} copy(f32[512,512]{1,0:T(8,128)S(1)} %fusion.24) | data formatting | bytes 2097152 | tf_op jit(solution)/shard_map/dot_general | solution.py:21
  110.0 3.2 %fusion.18 = f32[512,512]{1,0:T(8,128)S(1)} fusion(f32[512,512]{1,0:T(8,128)S(1)} %copy-done.2, f32[512,512]{1,0:T(8,128)S(1)} %fusion.24, f32[512,512]{0,1:T(8,128)} %copy.17), kind=kOutput, calls=%fused_computation.18 | convolution fusion | flops 1614282752 | bytes 4194304 | tf_op jit(solution)/shard_map/dot_general | solution.py:30
  113.2 0.0 copy-start.6
  113.2 1.8 %fusion.45 = f32[512,512]{1,0:T(8,128)S(1)} fusion(f32[512,512]{1,0:T(8,128)S(1)} %fusion.18, f32[512,512]{1,0:T(8,128)S(1)} %copy-done.2), kind=kOutput, calls=%fused_computation.52 | convolution fusion | flops 1610612736 | bytes 3145728 | tf_op jit(solution)/shard_map/dot_general | solution.py:31
  115.1 0.0 copy-start.3
  115.2 0.2 fusion.13
  115.3 0.7 reshape.58
  116.0 0.0 copy-done.3
  (11 shorter events, 0.1 us)
Async XLA Ops:
  0.6 104.7 %copy-start = (f32[512,512]{1,0:T(8,128)S(1)}, f32[512,512]{1,0:T(8,128)}, u32[]{:S(2)}) copy-start(f32[512,512]{1,0:T(8,128)} %param.12) | copy-start | bytes 3145732
  65.1 1.9 %slice-start = ((bf16[31,64,1024]{2,1,0:T(8,128)(2,1)}), bf16[31,64,512]{2,1,0:T(8,128)(2,1)S(1)}, s32[]{:S(2)}) async-start(bf16[31,64,1024]{2,1,0:T(8,128)(2,1)} %shard_map.120), calls=%async_computation | async-start | bytes 4063232 | tf_op jit(solution)/shard_map/slice | solution.py:311
  65.2 1.9 %copy-start.8 = (bf16[31,1,64,2,1,128]{5,3,4,2,1,0:T(2,128)(2,1)S(1)}, bf16[31,1,64,2,1,128]{5,3,4,2,1,0:T(2,128)(2,1)}, u32[]{:S(2)}) copy-start(bf16[31,1,64,2,1,128]{5,3,4,2,1,0:T(2,128)(2,1)} %param.9) | copy-start | bytes 3047428
  67.0 2.2 %copy-start.1 = (bf16[31,64,1024]{2,1,0:T(8,128)(2,1)S(1)}, bf16[31,64,1024]{2,1,0:T(8,128)(2,1)}, u32[]{:S(2)}) copy-start(bf16[31,64,1024]{2,1,0:T(8,128)(2,1)} %shard_map.120) | copy-start | bytes 12189700
  69.2 2.2 %copy-start.7 = (bf16[64,2,1,128]{3,1,2,0:T(2,128)(2,1)S(1)}, bf16[64,2,1,128]{3,1,2,0:T(2,128)(2,1)}, u32[]{:S(2)}) copy-start(bf16[64,2,1,128]{3,1,2,0:T(2,128)(2,1)} %param.11) | copy-start | bytes 98308
  70.5 29.9 %copy-start.9 = (bf16[31,1,64,2,1,128]{5,3,4,2,1,0:T(2,128)(2,1)S(1)}, bf16[31,1,64,2,1,128]{5,3,4,2,1,0:T(2,128)(2,1)}, u32[]{:S(2)}) copy-start(bf16[31,1,64,2,1,128]{5,3,4,2,1,0:T(2,128)(2,1)} %param.14) | copy-start | bytes 3047428
  105.3 4.7 %copy-start.2 = (f32[512,512]{1,0:T(8,128)S(1)}, f32[512,512]{1,0:T(8,128)}, u32[]{:S(2)}) copy-start(f32[512,512]{1,0:T(8,128)} %param.13) | copy-start | bytes 3145732
  113.2 1.9 %copy-start.6 = (bf16[64,2,1,128]{3,1,2,0:T(2,128)(2,1)S(1)}, bf16[64,2,1,128]{3,1,2,0:T(2,128)(2,1)}, u32[]{:S(2)}) copy-start(bf16[64,2,1,128]{3,1,2,0:T(2,128)(2,1)} %param.16) | copy-start | bytes 98308
  113.2 1.9 %copy-start.4 = (bf16[8,64,256]{2,1,0:T(8,128)(2,1)S(1)}, bf16[8,64,256]{2,1,0:T(8,128)(2,1)}, u32[]{:S(2)}) copy-start(bf16[8,64,256]{2,1,0:T(8,128)(2,1)} %get-tuple-element.7) | copy-start | bytes 786436
  113.2 1.9 %copy-start.5 = (f32[64,256]{1,0:T(8,128)S(1)}, f32[64,256]{1,0:T(8,128)}, u32[]{:S(2)}) copy-start(f32[64,256]{1,0:T(8,128)} %get-tuple-element.8) | copy-start | bytes 196612
  115.1 1.0 copy-start.3

commit v6 on v5

--- a/solution.py
+++ b/solution.py
@@ -31,14 +31,17 @@
     return jnp.dot(left_side, diag_inverse, precision=highest)
 
 
-def gather_kernel(n, line, x_ref, out_ref, sems, local_sem):
+def gather_kernel(n, line, x_ref, out_ref, s1, fsend, lrecv, brecv, rsend, local_sem):
     me = lax.axis_index("gc")
     row = lax.axis_index("gr")
     rows = x_ref.shape[1]
     lines = n // line
+    relay = lines == 4
+    direct = (1, lines - 1) if relay else tuple(range(1, lines))
     pos = lax.rem(me, line)
     grp = me // line
     base = grp * line
+    span = line * rows
 
     def line_peer(k):
         return base + lax.rem(pos + k, line)
@@ -52,13 +55,10 @@
         pl.semaphore_signal(barrier, inc=1, device_id=(row, line_peer(k)), device_id_type=MESH_ID)
         return carry
 
-    def greet_cross(k, carry):
+    lax.fori_loop(1, line, greet_line, 0)
+    for k in direct:
         pl.semaphore_signal(barrier, inc=1, device_id=(row, cross_peer(k)), device_id_type=MESH_ID)
-        return carry
-
-    lax.fori_loop(1, line, greet_line, 0)
-    lax.fori_loop(1, lines, greet_cross, 0)
-    pl.semaphore_wait(barrier, line + lines - 2)
+    pl.semaphore_wait(barrier, line - 1 + len(direct))
 
     own = pltpu.make_async_copy(x_ref, out_ref.at[:, pl.ds(me * rows, rows), :], local_sem)
     own.start()
@@ -67,8 +67,8 @@
         return pltpu.make_async_remote_copy(
             src_ref=x_ref,
             dst_ref=out_ref.at[:, pl.ds((base + sender_pos) * rows, rows), :],
-            send_sem=sems.at[0, k],
-            recv_sem=sems.at[1, sender_pos],
+            send_sem=s1.at[0, k],
+            recv_sem=s1.at[1, sender_pos],
             device_id=(row, line_peer(k)),
             device_id_type=MESH_ID,
         )
@@ -79,16 +79,39 @@
 
     lax.fori_loop(1, line, send_first, 0)
 
-    span = line * rows
-
-    def forward(k, block_pos, sender_grp):
-        slot = pl.ds((grp * line + block_pos) * rows, rows)
-        return pltpu.make_async_remote_copy(
-            src_ref=out_ref.at[:, slot, :],
-            dst_ref=out_ref.at[:, slot, :],
-            send_sem=sems.at[2 + block_pos, k],
-            recv_sem=sems.at[1, line + sender_grp],
+    def block(slot_line, block_pos):
+        return out_ref.at[:, pl.ds((slot_line * line + block_pos) * rows, rows), :]
+
+    def forward(k, block_pos):
+        recv = brecv.at[block_pos] if (relay and k == 1) else lrecv.at[grp]
+        return pltpu.make_async_remote_copy(
+            src_ref=block(grp, block_pos),
+            dst_ref=block(grp, block_pos),
+            send_sem=fsend.at[block_pos, k],
+            recv_sem=recv,
             device_id=(row, cross_peer(k)),
+            device_id_type=MESH_ID,
+        )
+
+    def from_previous(block_pos):
+        prev = lax.rem(grp + lines - 1, lines)
+        return pltpu.make_async_remote_copy(
+            src_ref=block(prev, block_pos),
+            dst_ref=block(prev, block_pos),
+            send_sem=rsend.at[block_pos],
+            recv_sem=lrecv.at[prev],
+            device_id=(row, cross_peer(1)),
+            device_id_type=MESH_ID,
+        )
+
+    def arrived(block_pos):
+        prev = lax.rem(grp + lines - 1, lines)
+        return pltpu.make_async_remote_copy(
+            src_ref=block(prev, block_pos),
+            dst_ref=block(prev, block_pos),
+            send_sem=rsend.at[block_pos],
+            recv_sem=brecv.at[block_pos],
+            device_id=(row, cross_peer(1)),
             device_id_type=MESH_ID,
         )
 
@@ -96,31 +119,33 @@
         return pltpu.make_async_remote_copy(
             src_ref=out_ref.at[:, pl.ds(sender_grp * span, span), :],
             dst_ref=out_ref.at[:, pl.ds(sender_grp * span, span), :],
-            send_sem=sems.at[0, 0],
-            recv_sem=sems.at[1, line + sender_grp],
+            send_sem=local_sem,
+            recv_sem=lrecv.at[sender_grp],
             device_id=(row, cross_peer(1)),
             device_id_type=MESH_ID,
         )
 
     own.wait()
-
-    def send_own(k, carry):
-        forward(k, pos, grp).start()
-        return carry
-
-    lax.fori_loop(1, lines, send_own, 0)
-
-    def relay(k, carry):
+    for k in direct:
+        forward(k, pos).start()
+
+    def relay_line(k, carry):
         sender_pos = lax.rem(pos + line - k, line)
         first(k, sender_pos).wait_recv()
-
-        def out(j, inner):
-            forward(j, sender_pos, grp).start()
-            return inner
-
-        return lax.fori_loop(1, lines, out, carry)
-
-    lax.fori_loop(1, line, relay, 0)
+        for j in direct:
+            forward(j, sender_pos).start()
+        return carry
+
+    lax.fori_loop(1, line, relay_line, 0)
+
+    if relay:
+        def relay_ring(k, carry):
+            block_pos = lax.rem(pos + line - k, line)
+            arrived(block_pos).wait_recv()
+            from_previous(block_pos).start()
+            return carry
+
+        lax.fori_loop(0, line, relay_ring, 0)
 
     def wait_first(k, carry):
         first(k, pos).wait_send()
@@ -128,31 +153,40 @@
 
     lax.fori_loop(1, line, wait_first, 0)
 
-    def wait_sent(k, carry):
-        def done(j, inner):
-            forward(j, k, grp).wait_send()
-            return inner
-
-        return lax.fori_loop(1, lines, done, carry)
+    def wait_sent(p, carry):
+        for k in direct:
+            forward(k, p).wait_send()
+        if relay:
+            from_previous(p).wait_send()
+        return carry
 
     lax.fori_loop(0, line, wait_sent, 0)
 
-    def wait_lines(k, carry):
-        whole_line(lax.rem(grp + lines - k, lines)).wait_recv()
-        return carry
-
-    lax.fori_loop(1, lines, wait_lines, 0)
+    if relay:
+        whole_line(lax.rem(grp + 1, lines)).wait_recv()
+        whole_line(lax.rem(grp + 2, lines)).wait_recv()
+    else:
+        def wait_lines(k, carry):
+            whole_line(lax.rem(grp + lines - k, lines)).wait_recv()
+            return carry
+
+        lax.fori_loop(1, lines, wait_lines, 0)
 
 
 def gather_gc(block, n, line):
     tiles, rows, width = block.shape
+    lines = n // line
     return pl.pallas_call(
         functools.partial(gather_kernel, n, line),
         out_shape=jax.ShapeDtypeStruct((tiles, rows * n, width), block.dtype),
         in_specs=[pl.BlockSpec(memory_space=pl.ANY)],
         out_specs=pl.BlockSpec(memory_space=pl.ANY),
         scratch_shapes=[
-            pltpu.SemaphoreType.DMA((2 + line, line + n // line)),
+            pltpu.SemaphoreType.DMA((2, line)),
+            pltpu.SemaphoreType.DMA((line, lines)),
+            pltpu.SemaphoreType.DMA((lines,)),
+            pltpu.SemaphoreType.DMA((line,)),
+            pltpu.SemaphoreType.DMA((line,)),
             pltpu.SemaphoreType.DMA,
         ],
         compiler_params=pltpu.CompilerParams(collective_id=0, has_side_effects=True),

time: 116 us -> 121 us (1.043)
  Pallas kernels: 87.8 us -> 91.9 us
    pallas_call x1, Pallas kernels: 60.4 us -> 63.9 us  [gather_gc(): pl.pallas_call(functools.partial(gather_kernel, n, line), out_shape=jax.S...]
where the time goes in v6:
time: 121 us; the launch traced here: 120 us
  Pallas kernels  91.9 us (76%)
  matrix products  14.3 us (12%)
  local copies, waits for them, and re-layouts  10.6 us (9%)
  other arithmetic  2.56 us (2%)
    pallas_call x1, Pallas kernels, gather_gc(): pl.pallas_call(functools.partial(gather_kernel, n, line), out_shape=jax.S...  63.9 us
    pallas_call x1, Pallas kernels, reduce_gr(): pl.pallas_call(functools.partial(reduce_kernel, n), out_shape=(jax.ShapeD...  28 us
    unnamed x22, local copies, waits for them, and re-layouts  4.07 us
    dot_general x1, matrix products, diag_solve(): chol_proj = jnp.dot(diag_factor.T, diag_reduced, precision=highest)  3.33 us
    dot_general x1, matrix products, diag_solve(): left_side = jnp.dot(diag_inverse.T, symmetric, precision=highest)  3.22 us

profile of v6, /device:TPU:1, one launch (start us, length us, event | category | flops | bytes accessed | tf_op | source)
XLA Modules:
  0.0 120.2 jit_solution(15520017776486982014)
XLA Ops:
  0.6 0.0 copy-start
  0.6 1.0 reshape.48
  1.6 1.4 %convolution_convert_fusion.1 = bf16[62,512]{1,0:T(8,128)(2,1)S(1)} fusion(bf16[62,512]{1,0:T(8,128)(2,1)S(1)} %reshape.48, f32[512,512]{1,0:T(8,128)} %param.13), kind=kOutput, calls=%fused_computation.11 | convolution fusion | flops 32799744 | bytes 1175552 | tf_op jit(solution)/shard_map/dot_general | solution.py:334
  3.1 1.6 %pad_maximum_fusion.1.x_ref = bf16[31,2,1024]{2,1,0:T(2,128)(2,1)} fusion(bf16[31,2,512]{2,1,0:T(2,128)(2,1)} %bitcast.62, bf16[31,2,512]{2,1,0:T(2,128)(2,1)S(1)} %reshape.49), kind=kLoop, calls=%fused_computation.41 | loop fusion | flops 253952 | bytes 253952 | tf_op jit(solution)/shard_map/concatenate | solution.py:340
  4.7 63.9 %shard_map.120 = bf16[31,64,1024]{2,1,0:T(8,128)(2,1)} custom-call(bf16[31,2,1024]{2,1,0:T(2,128)(2,1)} %pad_maximum_fusion.1.x_ref), custom_call_target="tpu_custom_call" | custom-call | tf_op jit(solution)/shard_map/pallas_call | solution.py:179
  68.6 0.0 slice-start
  68.6 0.0 copy-start.8
  68.6 1.9 %slice-done = bf16[31,64,512]{2,1,0:T(8,128)(2,1)S(1)} async-done(((bf16[31,64,1024]{2,1,0:T(8,128)(2,1)}), bf16[31,64,512]{2,1,0:T(8,128)(2,1)S(1)}, s32[]{:S(2)}) %slice-start) | async-done | bytes 2031640 | tf_op jit(solution)/shard_map/slice | solution.py:345
  70.5 0.0 copy-done.8
  70.5 0.8 convolution_convert_fusion
  71.2 1.4 %copy-done.1 = bf16[31,64,1024]{2,1,0:T(8,128)(2,1)S(1)} copy-done((bf16[31,64,1024]{2,1,0:T(8,128)(2,1)S(1)}, bf16[31,64,1024]{2,1,0:T(8,128)(2,1)}, u32[]{:S(2)}) %copy-start.1) | copy-done | bytes 4063256
  72.6 1.3 %fusion.10 = bf16[512,512]{1,0:T(8,128)(2,1)S(1)} fusion(bf16[31,64,1024]{2,1,0:T(8,128)(2,1)S(1)} %copy-done.1), kind=kOutput, calls=%fused_computation.9 | convolution fusion | flops 1040449536 | bytes 4587520 | tf_op jit(solution)/shard_map/dot_general | solution.py:14
  73.9 0.0 copy-start.9
  73.9 0.9 pad_maximum_fusion.part_ref
  74.8 0.0 copy-done.7
  74.8 0.6 copy.39
  75.5 28.0 %shard_map.121 = (bf16[8,64,512]{2,1,0:T(8,128)(2,1)}, bf16[8,64,256]{2,1,0:T(8,128)(2,1)}, f32[64,256]{1,0:T(8,128)}) custom-call(bf16[512,768]{1,0:T(8,128)(2,1)} %pad_maximum_fusion.part_ref, bf16[64,256]{1,0:T(8,128)(2,1)} %bitcast.60), custom_call_target="tpu_custom_call" | custom-call | tf_op jit(solution)/shard_map/pallas_call | solution.py:287
  103.5 1.0 reshape.54
  104.5 0.0 copy-done.9
  104.5 2.3 %fusion.2 = bf16[31,1,64,2,1,128]{5,2,3,0,4,1:T(8,128)(2,1)S(1)} fusion(bf16[31,1,64,2,1,128]{5,3,4,2,1,0:T(2,128)(2,1)S(1)} %copy-done.9, bf16[512,2,128]{2,1,0:T(2,128)(2,1)S(1)} %reshape.54, bf16[31,64,1024]{2,1,0:T(8,128)(2,1)} %shard_map.120), kind=kOutput, calls=%fused_computation.3 | convolution fusion | flops 521617408 | bytes 4325376 | tf_op jit(solution)/shard_map/dot_general | solution.py:356
  106.8 2.0 %copy.18 = bf16[31,1,64,2,1,128]{5,3,4,2,1,0:T(2,128)(2,1)} copy(bf16[31,1,64,2,1,128]{5,2,3,0,4,1:T(8,128)(2,1)S(1)} %fusion.2) | data formatting | bytes 2031616
  108.8 0.7 reshape.56
  109.5 0.0 copy-done
  109.5 3.3 %fusion.24 = f32[512,512]{1,0:T(8,128)S(1)} fusion(f32[512,512]{1,0:T(8,128)S(1)} %copy-done, f32[512,512]{1,0:T(8,128)} %param.17, bf16[512,512]{1,0:T(8,128)(2,1)} %bitcast.59), kind=kOutput, calls=%fused_computation.23 | convolution fusion | flops 1611661312 | bytes 3670016 | tf_op jit(solution)/shard_map/dot_general | solution.py:21
  112.8 1.3 %copy.17 = f32[512,512]{0,1:T(8,128)} copy(f32[512,512]{1,0:T(8,128)S(1)} %fusion.24) | data formatting | bytes 2097152 | tf_op jit(solution)/shard_map/dot_general | solution.py:21
  114.1 3.2 %fusion.18 = f32[512,512]{1,0:T(8,128)S(1)} fusion(f32[512,512]{1,0:T(8,128)S(1)} %copy-done.2, f32[512,512]{1,0:T(8,128)S(1)} %fusion.24, f32[512,512]{0,1:T(8,128)} %copy.17), kind=kOutput, calls=%fused_computation.18 | convolution fusion | flops 1614282752 | bytes 4194304 | tf_op jit(solution)/shard_map/dot_general | solution.py:30
  117.3 0.0 copy-start.6
  117.4 1.8 %fusion.45 = f32[512,512]{1,0:T(8,128)S(1)} fusion(f32[512,512]{1,0:T(8,128)S(1)} %fusion.18, f32[512,512]{1,0:T(8,128)S(1)} %copy-done.2), kind=kOutput, calls=%fused_computation.52 | convolution fusion | flops 1610612736 | bytes 3145728 | tf_op jit(solution)/shard_map/dot_general | solution.py:31
  119.2 0.0 copy-start.3
  119.3 0.2 fusion.13
  119.5 0.7 reshape.58
  120.2 0.0 copy-done.3
  (11 shorter events, 0.1 us)
Async XLA Ops:
  0.6 108.8 %copy-start = (f32[512,512]{1,0:T(8,128)S(1)}, f32[512,512]{1,0:T(8,128)}, u32[]{:S(2)}) copy-start(f32[512,512]{1,0:T(8,128)} %param.12) | copy-start | bytes 3145732
  68.6 1.9 %slice-start = ((bf16[31,64,1024]{2,1,0:T(8,128)(2,1)}), bf16[31,64,512]{2,1,0:T(8,128)(2,1)S(1)}, s32[]{:S(2)}) async-start(bf16[31,64,1024]{2,1,0:T(8,128)(2,1)} %shard_map.120), calls=%async_computation | async-start | bytes 4063232 | tf_op jit(solution)/shard_map/slice | solution.py:345
  68.6 1.9 %copy-start.8 = (bf16[31,1,64,2,1,128]{5,3,4,2,1,0:T(2,128)(2,1)S(1)}, bf16[31,1,64,2,1,128]{5,3,4,2,1,0:T(2,128)(2,1)}, u32[]{:S(2)}) copy-start(bf16[31,1,64,2,1,128]{5,3,4,2,1,0:T(2,128)(2,1)} %param.9) | copy-start | bytes 3047428
  70.5 2.2 %copy-start.1 = (bf16[31,64,1024]{2,1,0:T(8,128)(2,1)S(1)}, bf16[31,64,1024]{2,1,0:T(8,128)(2,1)}, u32[]{:S(2)}) copy-start(bf16[31,64,1024]{2,1,0:T(8,128)(2,1)} %shard_map.120) | copy-start | bytes 12189700
  72.6 2.2 %copy-start.7 = (bf16[64,2,1,128]{3,1,2,0:T(2,128)(2,1)S(1)}, bf16[64,2,1,128]{3,1,2,0:T(2,128)(2,1)}, u32[]{:S(2)}) copy-start(bf16[64,2,1,128]{3,1,2,0:T(2,128)(2,1)} %param.11) | copy-start | bytes 98308
  73.9 30.6 %copy-start.9 = (bf16[31,1,64,2,1,128]{5,3,4,2,1,0:T(2,128)(2,1)S(1)}, bf16[31,1,64,2,1,128]{5,3,4,2,1,0:T(2,128)(2,1)}, u32[]{:S(2)}) copy-start(bf16[31,1,64,2,1,128]{5,3,4,2,1,0:T(2,128)(2,1)} %param.14) | copy-start | bytes 3047428
  109.5 4.7 %copy-start.2 = (f32[512,512]{1,0:T(8,128)S(1)}, f32[512,512]{1,0:T(8,128)}, u32[]{:S(2)}) copy-start(f32[512,512]{1,0:T(8,128)} %param.13) | copy-start | bytes 3145732
  117.3 1.9 %copy-start.6 = (bf16[64,2,1,128]{3,1,2,0:T(2,128)(2,1)S(1)}, bf16[64,2,1,128]{3,1,2,0:T(2,128)(2,1)}, u32[]{:S(2)}) copy-start(bf16[64,2,1,128]{3,1,2,0:T(2,128)(2,1)} %param.16) | copy-start | bytes 98308
  117.4 1.9 %copy-start.4 = (bf16[8,64,256]{2,1,0:T(8,128)(2,1)S(1)}, bf16[8,64,256]{2,1,0:T(8,128)(2,1)}, u32[]{:S(2)}) copy-start(bf16[8,64,256]{2,1,0:T(8,128)(2,1)} %get-tuple-element.7) | copy-start | bytes 786436
  117.4 1.9 %copy-start.5 = (f32[64,256]{1,0:T(8,128)S(1)}, f32[64,256]{1,0:T(8,128)}, u32[]{:S(2)}) copy-start(f32[64,256]{1,0:T(8,128)} %get-tuple-element.8) | copy-start | bytes 196612
  119.2 1.0 copy-start.3

commit v7 on v5

--- a/solution.py
+++ b/solution.py
@@ -17,7 +17,7 @@
 
 
 def diag_solve(diag_factor, diag_inverse, diag_reduced):
-    highest = lax.Precision.HIGHEST
+    highest = lax.Precision.HIGH
     chol_proj = jnp.dot(diag_factor.T, diag_reduced, precision=highest)
     index_row = lax.broadcasted_iota(jnp.int32, chol_proj.shape, 0)
     index_col = lax.broadcasted_iota(jnp.int32, chol_proj.shape, 1)

time: 116 us -> 114 us (0.983)
  matrix products: 14.3 us -> 11.7 us
where the time goes in v7:
time: 114 us; the launch traced here: 113 us
  Pallas kernels  87.8 us (77%)
  matrix products  11.7 us (10%)
  local copies, waits for them, and re-layouts  10.6 us (9%)
  other arithmetic  2.56 us (2%)
    pallas_call x1, Pallas kernels, gather_gc(): pl.pallas_call(functools.partial(gather_kernel, n, line), out_shape=jax.S...  60.4 us
    pallas_call x1, Pallas kernels, reduce_gr(): pl.pallas_call(functools.partial(reduce_kernel, n), out_shape=(jax.ShapeD...  27.3 us
    unnamed x22, local copies, waits for them, and re-layouts  4.07 us
    dot_general x1, matrix products, diag_solve(): chol_proj = jnp.dot(diag_factor.T, diag_reduced, precision=highest)  2.49 us
    dot_general x1, matrix products, diag_solve(): left_side = jnp.dot(diag_inverse.T, symmetric, precision=highest)  2.33 us

profile of v7, /device:TPU:1, one launch (start us, length us, event | category | flops | bytes accessed | tf_op | source)
XLA Modules:
  0.0 113.5 jit_solution(17970923314555143147)
XLA Ops:
  0.6 0.0 copy-start
  0.6 1.0 reshape.48
  1.6 1.4 %convolution_convert_fusion.1 = bf16[62,512]{1,0:T(8,128)(2,1)S(1)} fusion(bf16[62,512]{1,0:T(8,128)(2,1)S(1)} %reshape.48, f32[512,512]{1,0:T(8,128)} %param.13), kind=kOutput, calls=%fused_computation.11 | convolution fusion | flops 32799744 | bytes 1175552 | tf_op jit(solution)/shard_map/dot_general | solution.py:300
  3.1 1.6 %pad_maximum_fusion.1.x_ref = bf16[31,2,1024]{2,1,0:T(2,128)(2,1)} fusion(bf16[31,2,512]{2,1,0:T(2,128)(2,1)} %bitcast.62, bf16[31,2,512]{2,1,0:T(2,128)(2,1)S(1)} %reshape.49), kind=kLoop, calls=%fused_computation.41 | loop fusion | flops 253952 | bytes 253952 | tf_op jit(solution)/shard_map/concatenate | solution.py:306
  4.7 60.4 %shard_map.120 = bf16[31,64,1024]{2,1,0:T(8,128)(2,1)} custom-call(bf16[31,2,1024]{2,1,0:T(2,128)(2,1)} %pad_maximum_fusion.1.x_ref), custom_call_target="tpu_custom_call" | custom-call | tf_op jit(solution)/shard_map/pallas_call | solution.py:149
  65.1 0.0 slice-start
  65.2 0.0 copy-start.8
  65.2 1.9 %slice-done = bf16[31,64,512]{2,1,0:T(8,128)(2,1)S(1)} async-done(((bf16[31,64,1024]{2,1,0:T(8,128)(2,1)}), bf16[31,64,512]{2,1,0:T(8,128)(2,1)S(1)}, s32[]{:S(2)}) %slice-start) | async-done | bytes 2031640 | tf_op jit(solution)/shard_map/slice | solution.py:311
  67.0 0.0 copy-done.8
  67.0 0.8 convolution_convert_fusion
  67.8 1.4 %copy-done.1 = bf16[31,64,1024]{2,1,0:T(8,128)(2,1)S(1)} copy-done((bf16[31,64,1024]{2,1,0:T(8,128)(2,1)S(1)}, bf16[31,64,1024]{2,1,0:T(8,128)(2,1)}, u32[]{:S(2)}) %copy-start.1) | copy-done | bytes 4063256
  69.2 1.3 %fusion.10 = bf16[512,512]{1,0:T(8,128)(2,1)S(1)} fusion(bf16[31,64,1024]{2,1,0:T(8,128)(2,1)S(1)} %copy-done.1), kind=kOutput, calls=%fused_computation.9 | convolution fusion | flops 1040449536 | bytes 4587520 | tf_op jit(solution)/shard_map/dot_general | solution.py:14
  70.5 0.0 copy-start.9
  70.5 0.9 pad_maximum_fusion.part_ref
  71.4 0.0 copy-done.7
  71.4 0.6 copy.39
  72.0 27.3 %shard_map.121 = (bf16[8,64,512]{2,1,0:T(8,128)(2,1)}, bf16[8,64,256]{2,1,0:T(8,128)(2,1)}, f32[64,256]{1,0:T(8,128)}) custom-call(bf16[512,768]{1,0:T(8,128)(2,1)} %pad_maximum_fusion.part_ref, bf16[64,256]{1,0:T(8,128)(2,1)} %bitcast.60), custom_call_target="tpu_custom_call" | custom-call | tf_op jit(solution)/shard_map/pallas_call | solution.py:253
  99.4 1.0 reshape.54
  100.4 0.0 copy-done.9
  100.4 2.3 %fusion.2 = bf16[31,1,64,2,1,128]{5,2,3,0,4,1:T(8,128)(2,1)S(1)} fusion(bf16[31,1,64,2,1,128]{5,3,4,2,1,0:T(2,128)(2,1)S(1)} %copy-done.9, bf16[512,2,128]{2,1,0:T(2,128)(2,1)S(1)} %reshape.54, bf16[31,64,1024]{2,1,0:T(8,128)(2,1)} %shard_map.120), kind=kOutput, calls=%fused_computation.3 | convolution fusion | flops 521617408 | bytes 4325376 | tf_op jit(solution)/shard_map/dot_general | solution.py:322
  102.6 2.0 %copy.18 = bf16[31,1,64,2,1,128]{5,3,4,2,1,0:T(2,128)(2,1)} copy(bf16[31,1,64,2,1,128]{5,2,3,0,4,1:T(8,128)(2,1)S(1)} %fusion.2) | data formatting | bytes 2031616
  104.7 0.7 reshape.56
  105.3 2.5 %fusion.24 = f32[512,512]{1,0:T(8,128)S(1)} fusion(f32[512,512]{1,0:T(8,128)S(1)} %copy-done, f32[512,512]{1,0:T(8,128)} %param.17, bf16[512,512]{1,0:T(8,128)(2,1)} %bitcast.59), kind=kOutput, calls=%fused_computation.23 | convolution fusion | flops 806354944 | bytes 3670016 | tf_op jit(solution)/shard_map/dot_general | solution.py:21
  107.8 1.3 %copy.17 = f32[512,512]{0,1:T(8,128)} copy(f32[512,512]{1,0:T(8,128)S(1)} %fusion.24) | data formatting | bytes 2097152 | tf_op jit(solution)/shard_map/dot_general | solution.py:21
  109.1 2.3 %fusion.18 = f32[512,512]{1,0:T(8,128)S(1)} fusion(f32[512,512]{1,0:T(8,128)S(1)} %copy-done.2, f32[512,512]{1,0:T(8,128)S(1)} %fusion.24, f32[512,512]{0,1:T(8,128)} %copy.17), kind=kOutput, calls=%fused_computation.18 | convolution fusion | flops 808976384 | bytes 4194304 | tf_op jit(solution)/shard_map/dot_general | solution.py:30
  111.5 0.0 copy-start.6
  111.5 1.0 fusion.45
  112.5 0.0 copy-start.3
  112.5 0.0 copy-done.6
  112.6 0.2 fusion.13
  112.8 0.7 reshape.58
  113.5 0.0 copy-done.3
  (11 shorter events, 0.1 us)
Async XLA Ops:
  0.6 104.7 %copy-start = (f32[512,512]{1,0:T(8,128)S(1)}, f32[512,512]{1,0:T(8,128)}, u32[]{:S(2)}) copy-start(f32[512,512]{1,0:T(8,128)} %param.12) | copy-start | bytes 3145732
  65.1 1.9 %slice-start = ((bf16[31,64,1024]{2,1,0:T(8,128)(2,1)}), bf16[31,64,512]{2,1,0:T(8,128)(2,1)S(1)}, s32[]{:S(2)}) async-start(bf16[31,64,1024]{2,1,0:T(8,128)(2,1)} %shard_map.120), calls=%async_computation | async-start | bytes 4063232 | tf_op jit(solution)/shard_map/slice | solution.py:311
  65.2 1.9 %copy-start.8 = (bf16[31,1,64,2,1,128]{5,3,4,2,1,0:T(2,128)(2,1)S(1)}, bf16[31,1,64,2,1,128]{5,3,4,2,1,0:T(2,128)(2,1)}, u32[]{:S(2)}) copy-start(bf16[31,1,64,2,1,128]{5,3,4,2,1,0:T(2,128)(2,1)} %param.9) | copy-start | bytes 3047428
  67.0 2.2 %copy-start.1 = (bf16[31,64,1024]{2,1,0:T(8,128)(2,1)S(1)}, bf16[31,64,1024]{2,1,0:T(8,128)(2,1)}, u32[]{:S(2)}) copy-start(bf16[31,64,1024]{2,1,0:T(8,128)(2,1)} %shard_map.120) | copy-start | bytes 12189700
  69.2 2.2 %copy-start.7 = (bf16[64,2,1,128]{3,1,2,0:T(2,128)(2,1)S(1)}, bf16[64,2,1,128]{3,1,2,0:T(2,128)(2,1)}, u32[]{:S(2)}) copy-start(bf16[64,2,1,128]{3,1,2,0:T(2,128)(2,1)} %param.11) | copy-start | bytes 98308
  70.5 29.9 %copy-start.9 = (bf16[31,1,64,2,1,128]{5,3,4,2,1,0:T(2,128)(2,1)S(1)}, bf16[31,1,64,2,1,128]{5,3,4,2,1,0:T(2,128)(2,1)}, u32[]{:S(2)}) copy-start(bf16[31,1,64,2,1,128]{5,3,4,2,1,0:T(2,128)(2,1)} %param.14) | copy-start | bytes 3047428
  105.3 3.8 %copy-start.2 = (f32[512,512]{1,0:T(8,128)S(1)}, f32[512,512]{1,0:T(8,128)}, u32[]{:S(2)}) copy-start(f32[512,512]{1,0:T(8,128)} %param.13) | copy-start | bytes 3145732
  111.5 1.1 copy-start.6
  111.5 1.1 copy-start.4
  111.5 1.1 copy-start.5
  112.5 1.0 copy-start.3

commit v8 on v7

--- a/solution.py
+++ b/solution.py
@@ -34,7 +34,7 @@
 def gather_kernel(n, line, x_ref, out_ref, sems, local_sem):
     me = lax.axis_index("gc")
     row = lax.axis_index("gr")
-    rows = x_ref.shape[1]
+    rows = x_ref.shape[2]
     lines = n // line
     pos = lax.rem(me, line)
     grp = me // line
@@ -60,13 +60,13 @@
     lax.fori_loop(1, lines, greet_cross, 0)
     pl.semaphore_wait(barrier, line + lines - 2)
 
-    own = pltpu.make_async_copy(x_ref, out_ref.at[:, pl.ds(me * rows, rows), :], local_sem)
+    own = pltpu.make_async_copy(x_ref, out_ref.at[:, :, pl.ds(me * rows, rows), :], local_sem)
     own.start()
 
     def first(k, sender_pos):
         return pltpu.make_async_remote_copy(
             src_ref=x_ref,
-            dst_ref=out_ref.at[:, pl.ds((base + sender_pos) * rows, rows), :],
+            dst_ref=out_ref.at[:, :, pl.ds((base + sender_pos) * rows, rows), :],
             send_sem=sems.at[0, k],
             recv_sem=sems.at[1, sender_pos],
             device_id=(row, line_peer(k)),
@@ -84,8 +84,8 @@
     def forward(k, block_pos, sender_grp):
         slot = pl.ds((grp * line + block_pos) * rows, rows)
         return pltpu.make_async_remote_copy(
-            src_ref=out_ref.at[:, slot, :],
-            dst_ref=out_ref.at[:, slot, :],
+            src_ref=out_ref.at[:, :, slot, :],
+            dst_ref=out_ref.at[:, :, slot, :],
             send_sem=sems.at[2 + block_pos, k],
             recv_sem=sems.at[1, line + sender_grp],
             device_id=(row, cross_peer(k)),
@@ -94,8 +94,8 @@
 
     def whole_line(sender_grp):
         return pltpu.make_async_remote_copy(
-            src_ref=out_ref.at[:, pl.ds(sender_grp * span, span), :],
-            dst_ref=out_ref.at[:, pl.ds(sender_grp * span, span), :],
+            src_ref=out_ref.at[:, :, pl.ds(sender_grp * span, span), :],
+            dst_ref=out_ref.at[:, :, pl.ds(sender_grp * span, span), :],
             send_sem=sems.at[0, 0],
             recv_sem=sems.at[1, line + sender_grp],
             device_id=(row, cross_peer(1)),
@@ -145,10 +145,10 @@
 
 
 def gather_gc(block, n, line):
-    tiles, rows, width = block.shape
+    count, tiles, rows, width = block.shape
     return pl.pallas_call(
         functools.partial(gather_kernel, n, line),
-        out_shape=jax.ShapeDtypeStruct((tiles, rows * n, width), block.dtype),
+        out_shape=jax.ShapeDtypeStruct((count, tiles, rows * n, width), block.dtype),
         in_specs=[pl.BlockSpec(memory_space=pl.ANY)],
         out_specs=pl.BlockSpec(memory_space=pl.ANY),
         scratch_shapes=[
@@ -303,13 +303,12 @@
         preferred_element_type=jnp.float32,
     ).astype(jnp.bfloat16)
     panel_grad = own_grad.reshape(panel_adjoint.shape)
-    both = jnp.concatenate(
-        [own_grad.reshape(tile_count, own_rows, width), panel_factor.reshape(tile_count, own_rows, width)],
-        axis=2,
+    both = jnp.stack(
+        [own_grad.reshape(tile_count, own_rows, width), panel_factor.reshape(tile_count, own_rows, width)]
     )
     whole = gather_gc(both, n_gc, line)
-    grad_rows = whole[:, :, :width].reshape(local_rows, width)
-    whole_factor = whole[:, :, width:].reshape(local_rows, width)
+    grad_rows = whole[0].reshape(local_rows, width)
+    whole_factor = whole[1].reshape(local_rows, width)
     prior_here = prior_factor.reshape(prior_local, local_cols)
     part = jnp.concatenate(
         [row_product(grad_rows, whole_factor), row_product(grad_rows, below_mat)], axis=1

time: 114 us -> 114 us (level)
    another operation x0 -> x1, other arithmetic: none -> 1.67 us  [local(): jnp.stack([own_grad.reshape(tile_count, own_rows, width), panel_factor.re...]
    concatenate x1 -> x0, other arithmetic: 1.6 us -> none  [local(): jnp.concatenate([own_grad.reshape(tile_count, own_rows, width), panel_fac...]
where the time goes in v8:
time: 114 us
  Pallas kernels  87.8 us (77%)
  matrix products  11.7 us (10%)
  local copies, waits for them, and re-layouts  10.6 us (9%)
  other arithmetic  2.63 us (2%)
    pallas_call x1, Pallas kernels, gather_gc(): pl.pallas_call(functools.partial(gather_kernel, n, line), out_shape=jax.S...  60.4 us
    pallas_call x1, Pallas kernels, reduce_gr(): pl.pallas_call(functools.partial(reduce_kernel, n), out_shape=(jax.ShapeD...  27.3 us
    unnamed x22, local copies, waits for them, and re-layouts  4.07 us
    dot_general x1, matrix products, diag_solve(): chol_proj = jnp.dot(diag_factor.T, diag_reduced, precision=highest)  2.49 us
    dot_general x1, matrix products, diag_solve(): left_side = jnp.dot(diag_inverse.T, symmetric, precision=highest)  2.33 us

profile of v8, /device:TPU:1, one launch (start us, length us, event | category | flops | bytes accessed | tf_op | source)
XLA Modules:
  0.0 113.6 jit_solution(13657605855877109267)
XLA Ops:
  0.6 0.0 copy-start
  0.6 1.0 reshape.42
  1.6 1.4 %convolution_convert_fusion.1 = bf16[62,512]{1,0:T(8,128)(2,1)S(1)} fusion(bf16[62,512]{1,0:T(8,128)(2,1)S(1)} %reshape.42, f32[512,512]{1,0:T(8,128)} %param.13), kind=kOutput, calls=%fused_computation.13 | convolution fusion | flops 32799744 | bytes 1175552 | tf_op jit(solution)/shard_map/dot_general | solution.py:300
  3.1 1.7 %pad_maximum_fusion.1.x_ref = bf16[2,31,2,512]{3,2,1,0:T(2,128)(2,1)} fusion(bf16[1,31,2,512]{3,2,1,0:T(2,128)(2,1)} %bitcast.76, bf16[1,31,2,512]{3,2,1,0:T(2,128)(2,1)S(1)} %stack_reshape.6), kind=kLoop, calls=%fused_computation.43 | loop fusion | flops 63488 | bytes 253952 | tf_op jit(solution)/shard_map/stack | solution.py:306
  4.8 60.4 %shard_map.120 = bf16[2,31,64,512]{3,2,1,0:T(8,128)(2,1)} custom-call(bf16[2,31,2,512]{3,2,1,0:T(2,128)(2,1)} %pad_maximum_fusion.1.x_ref), custom_call_target="tpu_custom_call" | custom-call | tf_op jit(solution)/shard_map/pallas_call | solution.py:149
  65.2 0.0 slice-start
  65.2 0.0 copy-start.8
  65.2 1.9 %slice-done = bf16[1,31,64,512]{3,2,1,0:T(8,128)(2,1)S(1)} async-done(((bf16[2,31,64,512]{3,2,1,0:T(8,128)(2,1)}), bf16[1,31,64,512]{3,2,1,0:T(8,128)(2,1)S(1)}, s32[]{:S(2)}) %slice-start) | async-done | bytes 2031640 | tf_op jit(solution)/shard_map/slice | solution.py:310
  67.1 0.0 copy-done.8
  67.1 0.8 convolution_convert_fusion
  67.9 1.4 %copy-done.1 = bf16[2,31,64,512]{3,2,1,0:T(8,128)(2,1)S(1)} copy-done((bf16[2,31,64,512]{3,2,1,0:T(8,128)(2,1)S(1)}, bf16[2,31,64,512]{3,2,1,0:T(8,128)(2,1)}, u32[]{:S(2)}) %copy-start.1) | copy-done | bytes 4063256
  69.2 1.3 %fusion.14 = bf16[512,512]{1,0:T(8,128)(2,1)S(1)} fusion(bf16[2,31,64,512]{3,2,1,0:T(8,128)(2,1)S(1)} %copy-done.1), kind=kOutput, calls=%fused_computation.11 | convolution fusion | flops 1040449536 | bytes 4587520 | tf_op jit(solution)/shard_map/dot_general | solution.py:14
  70.5 0.0 copy-start.9
  70.5 0.9 pad_maximum_fusion.part_ref
  71.5 0.0 copy-done.7
  71.5 0.6 copy.39
  72.1 27.3 %shard_map.121 = (bf16[8,64,512]{2,1,0:T(8,128)(2,1)}, bf16[8,64,256]{2,1,0:T(8,128)(2,1)}, f32[64,256]{1,0:T(8,128)}) custom-call(bf16[512,768]{1,0:T(8,128)(2,1)} %pad_maximum_fusion.part_ref, bf16[64,256]{1,0:T(8,128)(2,1)} %bitcast.74), custom_call_target="tpu_custom_call" | custom-call | tf_op jit(solution)/shard_map/pallas_call | solution.py:253
  99.4 1.0 reshape.46
  100.4 0.0 copy-done.9
  100.4 2.3 %fusion.2 = bf16[31,1,64,2,1,128]{5,2,3,0,4,1:T(8,128)(2,1)S(1)} fusion(bf16[31,1,64,2,1,128]{5,3,4,2,1,0:T(2,128)(2,1)S(1)} %copy-done.9, bf16[512,2,128]{2,1,0:T(2,128)(2,1)S(1)} %reshape.46, bf16[2,31,64,512]{3,2,1,0:T(8,128)(2,1)} %shard_map.120), kind=kOutput, calls=%fused_computation.3 | convolution fusion | flops 521617408 | bytes 4325376 | tf_op jit(solution)/shard_map/dot_general | solution.py:321
  102.7 2.0 %copy.18 = bf16[31,1,64,2,1,128]{5,3,4,2,1,0:T(2,128)(2,1)} copy(bf16[31,1,64,2,1,128]{5,2,3,0,4,1:T(8,128)(2,1)S(1)} %fusion.2) | data formatting | bytes 2031616
  104.7 0.7 reshape.48
  105.4 2.5 %fusion.30 = f32[512,512]{1,0:T(8,128)S(1)} fusion(f32[512,512]{1,0:T(8,128)S(1)} %copy-done, f32[512,512]{1,0:T(8,128)} %param.17, bf16[512,512]{1,0:T(8,128)(2,1)} %bitcast.73), kind=kOutput, calls=%fused_computation.25 | convolution fusion | flops 806354944 | bytes 3670016 | tf_op jit(solution)/shard_map/dot_general | solution.py:21
  107.9 1.3 %copy.17 = f32[512,512]{0,1:T(8,128)} copy(f32[512,512]{1,0:T(8,128)S(1)} %fusion.30) | data formatting | bytes 2097152 | tf_op jit(solution)/shard_map/dot_general | solution.py:21
  109.2 2.3 %fusion.24 = f32[512,512]{1,0:T(8,128)S(1)} fusion(f32[512,512]{1,0:T(8,128)S(1)} %copy-done.2, f32[512,512]{1,0:T(8,128)S(1)} %fusion.30, f32[512,512]{0,1:T(8,128)} %copy.17), kind=kOutput, calls=%fused_computation.20 | convolution fusion | flops 808976384 | bytes 4194304 | tf_op jit(solution)/shard_map/dot_general | solution.py:30
  111.5 0.0 copy-start.6
  111.6 1.0 fusion.51
  112.6 0.0 copy-start.3
  112.6 0.0 copy-done.6
  112.7 0.2 fusion.19
  112.9 0.7 reshape.50
  113.6 0.0 copy-done.3
  (11 shorter events, 0.1 us)
Async XLA Ops:
  0.6 104.7 %copy-start = (f32[512,512]{1,0:T(8,128)S(1)}, f32[512,512]{1,0:T(8,128)}, u32[]{:S(2)}) copy-start(f32[512,512]{1,0:T(8,128)} %param.12) | copy-start | bytes 3145732
  65.2 1.9 %slice-start = ((bf16[2,31,64,512]{3,2,1,0:T(8,128)(2,1)}), bf16[1,31,64,512]{3,2,1,0:T(8,128)(2,1)S(1)}, s32[]{:S(2)}) async-start(bf16[2,31,64,512]{3,2,1,0:T(8,128)(2,1)} %shard_map.120), calls=%async_computation | async-start | bytes 4063232 | tf_op jit(solution)/shard_map/slice | solution.py:310
  65.2 1.9 %copy-start.8 = (bf16[31,1,64,2,1,128]{5,3,4,2,1,0:T(2,128)(2,1)S(1)}, bf16[31,1,64,2,1,128]{5,3,4,2,1,0:T(2,128)(2,1)}, u32[]{:S(2)}) copy-start(bf16[31,1,64,2,1,128]{5,3,4,2,1,0:T(2,128)(2,1)} %param.9) | copy-start | bytes 3047428
  67.1 2.2 %copy-start.1 = (bf16[2,31,64,512]{3,2,1,0:T(8,128)(2,1)S(1)}, bf16[2,31,64,512]{3,2,1,0:T(8,128)(2,1)}, u32[]{:S(2)}) copy-start(bf16[2,31,64,512]{3,2,1,0:T(8,128)(2,1)} %shard_map.120) | copy-start | bytes 12189700
  69.2 2.2 %copy-start.7 = (bf16[64,2,1,128]{3,1,2,0:T(2,128)(2,1)S(1)}, bf16[64,2,1,128]{3,1,2,0:T(2,128)(2,1)}, u32[]{:S(2)}) copy-start(bf16[64,2,1,128]{3,1,2,0:T(2,128)(2,1)} %param.11) | copy-start | bytes 98308
  70.5 29.9 %copy-start.9 = (bf16[31,1,64,2,1,128]{5,3,4,2,1,0:T(2,128)(2,1)S(1)}, bf16[31,1,64,2,1,128]{5,3,4,2,1,0:T(2,128)(2,1)}, u32[]{:S(2)}) copy-start(bf16[31,1,64,2,1,128]{5,3,4,2,1,0:T(2,128)(2,1)} %param.14) | copy-start | bytes 3047428
  105.4 3.8 %copy-start.2 = (f32[512,512]{1,0:T(8,128)S(1)}, f32[512,512]{1,0:T(8,128)}, u32[]{:S(2)}) copy-start(f32[512,512]{1,0:T(8,128)} %param.13) | copy-start | bytes 3145732
  111.5 1.1 copy-start.6
  111.5 1.1 copy-start.4
  111.6 1.1 copy-start.5
  112.6 1.0 copy-start.3

commit v9 on v8

--- a/solution.py
+++ b/solution.py
@@ -31,7 +31,7 @@
     return jnp.dot(left_side, diag_inverse, precision=highest)
 
 
-def gather_kernel(n, line, x_ref, out_ref, sems, local_sem):
+def gather_kernel(n, line, x_ref, p_ref, out_ref, psum_ref, precv, psems, sems, local_sem):
     me = lax.axis_index("gc")
     row = lax.axis_index("gr")
     rows = x_ref.shape[2]
@@ -48,17 +48,23 @@
 
     barrier = pltpu.get_barrier_semaphore()
 
-    def greet_line(k, carry):
-        pl.semaphore_signal(barrier, inc=1, device_id=(row, line_peer(k)), device_id_type=MESH_ID)
-        return carry
-
-    def greet_cross(k, carry):
-        pl.semaphore_signal(barrier, inc=1, device_id=(row, cross_peer(k)), device_id_type=MESH_ID)
-        return carry
-
-    lax.fori_loop(1, line, greet_line, 0)
-    lax.fori_loop(1, lines, greet_cross, 0)
-    pl.semaphore_wait(barrier, line + lines - 2)
+    def greet(k, carry):
+        pl.semaphore_signal(barrier, inc=1, device_id=(row, lax.rem(me + k, n)), device_id_type=MESH_ID)
+        return carry
+
+    lax.fori_loop(1, n, greet, 0)
+    pl.semaphore_wait(barrier, n - 1)
+
+    def part_copy(k, sender):
+        peer = lax.rem(me + k, n)
+        return pltpu.make_async_remote_copy(
+            src_ref=p_ref.at[peer],
+            dst_ref=precv.at[sender],
+            send_sem=psems.at[0, k],
+            recv_sem=psems.at[1, sender],
+            device_id=(row, peer),
+            device_id_type=MESH_ID,
+        )
 
     own = pltpu.make_async_copy(x_ref, out_ref.at[:, :, pl.ds(me * rows, rows), :], local_sem)
     own.start()
@@ -79,6 +85,12 @@
 
     lax.fori_loop(1, line, send_first, 0)
 
+    def send_parts(k, carry):
+        part_copy(k, me).start()
+        return carry
+
+    lax.fori_loop(1, n, send_parts, 0)
+
     span = line * rows
 
     def forward(k, block_pos, sender_grp):
@@ -143,130 +155,169 @@
 
     lax.fori_loop(1, lines, wait_lines, 0)
 
-
-def gather_gc(block, n, line):
+    precv[me] = p_ref[me]
+
+    def wait_parts(k, carry):
+        part_copy(k, me).wait_send()
+        part_copy(k, lax.rem(me + n - k, n)).wait_recv()
+        return carry
+
+    lax.fori_loop(1, n, wait_parts, 0)
+
+    def add_part(j, total):
+        return total + precv[j].astype(jnp.float32)
+
+    psum_ref[...] = lax.fori_loop(0, n, add_part, jnp.zeros(psum_ref.shape, jnp.float32))
+
+
+def gather_gc(block, part, n, line):
     count, tiles, rows, width = block.shape
+    vmem = pl.BlockSpec(memory_space=pltpu.VMEM)
     return pl.pallas_call(
         functools.partial(gather_kernel, n, line),
-        out_shape=jax.ShapeDtypeStruct((count, tiles, rows * n, width), block.dtype),
-        in_specs=[pl.BlockSpec(memory_space=pl.ANY)],
-        out_specs=pl.BlockSpec(memory_space=pl.ANY),
+        out_shape=(
+            jax.ShapeDtypeStruct((count, tiles, rows * n, width), block.dtype),
+            jax.ShapeDtypeStruct(part.shape[1:], jnp.float32),
+        ),
+        in_specs=[pl.BlockSpec(memory_space=pl.ANY), vmem],
+        out_specs=(pl.BlockSpec(memory_space=pl.ANY), vmem),
         scratch_shapes=[
+            pltpu.VMEM(part.shape, part.dtype),
+            pltpu.SemaphoreType.DMA((2, n)),
             pltpu.SemaphoreType.DMA((2 + line, line + n // line)),
             pltpu.SemaphoreType.DMA,
         ],
         compiler_params=pltpu.CompilerParams(collective_id=0, has_side_effects=True),
-    )(block)
-
-
-def reduce_kernel(n, part_ref, prior_ref, cross_out, prior_out, crossing_out,
-                  recv_part, cross_slots, prior_slots, sems):
+    )(block, part)
+
+
+def reduce_kernel(n, n_gc, crossing_ref, piece_ref, prior_ref, cross_out, prior_out, crossing_out,
+                  recv_crossing, recv_piece, prior_slots, cross_slots, sems):
     me = lax.axis_index("gr")
     col = lax.axis_index("gc")
     rows = prior_ref.shape[0]
-    wide = cross_out.shape[2]
 
     barrier = pltpu.get_barrier_semaphore()
 
-    def greet(k, carry):
+    def greet_gr(k, carry):
+        pl.semaphore_signal(barrier, inc=1, device_id=(lax.rem(me + k, n), col), device_id_type=MESH_ID)
+        return carry
+
+    def greet_gc(k, carry):
+        pl.semaphore_signal(barrier, inc=1, device_id=(me, lax.rem(col + k, n_gc)), device_id_type=MESH_ID)
+        return carry
+
+    lax.fori_loop(1, n, greet_gr, 0)
+    lax.fori_loop(1, n_gc, greet_gc, 0)
+    pl.semaphore_wait(barrier, n + n_gc - 2)
+
+    def gr_copy(k, sender, src, dst, index):
+        return pltpu.make_async_remote_copy(
+            src_ref=src,
+            dst_ref=dst.at[sender],
+            send_sem=sems.at[index, k],
+            recv_sem=sems.at[index + 1, sender],
+            device_id=(lax.rem(me + k, n), col),
+            device_id_type=MESH_ID,
+        )
+
+    def crossing_copy(k, sender):
         peer = lax.rem(me + k, n)
-        pl.semaphore_signal(barrier, inc=1, device_id=(peer, col), device_id_type=MESH_ID)
-        return carry
-
-    lax.fori_loop(1, n, greet, 0)
-    pl.semaphore_wait(barrier, n - 1)
+        src = crossing_ref.at[pl.ds(pl.multiple_of(peer * rows, rows), rows), :]
+        return gr_copy(k, sender, src, recv_crossing, 0)
+
+    def piece_copy(k, sender):
+        return gr_copy(k, sender, piece_ref, recv_piece, 2)
 
     def prior_copy(k, sender):
-        return pltpu.make_async_remote_copy(
-            src_ref=prior_ref,
-            dst_ref=prior_slots.at[sender],
-            send_sem=sems.at[0, k],
-            recv_sem=sems.at[1, sender],
-            device_id=(lax.rem(me + k, n), col),
-            device_id_type=MESH_ID,
-        )
-
-    def part_copy(k, sender):
-        peer = lax.rem(me + k, n)
-        return pltpu.make_async_remote_copy(
-            src_ref=part_ref.at[pl.ds(pl.multiple_of(peer * rows, rows), rows), :],
-            dst_ref=recv_part.at[sender],
-            send_sem=sems.at[2, k],
-            recv_sem=sems.at[3, sender],
-            device_id=(peer, col),
-            device_id_type=MESH_ID,
-        )
+        return gr_copy(k, sender, prior_ref, prior_slots, 4)
 
     def cross_copy(k, sender):
         return pltpu.make_async_remote_copy(
-            src_ref=cross_slots.at[me],
+            src_ref=cross_slots.at[col],
             dst_ref=cross_slots.at[sender],
-            send_sem=sems.at[4, k],
-            recv_sem=sems.at[5, sender],
-            device_id=(lax.rem(me + k, n), col),
+            send_sem=sems.at[6, k],
+            recv_sem=sems.at[7, sender],
+            device_id=(me, lax.rem(col + k, n_gc)),
             device_id_type=MESH_ID,
         )
 
     def send_first(k, carry):
+        piece_copy(k, me).start()
+        crossing_copy(k, me).start()
         prior_copy(k, me).start()
-        part_copy(k, me).start()
         return carry
 
     lax.fori_loop(1, n, send_first, 0)
     prior_slots[me] = prior_ref[...]
-
-    acc = part_ref[pl.ds(pl.multiple_of(me * rows, rows), rows), :].astype(jnp.float32)
-
-    def add(k, total):
+    recv_piece[me] = piece_ref[...]
+    recv_crossing[me] = crossing_ref[pl.ds(pl.multiple_of(me * rows, rows), rows), :]
+
+    def wait_first(k, carry):
         sender = lax.rem(me + n - k, n)
-        part_copy(k, me).wait_send()
-        part_copy(k, sender).wait_recv()
-        return total + recv_part[sender].astype(jnp.float32)
-
-    acc = lax.fori_loop(1, n, add, acc)
-    crossing_out[...] = acc[:, wide:]
-    cross_slots[me] = acc[:, :wide].astype(cross_slots.dtype)
+        piece_copy(k, me).wait_send()
+        piece_copy(k, sender).wait_recv()
+        crossing_copy(k, me).wait_send()
+        crossing_copy(k, sender).wait_recv()
+        return carry
+
+    lax.fori_loop(1, n, wait_first, 0)
+
+    def add_piece(j, total):
+        return total + recv_piece[j]
+
+    piece = lax.fori_loop(0, n, add_piece, jnp.zeros(piece_ref.shape, jnp.float32))
+    cross_slots[col] = piece.astype(cross_slots.dtype)
 
     def send_second(k, carry):
-        cross_copy(k, me).start()
-        return carry
-
-    lax.fori_loop(1, n, send_second, 0)
+        cross_copy(k, col).start()
+        return carry
+
+    lax.fori_loop(1, n_gc, send_second, 0)
+
+    def add_crossing(j, total):
+        return total + recv_crossing[j].astype(jnp.float32)
+
+    crossing_out[...] = lax.fori_loop(0, n, add_crossing, jnp.zeros(crossing_out.shape, jnp.float32))
 
     def wait_second(k, carry):
-        sender = lax.rem(me + n - k, n)
-        cross_copy(k, me).wait_send()
-        cross_copy(k, sender).wait_recv()
+        cross_copy(k, col).wait_send()
+        cross_copy(k, lax.rem(col + n_gc - k, n_gc)).wait_recv()
+        return carry
+
+    lax.fori_loop(1, n_gc, wait_second, 0)
+
+    def wait_prior(k, carry):
         prior_copy(k, me).wait_send()
-        prior_copy(k, sender).wait_recv()
-        return carry
-
-    lax.fori_loop(1, n, wait_second, 0)
+        prior_copy(k, lax.rem(me + n - k, n)).wait_recv()
+        return carry
+
+    lax.fori_loop(1, n, wait_prior, 0)
     cross_out[...] = cross_slots[...]
     prior_out[...] = prior_slots[...]
 
 
-def reduce_gr(part, prior_rows, n):
+def reduce_gr(crossing_part, piece, prior_rows, n, n_gc):
     rows, cols = prior_rows.shape
-    wide = part.shape[1] - cols
     vmem = pl.BlockSpec(memory_space=pltpu.VMEM)
     return pl.pallas_call(
-        functools.partial(reduce_kernel, n),
+        functools.partial(reduce_kernel, n, n_gc),
         out_shape=(
-            jax.ShapeDtypeStruct((n, rows, wide), part.dtype),
+            jax.ShapeDtypeStruct((n_gc,) + piece.shape, jnp.bfloat16),
             jax.ShapeDtypeStruct((n, rows, cols), prior_rows.dtype),
             jax.ShapeDtypeStruct((rows, cols), jnp.float32),
         ),
-        in_specs=[vmem, vmem],
+        in_specs=[vmem, vmem, vmem],
         out_specs=(vmem, vmem, vmem),
         scratch_shapes=[
-            pltpu.VMEM((n, rows, part.shape[1]), part.dtype),
-            pltpu.VMEM((n, rows, wide), part.dtype),
+            pltpu.VMEM((n, rows, cols), crossing_part.dtype),
+            pltpu.VMEM((n,) + piece.shape, jnp.float32),
             pltpu.VMEM((n, rows, cols), prior_rows.dtype),
-            pltpu.SemaphoreType.DMA((6, n)),
+            pltpu.VMEM((n_gc,) + piece.shape, jnp.bfloat16),
+            pltpu.SemaphoreType.DMA((8, max(n, n_gc))),
         ],
         compiler_params=pltpu.CompilerParams(collective_id=1, has_side_effects=True),
-    )(part, prior_rows)
+    )(crossing_part, piece, prior_rows)
 
 
 def prior_factor_rows(prior_rows, below_shape):
@@ -303,17 +354,18 @@
         preferred_element_type=jnp.float32,
     ).astype(jnp.bfloat16)
     panel_grad = own_grad.reshape(panel_adjoint.shape)
-    both = jnp.stack(
-        [own_grad.reshape(tile_count, own_rows, width), panel_factor.reshape(tile_count, own_rows, width)]
-    )
-    whole = gather_gc(both, n_gc, line)
+    own_factor = panel_factor.reshape(tile_count * own_rows, width)
+    own_part = row_product(own_grad, own_factor).astype(jnp.bfloat16)
+    whole, piece = gather_gc(
+        own_grad.reshape(1, tile_count, own_rows, width),
+        own_part.reshape(n_gc, width // n_gc, width),
+        n_gc,
+        line,
+    )
     grad_rows = whole[0].reshape(local_rows, width)
-    whole_factor = whole[1].reshape(local_rows, width)
     prior_here = prior_factor.reshape(prior_local, local_cols)
-    part = jnp.concatenate(
-        [row_product(grad_rows, whole_factor), row_product(grad_rows, below_mat)], axis=1
-    ).astype(jnp.bfloat16)
-    cross_rows, prior_rows, crossing = reduce_gr(part, prior_here, n_gr)
+    crossing_part = row_product(grad_rows, below_mat).astype(jnp.bfloat16)
+    cross_rows, prior_rows, crossing = reduce_gr(crossing_part, piece, prior_here, n_gr, n_gc)
     summed = cross_rows.reshape(width, width).astype(jnp.float32)
     prior_whole = prior_rows.reshape(width, local_cols)
     diag_reduced = jnp.tril(diag_adjoint - summed)

time: 114 us -> 104 us (0.912)
  Pallas kernels: 87.8 us -> 80.4 us
  other arithmetic: 2.63 us -> 0.02 us
  matrix products: 11.7 us -> 13.9 us
  local copies, waits for them, and re-layouts: 10.6 us -> 8.83 us
    pallas_call x2, Pallas kernels: 87.8 us -> 80.4 us  [the longest x1 44.8 us: gather_gc(): pl.pallas_call(functools.partial(gather_kernel, n, line), out_shape=(jax....]
    dot_general x2, matrix products: 2.02 us -> 4.55 us  [row_product(): lax.dot_general(left_rows, right_rows, (((0,), (0,)), ((), ())), preferre...]
    slice x2 -> x0, local copies, waits for them, and re-layouts: 1.85 us -> none  [local(): grad_rows = whole[0].reshape(local_rows, width)]
    another operation x1 -> x0, other arithmetic: 1.67 us -> none  [local(): jnp.stack([own_grad.reshape(tile_count, own_rows, width), panel_factor.re...]
    reshape x0 -> x2, local copies, waits for them, and re-layouts: none -> 1.52 us  [the longest x1 0.86 us: local(): own_factor = panel_factor.reshape(tile_count * own_rows, width)]
    unnamed x22 -> x18, local copies, waits for them, and re-layouts: 4.07 us -> 2.68 us
where the time goes in v9:
time: 104 us
  Pallas kernels  80.4 us (77%)
  matrix products  13.9 us (13%)
  local copies, waits for them, and re-layouts  8.83 us (8%)
    pallas_call x1, Pallas kernels, gather_gc(): pl.pallas_call(functools.partial(gather_kernel, n, line), out_shape=(jax....  44.8 us
    pallas_call x1, Pallas kernels, reduce_gr(): pl.pallas_call(functools.partial(reduce_kernel, n, n_gc), out_shape=(jax....  35.6 us
    dot_general x2, matrix products, row_product(): lax.dot_general(left_rows, right_rows, (((0,), (0,)), ((), ())), preferre...  4.55 us
    unnamed x18, local copies, waits for them, and re-layouts  2.68 us
    dot_general x1, matrix products, diag_solve(): chol_proj = jnp.dot(diag_factor.T, diag_reduced, precision=highest)  2.49 us
    dot_general x1, matrix products, diag_solve(): left_side = jnp.dot(diag_inverse.T, symmetric, precision=highest)  2.33 us

profile of v9, /device:TPU:1, one launch (start us, length us, event | category | flops | bytes accessed | tf_op | source)
XLA Modules:
  0.0 104.0 jit_solution(7181684255728352756)
XLA Ops:
  0.6 0.0 copy-start
  0.6 1.0 reshape.47
  1.6 1.4 %convolution_convert_fusion.2 = bf16[62,512]{1,0:T(8,128)(2,1)S(1)} fusion(bf16[62,512]{1,0:T(8,128)(2,1)S(1)} %reshape.47, f32[512,512]{1,0:T(8,128)} %param.13), kind=kOutput, calls=%fused_computation.8 | convolution fusion | flops 32799744 | bytes 1175552 | tf_op jit(solution)/shard_map/dot_general | solution.py:351
  3.0 0.7 reshape.48.x_ref
  3.7 0.9 reshape.49
  4.6 1.1 %convolution_convert_fusion = bf16[512,512]{1,0:T(8,128)(2,1)} fusion(bf16[62,512]{1,0:T(8,128)(2,1)S(1)} %convolution_convert_fusion.2, bf16[62,512]{1,0:T(8,128)(2,1)S(1)} %reshape.49), kind=kOutput, calls=%fused_computation.6 | convolution fusion | flops 32768000 | bytes 651264 | tf_op jit(solution)/shard_map/dot_general | solution.py:14
  5.7 44.8 %shard_map.120 = (bf16[1,31,64,512]{3,2,1,0:T(8,128)(2,1)}, f32[16,512]{1,0:T(8,128)}) custom-call(bf16[1,31,2,512]{3,2,1,0:T(2,128)(2,1)} %reshape.48.x_ref, bf16[32,16,512]{2,1,0:T(8,128)(2,1)} %bitcast.56), custom_call_target="tpu_custom_call" | custom-call | tf_op jit(solution)/shard_map/pallas_call | solution.py:176
  50.5 0.0 copy-start.6
  50.5 0.0 copy-start.7
  50.5 3.4 %convolution_convert_fusion.1.crossing_ref = bf16[512,256]{1,0:T(8,128)(2,1)} fusion(bf16[1984,512]{1,0:T(8,128)(2,1)} %bitcast.64, bf16[248,8,2,128]{3,2,1,0:T(2,128)(2,1)} %bitcast.65), kind=kOutput, calls=%fused_computation.7 | convolution fusion | flops 520224768 | bytes 3309568 | tf_op jit(solution)/shard_map/dot_general | solution.py:14
  53.9 0.0 copy-done.6
  53.9 0.6 copy.34
  54.6 35.6 %shard_map.121 = (bf16[32,16,512]{2,1,0:T(8,128)(2,1)}, bf16[8,64,256]{2,1,0:T(8,128)(2,1)}, f32[64,256]{1,0:T(8,128)}) custom-call(bf16[512,256]{1,0:T(8,128)(2,1)} %convolution_convert_fusion.1.crossing_ref, f32[16,512]{1,0:T(8,128)} %get-tuple-element.10.piece_ref, bf16[64,256]{1,0:T(8,128)(2,1)} %bitcast.59), custom_call_target="tpu_custom_call" | custom-call | tf_op jit(solution)/shard_map/pallas_call | solution.py:303
  90.2 1.0 reshape.53
  91.2 0.0 copy-done.7
  91.2 1.9 %fusion.2 = bf16[31,1,64,2,1,128]{5,2,3,0,4,1:T(8,128)(2,1)S(1)} fusion(bf16[1,31,64,512]{3,2,1,0:T(8,128)(2,1)S(1)} %copy-done.7, bf16[31,1,64,2,1,128]{5,3,4,2,1,0:T(2,128)(2,1)} %param.14, bf16[512,2,128]{2,1,0:T(2,128)(2,1)S(1)} %reshape.53), kind=kOutput, calls=%fused_computation.3 | convolution fusion | flops 521617408 | bytes 4325376 | tf_op jit(solution)/shard_map/dot_general | solution.py:373
  93.1 2.0 %copy.16 = bf16[31,1,64,2,1,128]{5,3,4,2,1,0:T(2,128)(2,1)} copy(bf16[31,1,64,2,1,128]{5,2,3,0,4,1:T(8,128)(2,1)S(1)} %fusion.2) | data formatting | bytes 2031616
  95.1 0.7 reshape.55
  95.8 0.0 copy-done
  95.8 2.5 %fusion.16 = f32[512,512]{1,0:T(8,128)S(1)} fusion(f32[512,512]{1,0:T(8,128)S(1)} %copy-done, f32[512,512]{1,0:T(8,128)} %param.17, bf16[512,512]{1,0:T(8,128)(2,1)} %bitcast.58), kind=kOutput, calls=%fused_computation.20 | convolution fusion | flops 806354944 | bytes 3670016 | tf_op jit(solution)/shard_map/dot_general | solution.py:21
  98.3 1.3 %copy.15 = f32[512,512]{0,1:T(8,128)} copy(f32[512,512]{1,0:T(8,128)S(1)} %fusion.16) | data formatting | bytes 2097152 | tf_op jit(solution)/shard_map/dot_general | solution.py:21
  99.6 0.0 copy-done.1
  99.6 2.3 %fusion.10 = f32[512,512]{1,0:T(8,128)S(1)} fusion(f32[512,512]{1,0:T(8,128)S(1)} %copy-done.1, f32[512,512]{1,0:T(8,128)S(1)} %fusion.16, f32[512,512]{0,1:T(8,128)} %copy.15), kind=kOutput, calls=%fused_computation.15 | convolution fusion | flops 808976384 | bytes 4194304 | tf_op jit(solution)/shard_map/dot_general | solution.py:30
  101.9 0.0 copy-start.5
  101.9 0.0 copy-start.3
  102.0 1.0 fusion.35
  103.0 0.0 copy-start.2
  103.1 0.0 copy-done.3
  103.1 0.0 copy-done.4
  103.1 0.2 fusion.5
  103.2 0.7 reshape.57
  104.0 0.0 copy-done.2
  (4 shorter events, 0.0 us)
Async XLA Ops:
  0.6 95.2 %copy-start = (f32[512,512]{1,0:T(8,128)S(1)}, f32[512,512]{1,0:T(8,128)}, u32[]{:S(2)}) copy-start(f32[512,512]{1,0:T(8,128)} %param.12) | copy-start | bytes 3145732
  50.5 3.5 %copy-start.6 = (bf16[64,2,1,128]{3,1,2,0:T(2,128)(2,1)S(1)}, bf16[64,2,1,128]{3,1,2,0:T(2,128)(2,1)}, u32[]{:S(2)}) copy-start(bf16[64,2,1,128]{3,1,2,0:T(2,128)(2,1)} %param.11) | copy-start | bytes 98308
  50.5 40.7 %copy-start.7 = (bf16[1,31,64,512]{3,2,1,0:T(8,128)(2,1)S(1)}, bf16[1,31,64,512]{3,2,1,0:T(8,128)(2,1)}, u32[]{:S(2)}) copy-start(bf16[1,31,64,512]{3,2,1,0:T(8,128)(2,1)} %get-tuple-element.9) | copy-start | bytes 6094852
  95.8 3.8 %copy-start.1 = (f32[512,512]{1,0:T(8,128)S(1)}, f32[512,512]{1,0:T(8,128)}, u32[]{:S(2)}) copy-start(f32[512,512]{1,0:T(8,128)} %param.13) | copy-start | bytes 3145732
  101.9 1.1 %copy-start.5 = (bf16[64,2,1,128]{3,1,2,0:T(2,128)(2,1)S(1)}, bf16[64,2,1,128]{3,1,2,0:T(2,128)(2,1)}, u32[]{:S(2)}) copy-start(bf16[64,2,1,128]{3,1,2,0:T(2,128)(2,1)} %param.16) | copy-start | bytes 98308
  101.9 1.1 %copy-start.3 = (bf16[8,64,256]{2,1,0:T(8,128)(2,1)S(1)}, bf16[8,64,256]{2,1,0:T(8,128)(2,1)}, u32[]{:S(2)}) copy-start(bf16[8,64,256]{2,1,0:T(8,128)(2,1)} %get-tuple-element.11) | copy-start | bytes 786436
  102.0 1.1 %copy-start.4 = (f32[64,256]{1,0:T(8,128)S(1)}, f32[64,256]{1,0:T(8,128)}, u32[]{:S(2)}) copy-start(f32[64,256]{1,0:T(8,128)} %get-tuple-element.12) | copy-start | bytes 196612
  103.0 1.0 copy-start.2

commit v10 on v9

--- a/solution.py
+++ b/solution.py
@@ -254,11 +254,8 @@
     recv_crossing[me] = crossing_ref[pl.ds(pl.multiple_of(me * rows, rows), rows), :]
 
     def wait_first(k, carry):
-        sender = lax.rem(me + n - k, n)
         piece_copy(k, me).wait_send()
-        piece_copy(k, sender).wait_recv()
-        crossing_copy(k, me).wait_send()
-        crossing_copy(k, sender).wait_recv()
+        piece_copy(k, lax.rem(me + n - k, n)).wait_recv()
         return carry
 
     lax.fori_loop(1, n, wait_first, 0)
@@ -274,6 +271,13 @@
         return carry
 
     lax.fori_loop(1, n_gc, send_second, 0)
+
+    def wait_crossing(k, carry):
+        crossing_copy(k, me).wait_send()
+        crossing_copy(k, lax.rem(me + n - k, n)).wait_recv()
+        return carry
+
+    lax.fori_loop(1, n, wait_crossing, 0)
 
     def add_crossing(j, total):
         return total + recv_crossing[j].astype(jnp.float32)

time: 104 us -> 104 us (level)
  no operation moved by 1% of the time
where the time goes in v10:
time: 104 us
  Pallas kernels  80 us (77%)
  matrix products  13.9 us (13%)
  local copies, waits for them, and re-layouts  8.83 us (8%)
    pallas_call x1, Pallas kernels, gather_gc(): pl.pallas_call(functools.partial(gather_kernel, n, line), out_shape=(jax....  44.8 us
    pallas_call x1, Pallas kernels, reduce_gr(): pl.pallas_call(functools.partial(reduce_kernel, n, n_gc), out_shape=(jax....  35.2 us
    dot_general x2, matrix products, row_product(): lax.dot_general(left_rows, right_rows, (((0,), (0,)), ((), ())), preferre...  4.55 us
    unnamed x18, local copies, waits for them, and re-layouts  2.68 us
    dot_general x1, matrix products, diag_solve(): chol_proj = jnp.dot(diag_factor.T, diag_reduced, precision=highest)  2.49 us
    dot_general x1, matrix products, diag_solve(): left_side = jnp.dot(diag_inverse.T, symmetric, precision=highest)  2.33 us

profile of v10, /device:TPU:1, one launch (start us, length us, event | category | flops | bytes accessed | tf_op | source)
XLA Modules:
  0.0 103.6 jit_solution(10638933143714803989)
XLA Ops:
  0.6 0.0 copy-start
  0.6 1.0 reshape.47
  1.6 1.4 %convolution_convert_fusion.2 = bf16[62,512]{1,0:T(8,128)(2,1)S(1)} fusion(bf16[62,512]{1,0:T(8,128)(2,1)S(1)} %reshape.47, f32[512,512]{1,0:T(8,128)} %param.13), kind=kOutput, calls=%fused_computation.8 | convolution fusion | flops 32799744 | bytes 1175552 | tf_op jit(solution)/shard_map/dot_general | solution.py:355
  3.0 0.7 reshape.48.x_ref
  3.7 0.9 reshape.49
  4.6 1.1 %convolution_convert_fusion = bf16[512,512]{1,0:T(8,128)(2,1)} fusion(bf16[62,512]{1,0:T(8,128)(2,1)S(1)} %convolution_convert_fusion.2, bf16[62,512]{1,0:T(8,128)(2,1)S(1)} %reshape.49), kind=kOutput, calls=%fused_computation.6 | convolution fusion | flops 32768000 | bytes 651264 | tf_op jit(solution)/shard_map/dot_general | solution.py:14
  5.7 44.8 %shard_map.120 = (bf16[1,31,64,512]{3,2,1,0:T(8,128)(2,1)}, f32[16,512]{1,0:T(8,128)}) custom-call(bf16[1,31,2,512]{3,2,1,0:T(2,128)(2,1)} %reshape.48.x_ref, bf16[32,16,512]{2,1,0:T(8,128)(2,1)} %bitcast.56), custom_call_target="tpu_custom_call" | custom-call | tf_op jit(solution)/shard_map/pallas_call | solution.py:176
  50.5 0.0 copy-start.6
  50.5 0.0 copy-start.7
  50.5 3.4 %convolution_convert_fusion.1.crossing_ref = bf16[512,256]{1,0:T(8,128)(2,1)} fusion(bf16[1984,512]{1,0:T(8,128)(2,1)} %bitcast.64, bf16[248,8,2,128]{3,2,1,0:T(2,128)(2,1)} %bitcast.65), kind=kOutput, calls=%fused_computation.7 | convolution fusion | flops 520224768 | bytes 3309568 | tf_op jit(solution)/shard_map/dot_general | solution.py:14
  53.9 0.0 copy-done.6
  53.9 0.6 copy.34
  54.6 35.2 %shard_map.121 = (bf16[32,16,512]{2,1,0:T(8,128)(2,1)}, bf16[8,64,256]{2,1,0:T(8,128)(2,1)}, f32[64,256]{1,0:T(8,128)}) custom-call(bf16[512,256]{1,0:T(8,128)(2,1)} %convolution_convert_fusion.1.crossing_ref, f32[16,512]{1,0:T(8,128)} %get-tuple-element.10.piece_ref, bf16[64,256]{1,0:T(8,128)(2,1)} %bitcast.59), custom_call_target="tpu_custom_call" | custom-call | tf_op jit(solution)/shard_map/pallas_call | solution.py:307
  89.8 1.0 reshape.53
  90.8 0.0 copy-done.7
  90.8 1.9 %fusion.2 = bf16[31,1,64,2,1,128]{5,2,3,0,4,1:T(8,128)(2,1)S(1)} fusion(bf16[1,31,64,512]{3,2,1,0:T(8,128)(2,1)S(1)} %copy-done.7, bf16[31,1,64,2,1,128]{5,3,4,2,1,0:T(2,128)(2,1)} %param.14, bf16[512,2,128]{2,1,0:T(2,128)(2,1)S(1)} %reshape.53), kind=kOutput, calls=%fused_computation.3 | convolution fusion | flops 521617408 | bytes 4325376 | tf_op jit(solution)/shard_map/dot_general | solution.py:377
  92.8 2.0 %copy.16 = bf16[31,1,64,2,1,128]{5,3,4,2,1,0:T(2,128)(2,1)} copy(bf16[31,1,64,2,1,128]{5,2,3,0,4,1:T(8,128)(2,1)S(1)} %fusion.2) | data formatting | bytes 2031616
  94.8 0.7 reshape.55
  95.4 0.0 copy-done
  95.4 2.5 %fusion.16 = f32[512,512]{1,0:T(8,128)S(1)} fusion(f32[512,512]{1,0:T(8,128)S(1)} %copy-done, f32[512,512]{1,0:T(8,128)} %param.17, bf16[512,512]{1,0:T(8,128)(2,1)} %bitcast.58), kind=kOutput, calls=%fused_computation.20 | convolution fusion | flops 806354944 | bytes 3670016 | tf_op jit(solution)/shard_map/dot_general | solution.py:21
  97.9 1.3 %copy.15 = f32[512,512]{0,1:T(8,128)} copy(f32[512,512]{1,0:T(8,128)S(1)} %fusion.16) | data formatting | bytes 2097152 | tf_op jit(solution)/shard_map/dot_general | solution.py:21
  99.2 0.0 copy-done.1
  99.2 2.3 %fusion.10 = f32[512,512]{1,0:T(8,128)S(1)} fusion(f32[512,512]{1,0:T(8,128)S(1)} %copy-done.1, f32[512,512]{1,0:T(8,128)S(1)} %fusion.16, f32[512,512]{0,1:T(8,128)} %copy.15), kind=kOutput, calls=%fused_computation.15 | convolution fusion | flops 808976384 | bytes 4194304 | tf_op jit(solution)/shard_map/dot_general | solution.py:30
  101.6 0.0 copy-start.5
  101.6 0.0 copy-start.3
  101.6 0.0 copy-start.4
  101.6 1.0 fusion.35
  102.6 0.0 copy-start.2
  102.7 0.0 copy-done.5
  102.7 0.2 fusion.5
  102.9 0.7 reshape.57
  103.6 0.0 copy-done.2
  (4 shorter events, 0.0 us)
Async XLA Ops:
  0.6 94.8 %copy-start = (f32[512,512]{1,0:T(8,128)S(1)}, f32[512,512]{1,0:T(8,128)}, u32[]{:S(2)}) copy-start(f32[512,512]{1,0:T(8,128)} %param.12) | copy-start | bytes 3145732
  50.5 3.5 %copy-start.6 = (bf16[64,2,1,128]{3,1,2,0:T(2,128)(2,1)S(1)}, bf16[64,2,1,128]{3,1,2,0:T(2,128)(2,1)}, u32[]{:S(2)}) copy-start(bf16[64,2,1,128]{3,1,2,0:T(2,128)(2,1)} %param.11) | copy-start | bytes 98308
  50.5 40.3 %copy-start.7 = (bf16[1,31,64,512]{3,2,1,0:T(8,128)(2,1)S(1)}, bf16[1,31,64,512]{3,2,1,0:T(8,128)(2,1)}, u32[]{:S(2)}) copy-start(bf16[1,31,64,512]{3,2,1,0:T(8,128)(2,1)} %get-tuple-element.9) | copy-start | bytes 6094852
  95.4 3.8 %copy-start.1 = (f32[512,512]{1,0:T(8,128)S(1)}, f32[512,512]{1,0:T(8,128)}, u32[]{:S(2)}) copy-start(f32[512,512]{1,0:T(8,128)} %param.13) | copy-start | bytes 3145732
  101.6 1.1 %copy-start.5 = (bf16[64,2,1,128]{3,1,2,0:T(2,128)(2,1)S(1)}, bf16[64,2,1,128]{3,1,2,0:T(2,128)(2,1)}, u32[]{:S(2)}) copy-start(bf16[64,2,1,128]{3,1,2,0:T(2,128)(2,1)} %param.16) | copy-start | bytes 98308
  101.6 1.1 %copy-start.3 = (bf16[8,64,256]{2,1,0:T(8,128)(2,1)S(1)}, bf16[8,64,256]{2,1,0:T(8,128)(2,1)}, u32[]{:S(2)}) copy-start(bf16[8,64,256]{2,1,0:T(8,128)(2,1)} %get-tuple-element.11) | copy-start | bytes 786436
  101.6 1.1 %copy-start.4 = (f32[64,256]{1,0:T(8,128)S(1)}, f32[64,256]{1,0:T(8,128)}, u32[]{:S(2)}) copy-start(f32[64,256]{1,0:T(8,128)} %get-tuple-element.12) | copy-start | bytes 196612
  102.6 1.0 copy-start.2

commit v11 on v10

--- a/solution.py
+++ b/solution.py
@@ -31,6 +31,14 @@
     return jnp.dot(left_side, diag_inverse, precision=highest)
 
 
+def by_width(index, rows, width, action):
+    group = (rows * (index + 1) - 1) // 128
+    for j in range(width // 128):
+        @pl.when(group == j)
+        def _():
+            action(128 * (j + 1))
+
+
 def gather_kernel(n, line, x_ref, p_ref, out_ref, psum_ref, precv, psems, sems, local_sem):
     me = lax.axis_index("gc")
     row = lax.axis_index("gr")
@@ -46,6 +54,8 @@
     def cross_peer(k):
         return lax.rem(grp + k, lines) * line + pos
 
+    part_rows, part_width = p_ref.shape[1], p_ref.shape[2]
+    precv[...] = jnp.zeros(precv.shape, precv.dtype)
     barrier = pltpu.get_barrier_semaphore()
 
     def greet(k, carry):
@@ -55,11 +65,11 @@
     lax.fori_loop(1, n, greet, 0)
     pl.semaphore_wait(barrier, n - 1)
 
-    def part_copy(k, sender):
+    def part_copy(k, sender, cols):
         peer = lax.rem(me + k, n)
         return pltpu.make_async_remote_copy(
-            src_ref=p_ref.at[peer],
-            dst_ref=precv.at[sender],
+            src_ref=p_ref.at[peer, :, pl.ds(0, cols)],
+            dst_ref=precv.at[sender, :, pl.ds(0, cols)],
             send_sem=psems.at[0, k],
             recv_sem=psems.at[1, sender],
             device_id=(row, peer),
@@ -86,7 +96,7 @@
     lax.fori_loop(1, line, send_first, 0)
 
     def send_parts(k, carry):
-        part_copy(k, me).start()
+        by_width(lax.rem(me + k, n), part_rows, part_width, lambda cols: part_copy(k, me, cols).start())
         return carry
 
     lax.fori_loop(1, n, send_parts, 0)
@@ -158,8 +168,9 @@
     precv[me] = p_ref[me]
 
     def wait_parts(k, carry):
-        part_copy(k, me).wait_send()
-        part_copy(k, lax.rem(me + n - k, n)).wait_recv()
+        sender = lax.rem(me + n - k, n)
+        by_width(lax.rem(me + k, n), part_rows, part_width, lambda cols: part_copy(k, me, cols).wait_send())
+        by_width(me, part_rows, part_width, lambda cols: part_copy(k, sender, cols).wait_recv())
         return carry
 
     lax.fori_loop(1, n, wait_parts, 0)
@@ -196,6 +207,8 @@
     me = lax.axis_index("gr")
     col = lax.axis_index("gc")
     rows = prior_ref.shape[0]
+    piece_rows, piece_width = piece_ref.shape
+    cross_slots[...] = jnp.zeros(cross_slots.shape, cross_slots.dtype)
 
     barrier = pltpu.get_barrier_semaphore()
 
@@ -232,10 +245,10 @@
     def prior_copy(k, sender):
         return gr_copy(k, sender, prior_ref, prior_slots, 4)
 
-    def cross_copy(k, sender):
-        return pltpu.make_async_remote_copy(
-            src_ref=cross_slots.at[col],
-            dst_ref=cross_slots.at[sender],
+    def cross_copy(k, sender, cols):
+        return pltpu.make_async_remote_copy(
+            src_ref=cross_slots.at[col, :, pl.ds(0, cols)],
+            dst_ref=cross_slots.at[sender, :, pl.ds(0, cols)],
             send_sem=sems.at[6, k],
             recv_sem=sems.at[7, sender],
             device_id=(me, lax.rem(col + k, n_gc)),
@@ -267,7 +280,7 @@
     cross_slots[col] = piece.astype(cross_slots.dtype)
 
     def send_second(k, carry):
-        cross_copy(k, col).start()
+        by_width(col, piece_rows, piece_width, lambda cols: cross_copy(k, col, cols).start())
         return carry
 
     lax.fori_loop(1, n_gc, send_second, 0)
@@ -285,8 +298,9 @@
     crossing_out[...] = lax.fori_loop(0, n, add_crossing, jnp.zeros(crossing_out.shape, jnp.float32))
 
     def wait_second(k, carry):
-        cross_copy(k, col).wait_send()
-        cross_copy(k, lax.rem(col + n_gc - k, n_gc)).wait_recv()
+        sender = lax.rem(col + n_gc - k, n_gc)
+        by_width(col, piece_rows, piece_width, lambda cols: cross_copy(k, col, cols).wait_send())
+        by_width(sender, piece_rows, piece_width, lambda cols: cross_copy(k, sender, cols).wait_recv())
         return carry
 
     lax.fori_loop(1, n_gc, wait_second, 0)

time: 104 us -> 102 us (0.981)
  the two profiles are of different devices: /device:TPU:1 before, /device:TPU:7 now
where the time goes in v11:
time: 102 us
  Pallas kernels  78 us (76%)
  matrix products  13.9 us (14%)
  local copies, waits for them, and re-layouts  8.83 us (9%)
    pallas_call x1, Pallas kernels, gather_gc(): pl.pallas_call(functools.partial(gather_kernel, n, line), out_shape=(jax....  44.8 us
    pallas_call x1, Pallas kernels, reduce_gr(): pl.pallas_call(functools.partial(reduce_kernel, n, n_gc), out_shape=(jax....  33.1 us
    dot_general x2, matrix products, row_product(): lax.dot_general(left_rows, right_rows, (((0,), (0,)), ((), ())), preferre...  4.54 us
    unnamed x18, local copies, waits for them, and re-layouts  2.68 us
    dot_general x1, matrix products, diag_solve(): chol_proj = jnp.dot(diag_factor.T, diag_reduced, precision=highest)  2.49 us
    dot_general x1, matrix products, diag_solve(): left_side = jnp.dot(diag_inverse.T, symmetric, precision=highest)  2.33 us

profile of v11, /device:TPU:7, one launch (start us, length us, event | category | flops | bytes accessed | tf_op | source)
XLA Modules:
  0.0 101.5 jit_solution(14121722714769411029)
XLA Ops:
  0.6 0.0 copy-start
  0.6 1.0 reshape.47
  1.6 1.4 %convolution_convert_fusion.2 = bf16[62,512]{1,0:T(8,128)(2,1)S(1)} fusion(bf16[62,512]{1,0:T(8,128)(2,1)S(1)} %reshape.47, f32[512,512]{1,0:T(8,128)} %param.13), kind=kOutput, calls=%fused_computation.8 | convolution fusion | flops 32799744 | bytes 1175552 | tf_op jit(solution)/shard_map/dot_general | solution.py:369
  3.0 0.7 reshape.48.x_ref
  3.7 0.9 reshape.49
  4.6 1.1 %convolution_convert_fusion = bf16[512,512]{1,0:T(8,128)(2,1)} fusion(bf16[62,512]{1,0:T(8,128)(2,1)S(1)} %convolution_convert_fusion.2, bf16[62,512]{1,0:T(8,128)(2,1)S(1)} %reshape.49), kind=kOutput, calls=%fused_computation.6 | convolution fusion | flops 32768000 | bytes 651264 | tf_op jit(solution)/shard_map/dot_general | solution.py:14
  5.7 44.8 %shard_map.120 = (bf16[1,31,64,512]{3,2,1,0:T(8,128)(2,1)}, f32[16,512]{1,0:T(8,128)}) custom-call(bf16[1,31,2,512]{3,2,1,0:T(2,128)(2,1)} %reshape.48.x_ref, bf16[32,16,512]{2,1,0:T(8,128)(2,1)} %bitcast.56), custom_call_target="tpu_custom_call" | custom-call | tf_op jit(solution)/shard_map/pallas_call | solution.py:187
  50.5 0.0 copy-start.6
  50.5 0.0 copy-start.7
  50.5 3.4 %convolution_convert_fusion.1.crossing_ref = bf16[512,256]{1,0:T(8,128)(2,1)} fusion(bf16[1984,512]{1,0:T(8,128)(2,1)} %bitcast.64, bf16[248,8,2,128]{3,2,1,0:T(2,128)(2,1)} %bitcast.65), kind=kOutput, calls=%fused_computation.7 | convolution fusion | flops 520224768 | bytes 3309568 | tf_op jit(solution)/shard_map/dot_general | solution.py:14
  54.0 0.0 copy-done.6
  54.0 0.6 copy.34
  54.6 33.1 %shard_map.121 = (bf16[32,16,512]{2,1,0:T(8,128)(2,1)}, bf16[8,64,256]{2,1,0:T(8,128)(2,1)}, f32[64,256]{1,0:T(8,128)}) custom-call(bf16[512,256]{1,0:T(8,128)(2,1)} %convolution_convert_fusion.1.crossing_ref, f32[16,512]{1,0:T(8,128)} %get-tuple-element.10.piece_ref, bf16[64,256]{1,0:T(8,128)(2,1)} %bitcast.59), custom_call_target="tpu_custom_call" | custom-call | tf_op jit(solution)/shard_map/pallas_call | solution.py:321
  87.7 1.0 %reshape.53 = bf16[512,2,128]{2,1,0:T(2,128)(2,1)S(1)} reshape(bf16[8,64,256]{2,1,0:T(8,128)(2,1)} %get-tuple-element.11) | data formatting | bytes 524288 | tf_op jit(solution)/shard_map/reshape | solution.py:342
  88.8 0.0 copy-done.7
  88.8 1.9 %fusion.2 = bf16[31,1,64,2,1,128]{5,2,3,0,4,1:T(8,128)(2,1)S(1)} fusion(bf16[1,31,64,512]{3,2,1,0:T(8,128)(2,1)S(1)} %copy-done.7, bf16[31,1,64,2,1,128]{5,3,4,2,1,0:T(2,128)(2,1)} %param.14, bf16[512,2,128]{2,1,0:T(2,128)(2,1)S(1)} %reshape.53), kind=kOutput, calls=%fused_computation.3 | convolution fusion | flops 521617408 | bytes 4325376 | tf_op jit(solution)/shard_map/dot_general | solution.py:391
  90.7 2.0 %copy.16 = bf16[31,1,64,2,1,128]{5,3,4,2,1,0:T(2,128)(2,1)} copy(bf16[31,1,64,2,1,128]{5,2,3,0,4,1:T(8,128)(2,1)S(1)} %fusion.2) | data formatting | bytes 2031616
  92.7 0.7 reshape.55
  93.3 0.0 copy-done
  93.3 2.5 %fusion.16 = f32[512,512]{1,0:T(8,128)S(1)} fusion(f32[512,512]{1,0:T(8,128)S(1)} %copy-done, f32[512,512]{1,0:T(8,128)} %param.17, bf16[512,512]{1,0:T(8,128)(2,1)} %bitcast.58), kind=kOutput, calls=%fused_computation.20 | convolution fusion | flops 806354944 | bytes 3670016 | tf_op jit(solution)/shard_map/dot_general | solution.py:21
  95.8 1.3 %copy.15 = f32[512,512]{0,1:T(8,128)} copy(f32[512,512]{1,0:T(8,128)S(1)} %fusion.16) | data formatting | bytes 2097152 | tf_op jit(solution)/shard_map/dot_general | solution.py:21
  97.2 0.0 copy-done.1
  97.2 2.3 %fusion.10 = f32[512,512]{1,0:T(8,128)S(1)} fusion(f32[512,512]{1,0:T(8,128)S(1)} %copy-done.1, f32[512,512]{1,0:T(8,128)S(1)} %fusion.16, f32[512,512]{0,1:T(8,128)} %copy.15), kind=kOutput, calls=%fused_computation.15 | convolution fusion | flops 808976384 | bytes 4194304 | tf_op jit(solution)/shard_map/dot_general | solution.py:30
  99.5 0.0 copy-start.5
  99.5 0.0 copy-start.3
  99.5 0.0 copy-start.4
  99.5 1.0 %fusion.35 = f32[512,512]{1,0:T(8,128)S(1)} fusion(f32[512,512]{1,0:T(8,128)S(1)} %fusion.10, f32[512,512]{1,0:T(8,128)S(1)} %copy-done.1), kind=kOutput, calls=%fused_computation.45 | convolution fusion | flops 805306368 | bytes 3145728 | tf_op jit(solution)/shard_map/dot_general | solution.py:31
  100.6 0.0 copy-start.2
  100.6 0.0 copy-done.5
  100.6 0.2 fusion.5
  100.8 0.7 reshape.57
  101.5 0.0 copy-done.2
  (4 shorter events, 0.0 us)
Async XLA Ops:
  0.6 92.7 %copy-start = (f32[512,512]{1,0:T(8,128)S(1)}, f32[512,512]{1,0:T(8,128)}, u32[]{:S(2)}) copy-start(f32[512,512]{1,0:T(8,128)} %param.12) | copy-start | bytes 3145732
  50.5 3.5 %copy-start.6 = (bf16[64,2,1,128]{3,1,2,0:T(2,128)(2,1)S(1)}, bf16[64,2,1,128]{3,1,2,0:T(2,128)(2,1)}, u32[]{:S(2)}) copy-start(bf16[64,2,1,128]{3,1,2,0:T(2,128)(2,1)} %param.11) | copy-start | bytes 98308
  50.5 38.2 %copy-start.7 = (bf16[1,31,64,512]{3,2,1,0:T(8,128)(2,1)S(1)}, bf16[1,31,64,512]{3,2,1,0:T(8,128)(2,1)}, u32[]{:S(2)}) copy-start(bf16[1,31,64,512]{3,2,1,0:T(8,128)(2,1)} %get-tuple-element.9) | copy-start | bytes 6094852
  93.3 3.8 %copy-start.1 = (f32[512,512]{1,0:T(8,128)S(1)}, f32[512,512]{1,0:T(8,128)}, u32[]{:S(2)}) copy-start(f32[512,512]{1,0:T(8,128)} %param.13) | copy-start | bytes 3145732
  99.5 1.1 %copy-start.5 = (bf16[64,2,1,128]{3,1,2,0:T(2,128)(2,1)S(1)}, bf16[64,2,1,128]{3,1,2,0:T(2,128)(2,1)}, u32[]{:S(2)}) copy-start(bf16[64,2,1,128]{3,1,2,0:T(2,128)(2,1)} %param.16) | copy-start | bytes 98308
  99.5 1.1 %copy-start.3 = (bf16[8,64,256]{2,1,0:T(8,128)(2,1)S(1)}, bf16[8,64,256]{2,1,0:T(8,128)(2,1)}, u32[]{:S(2)}) copy-start(bf16[8,64,256]{2,1,0:T(8,128)(2,1)} %get-tuple-element.11) | copy-start | bytes 786436
  99.5 1.1 %copy-start.4 = (f32[64,256]{1,0:T(8,128)S(1)}, f32[64,256]{1,0:T(8,128)}, u32[]{:S(2)}) copy-start(f32[64,256]{1,0:T(8,128)} %get-tuple-element.12) | copy-start | bytes 196612
  100.6 1.0 copy-start.2

commit v12 on v11

--- a/solution.py
+++ b/solution.py
@@ -209,6 +209,7 @@
     rows = prior_ref.shape[0]
     piece_rows, piece_width = piece_ref.shape
     cross_slots[...] = jnp.zeros(cross_slots.shape, cross_slots.dtype)
+    recv_piece[...] = jnp.zeros(recv_piece.shape, recv_piece.dtype)
 
     barrier = pltpu.get_barrier_semaphore()
 
@@ -239,8 +240,15 @@
         src = crossing_ref.at[pl.ds(pl.multiple_of(peer * rows, rows), rows), :]
         return gr_copy(k, sender, src, recv_crossing, 0)
 
-    def piece_copy(k, sender):
-        return gr_copy(k, sender, piece_ref, recv_piece, 2)
+    def piece_copy(k, sender, cols):
+        return pltpu.make_async_remote_copy(
+            src_ref=piece_ref.at[:, pl.ds(0, cols)],
+            dst_ref=recv_piece.at[sender, :, pl.ds(0, cols)],
+            send_sem=sems.at[2, k],
+            recv_sem=sems.at[3, sender],
+            device_id=(lax.rem(me + k, n), col),
+            device_id_type=MESH_ID,
+        )
 
     def prior_copy(k, sender):
         return gr_copy(k, sender, prior_ref, prior_slots, 4)
@@ -256,7 +264,10 @@
         )
 
     def send_first(k, carry):
-        piece_copy(k, me).start()
+        by_width(col, piece_rows, piece_width, lambda cols: piece_copy(k, me, cols).start())
+        return carry
+
+    def send_rest(k, carry):
         crossing_copy(k, me).start()
         prior_copy(k, me).start()
         return carry
@@ -267,8 +278,9 @@
     recv_crossing[me] = crossing_ref[pl.ds(pl.multiple_of(me * rows, rows), rows), :]
 
     def wait_first(k, carry):
-        piece_copy(k, me).wait_send()
-        piece_copy(k, lax.rem(me + n - k, n)).wait_recv()
+        sender = lax.rem(me + n - k, n)
+        by_width(col, piece_rows, piece_width, lambda cols: piece_copy(k, me, cols).wait_send())
+        by_width(col, piece_rows, piece_width, lambda cols: piece_copy(k, sender, cols).wait_recv())
         return carry
 
     lax.fori_loop(1, n, wait_first, 0)
@@ -284,6 +296,7 @@
         return carry
 
     lax.fori_loop(1, n_gc, send_second, 0)
+    lax.fori_loop(1, n, send_rest, 0)
 
     def wait_crossing(k, carry):
         crossing_copy(k, me).wait_send()

time: 102 us -> 97.3 us (0.954)
  the two profiles are of different devices: /device:TPU:7 before, /device:TPU:6 now
where the time goes in v12:
time: 97.3 us; the launch traced here: 96.9 us
  Pallas kernels  73.3 us (75%)
  matrix products  13.9 us (14%)
  local copies, waits for them, and re-layouts  8.83 us (9%)
    pallas_call x1, Pallas kernels, gather_gc(): pl.pallas_call(functools.partial(gather_kernel, n, line), out_shape=(jax....  45.2 us
    pallas_call x1, Pallas kernels, reduce_gr(): pl.pallas_call(functools.partial(reduce_kernel, n, n_gc), out_shape=(jax....  28.1 us
    dot_general x2, matrix products, row_product(): lax.dot_general(left_rows, right_rows, (((0,), (0,)), ((), ())), preferre...  4.54 us
    unnamed x18, local copies, waits for them, and re-layouts  2.68 us
    dot_general x1, matrix products, diag_solve(): chol_proj = jnp.dot(diag_factor.T, diag_reduced, precision=highest)  2.49 us
    dot_general x1, matrix products, diag_solve(): left_side = jnp.dot(diag_inverse.T, symmetric, precision=highest)  2.33 us

profile of v12, /device:TPU:6, one launch (start us, length us, event | category | flops | bytes accessed | tf_op | source)
XLA Modules:
  0.0 96.9 jit_solution(17897280360005736672)
XLA Ops:
  0.6 0.0 copy-start
  0.6 1.0 reshape.47
  1.6 1.4 %convolution_convert_fusion.2 = bf16[62,512]{1,0:T(8,128)(2,1)S(1)} fusion(bf16[62,512]{1,0:T(8,128)(2,1)S(1)} %reshape.47, f32[512,512]{1,0:T(8,128)} %param.13), kind=kOutput, calls=%fused_computation.8 | convolution fusion | flops 32799744 | bytes 1175552 | tf_op jit(solution)/shard_map/dot_general | solution.py:382
  3.0 0.7 reshape.48.x_ref
  3.7 0.9 reshape.49
  4.6 1.1 %convolution_convert_fusion = bf16[512,512]{1,0:T(8,128)(2,1)} fusion(bf16[62,512]{1,0:T(8,128)(2,1)S(1)} %convolution_convert_fusion.2, bf16[62,512]{1,0:T(8,128)(2,1)S(1)} %reshape.49), kind=kOutput, calls=%fused_computation.6 | convolution fusion | flops 32768000 | bytes 651264 | tf_op jit(solution)/shard_map/dot_general | solution.py:14
  5.7 45.2 %shard_map.120 = (bf16[1,31,64,512]{3,2,1,0:T(8,128)(2,1)}, f32[16,512]{1,0:T(8,128)}) custom-call(bf16[1,31,2,512]{3,2,1,0:T(2,128)(2,1)} %reshape.48.x_ref, bf16[32,16,512]{2,1,0:T(8,128)(2,1)} %bitcast.56), custom_call_target="tpu_custom_call" | custom-call | tf_op jit(solution)/shard_map/pallas_call | solution.py:187
  50.9 0.0 copy-start.6
  50.9 0.0 copy-start.7
  50.9 3.4 %convolution_convert_fusion.1.crossing_ref = bf16[512,256]{1,0:T(8,128)(2,1)} fusion(bf16[1984,512]{1,0:T(8,128)(2,1)} %bitcast.64, bf16[248,8,2,128]{3,2,1,0:T(2,128)(2,1)} %bitcast.65), kind=kOutput, calls=%fused_computation.7 | convolution fusion | flops 520224768 | bytes 3309568 | tf_op jit(solution)/shard_map/dot_general | solution.py:14
  54.4 0.0 copy-done.6
  54.4 0.6 copy.34
  55.0 28.1 %shard_map.121 = (bf16[32,16,512]{2,1,0:T(8,128)(2,1)}, bf16[8,64,256]{2,1,0:T(8,128)(2,1)}, f32[64,256]{1,0:T(8,128)}) custom-call(bf16[512,256]{1,0:T(8,128)(2,1)} %convolution_convert_fusion.1.crossing_ref, f32[16,512]{1,0:T(8,128)} %get-tuple-element.10.piece_ref, bf16[64,256]{1,0:T(8,128)(2,1)} %bitcast.59), custom_call_target="tpu_custom_call" | custom-call | tf_op jit(solution)/shard_map/pallas_call | solution.py:334
  83.1 1.0 %reshape.53 = bf16[512,2,128]{2,1,0:T(2,128)(2,1)S(1)} reshape(bf16[8,64,256]{2,1,0:T(8,128)(2,1)} %get-tuple-element.11) | data formatting | bytes 524288 | tf_op jit(solution)/shard_map/reshape | solution.py:355
  84.1 0.0 copy-done.7
  84.1 1.9 %fusion.2 = bf16[31,1,64,2,1,128]{5,2,3,0,4,1:T(8,128)(2,1)S(1)} fusion(bf16[1,31,64,512]{3,2,1,0:T(8,128)(2,1)S(1)} %copy-done.7, bf16[31,1,64,2,1,128]{5,3,4,2,1,0:T(2,128)(2,1)} %param.14, bf16[512,2,128]{2,1,0:T(2,128)(2,1)S(1)} %reshape.53), kind=kOutput, calls=%fused_computation.3 | convolution fusion | flops 521617408 | bytes 4325376 | tf_op jit(solution)/shard_map/dot_general | solution.py:404
  86.0 2.0 %copy.16 = bf16[31,1,64,2,1,128]{5,3,4,2,1,0:T(2,128)(2,1)} copy(bf16[31,1,64,2,1,128]{5,2,3,0,4,1:T(8,128)(2,1)S(1)} %fusion.2) | data formatting | bytes 2031616
  88.0 0.7 reshape.55
  88.7 0.0 copy-done
  88.7 2.5 %fusion.16 = f32[512,512]{1,0:T(8,128)S(1)} fusion(f32[512,512]{1,0:T(8,128)S(1)} %copy-done, f32[512,512]{1,0:T(8,128)} %param.17, bf16[512,512]{1,0:T(8,128)(2,1)} %bitcast.58), kind=kOutput, calls=%fused_computation.20 | convolution fusion | flops 806354944 | bytes 3670016 | tf_op jit(solution)/shard_map/dot_general | solution.py:21
  91.2 1.3 %copy.15 = f32[512,512]{0,1:T(8,128)} copy(f32[512,512]{1,0:T(8,128)S(1)} %fusion.16) | data formatting | bytes 2097152 | tf_op jit(solution)/shard_map/dot_general | solution.py:21
  92.5 0.0 copy-done.1
  92.5 2.3 %fusion.10 = f32[512,512]{1,0:T(8,128)S(1)} fusion(f32[512,512]{1,0:T(8,128)S(1)} %copy-done.1, f32[512,512]{1,0:T(8,128)S(1)} %fusion.16, f32[512,512]{0,1:T(8,128)} %copy.15), kind=kOutput, calls=%fused_computation.15 | convolution fusion | flops 808976384 | bytes 4194304 | tf_op jit(solution)/shard_map/dot_general | solution.py:30
  94.8 0.0 copy-start.5
  94.8 0.0 copy-start.3
  94.9 0.0 copy-start.4
  94.9 1.0 %fusion.35 = f32[512,512]{1,0:T(8,128)S(1)} fusion(f32[512,512]{1,0:T(8,128)S(1)} %fusion.10, f32[512,512]{1,0:T(8,128)S(1)} %copy-done.1), kind=kOutput, calls=%fused_computation.45 | convolution fusion | flops 805306368 | bytes 3145728 | tf_op jit(solution)/shard_map/dot_general | solution.py:31
  95.9 0.0 copy-start.2
  95.9 0.0 copy-done.5
  96.0 0.2 fusion.5
  96.2 0.7 reshape.57
  96.9 0.0 copy-done.2
  (4 shorter events, 0.0 us)
Async XLA Ops:
  0.6 88.1 %copy-start = (f32[512,512]{1,0:T(8,128)S(1)}, f32[512,512]{1,0:T(8,128)}, u32[]{:S(2)}) copy-start(f32[512,512]{1,0:T(8,128)} %param.12) | copy-start | bytes 3145732
  50.9 3.5 %copy-start.6 = (bf16[64,2,1,128]{3,1,2,0:T(2,128)(2,1)S(1)}, bf16[64,2,1,128]{3,1,2,0:T(2,128)(2,1)}, u32[]{:S(2)}) copy-start(bf16[64,2,1,128]{3,1,2,0:T(2,128)(2,1)} %param.11) | copy-start | bytes 98308
  50.9 33.2 %copy-start.7 = (bf16[1,31,64,512]{3,2,1,0:T(8,128)(2,1)S(1)}, bf16[1,31,64,512]{3,2,1,0:T(8,128)(2,1)}, u32[]{:S(2)}) copy-start(bf16[1,31,64,512]{3,2,1,0:T(8,128)(2,1)} %get-tuple-element.9) | copy-start | bytes 6094852
  88.7 3.8 %copy-start.1 = (f32[512,512]{1,0:T(8,128)S(1)}, f32[512,512]{1,0:T(8,128)}, u32[]{:S(2)}) copy-start(f32[512,512]{1,0:T(8,128)} %param.13) | copy-start | bytes 3145732
  94.8 1.1 %copy-start.5 = (bf16[64,2,1,128]{3,1,2,0:T(2,128)(2,1)S(1)}, bf16[64,2,1,128]{3,1,2,0:T(2,128)(2,1)}, u32[]{:S(2)}) copy-start(bf16[64,2,1,128]{3,1,2,0:T(2,128)(2,1)} %param.16) | copy-start | bytes 98308
  94.8 1.1 %copy-start.3 = (bf16[8,64,256]{2,1,0:T(8,128)(2,1)S(1)}, bf16[8,64,256]{2,1,0:T(8,128)(2,1)}, u32[]{:S(2)}) copy-start(bf16[8,64,256]{2,1,0:T(8,128)(2,1)} %get-tuple-element.11) | copy-start | bytes 786436
  94.9 1.1 %copy-start.4 = (f32[64,256]{1,0:T(8,128)S(1)}, f32[64,256]{1,0:T(8,128)}, u32[]{:S(2)}) copy-start(f32[64,256]{1,0:T(8,128)} %get-tuple-element.12) | copy-start | bytes 196612
  95.9 1.0 %copy-start.2 = (f32[512,512]{1,0:T(8,128)}, f32[512,512]{1,0:T(8,128)S(1)}, u32[]{:S(2)}) copy-start(f32[512,512]{1,0:T(8,128)S(1)} %fusion.35) | copy-start | bytes 3145732

commit v13 on v12

--- a/solution.py
+++ b/solution.py
@@ -379,14 +379,19 @@
     below_mat = below_factor.reshape(local_rows, local_cols)
     below_bar = below_adjoint.reshape(local_rows, local_cols)
     inverse_bf = diag_inverse.astype(jnp.bfloat16)
-    own_grad = jnp.dot(
-        panel_adjoint.reshape(tile_count * own_rows, width),
+    own_grad = lax.dot_general(
+        panel_adjoint.reshape(tile_count, own_rows, width),
         inverse_bf,
+        (((2,), (0,)), ((), ())),
         preferred_element_type=jnp.float32,
     ).astype(jnp.bfloat16)
     panel_grad = own_grad.reshape(panel_adjoint.shape)
-    own_factor = panel_factor.reshape(tile_count * own_rows, width)
-    own_part = row_product(own_grad, own_factor).astype(jnp.bfloat16)
+    own_part = lax.dot_general(
+        own_grad,
+        panel_factor.reshape(tile_count, own_rows, width),
+        (((0, 1), (0, 1)), ((), ())),
+        preferred_element_type=jnp.float32,
+    ).astype(jnp.bfloat16)
     whole, piece = gather_gc(
         own_grad.reshape(1, tile_count, own_rows, width),
         own_part.reshape(n_gc, width // n_gc, width),

time: 97.3 us -> 95.1 us (0.977)
  local copies, waits for them, and re-layouts: 8.83 us -> 7.17 us
    reshape x4 -> x0, local copies, waits for them, and re-layouts: 3.13 us -> none  [the longest x1 0.95 us: local(): panel_adjoint.reshape(tile_count * own_rows, width)]
    dot_general x1 -> x2, matrix products: 1.43 us -> 3.5 us  [the longest x1 1.95 us: local(): lax.dot_general(own_grad, panel_factor.reshape(tile_count, own_rows, widt...]
    unnamed x18 -> x25, local copies, waits for them, and re-layouts: 2.68 us -> 4.14 us
    dot_general x1, matrix products: 2.49 us -> 1.06 us  [diag_solve(): chol_proj = jnp.dot(diag_factor.T, diag_reduced, precision=highest)]
    dot_general x2 -> x1, matrix products: 4.54 us -> 3.43 us  [row_product(): lax.dot_general(left_rows, right_rows, (((0,), (0,)), ((), ())), preferre...]
where the time goes in v13:
time: 95.1 us; the launch traced here: 94.8 us
  Pallas kernels  73.3 us (77%)
  matrix products  13.4 us (14%)
  local copies, waits for them, and re-layouts  7.17 us (8%)
    pallas_call x1, Pallas kernels, gather_gc(): pl.pallas_call(functools.partial(gather_kernel, n, line), out_shape=(jax....  45.2 us
    pallas_call x1, Pallas kernels, reduce_gr(): pl.pallas_call(functools.partial(reduce_kernel, n, n_gc), out_shape=(jax....  28.1 us
    unnamed x25, local copies, waits for them, and re-layouts  4.14 us
    dot_general x1, matrix products, row_product(): lax.dot_general(left_rows, right_rows, (((0,), (0,)), ((), ())), preferre...  3.43 us
    dot_general x1, matrix products, diag_solve(): left_side = jnp.dot(diag_inverse.T, symmetric, precision=highest)  2.33 us
    dot_general x1, matrix products, local(): lax.dot_general(own_grad, panel_factor.reshape(tile_count, own_rows, widt...  1.95 us
    dot_general x1, matrix products, local(): lax.dot_general(grad_rows.reshape(tile_count, tile_rows, width), prior_fa...  1.9 us

profile of v13, /device:TPU:6, one launch (start us, length us, event | category | flops | bytes accessed | tf_op | source)
XLA Modules:
  0.0 94.8 jit_solution(8736621682037859397)
XLA Ops:
  0.6 0.0 copy-start
  0.6 1.6 %convolution_convert_fusion.1 = bf16[31,2,512]{2,0,1:T(8,128)(2,1)S(1)} fusion(f32[512,512]{1,0:T(8,128)} %param.13, bf16[31,2,512]{2,1,0:T(2,128)(2,1)} %bitcast.74), kind=kOutput, calls=%fused_computation.9 | convolution fusion | flops 32799744 | bytes 1175552 | tf_op jit(solution)/shard_map/dot_general | solution.py:382
  2.2 0.7 copy.49
  2.9 0.1 copy.27
  3.0 1.9 %fusion.5 = bf16[512,512]{1,0:T(8,128)(2,1)} fusion(bf16[31,2,512]{2,1,0:T(2,128)(2,1)} %bitcast.75, bf16[31,2,512]{2,1,0:T(2,128)(2,1)S(1)} %copy.27), kind=kOutput, calls=%fused_computation.7 | convolution fusion | flops 32768000 | bytes 651264 | tf_op jit(solution)/shard_map/dot_general | solution.py:389
  4.9 45.2 %shard_map.120 = (bf16[1,31,64,512]{3,2,1,0:T(8,128)(2,1)}, f32[16,512]{1,0:T(8,128)}) custom-call(bf16[1,31,2,512]{3,2,1,0:T(2,128)(2,1)} %bitcast.72, bf16[32,16,512]{2,1,0:T(8,128)(2,1)} %bitcast.69), custom_call_target="tpu_custom_call" | custom-call | tf_op jit(solution)/shard_map/pallas_call | solution.py:187
  50.1 0.0 copy-start.8
  50.1 0.0 copy-start.9
  50.2 3.4 %convolution_convert_fusion.crossing_ref = bf16[512,256]{1,0:T(8,128)(2,1)} fusion(bf16[1984,512]{1,0:T(8,128)(2,1)} %bitcast.80, bf16[248,8,2,128]{3,2,1,0:T(2,128)(2,1)} %bitcast.81), kind=kOutput, calls=%fused_computation.8 | convolution fusion | flops 520224768 | bytes 3309568 | tf_op jit(solution)/shard_map/dot_general | solution.py:14
  53.6 0.0 copy-done.8
  53.6 0.6 copy.47
  54.2 28.1 %shard_map.121 = (bf16[32,16,512]{2,1,0:T(8,128)(2,1)}, bf16[8,64,256]{2,1,0:T(8,128)(2,1)}, f32[64,256]{1,0:T(8,128)}) custom-call(bf16[512,256]{1,0:T(8,128)(2,1)} %convolution_convert_fusion.crossing_ref, f32[16,512]{1,0:T(8,128)} %get-tuple-element.10.piece_ref, bf16[64,256]{1,0:T(8,128)(2,1)} %bitcast.73), custom_call_target="tpu_custom_call" | custom-call | tf_op jit(solution)/shard_map/pallas_call | solution.py:334
  82.3 1.0 %reshape.53 = bf16[512,2,128]{2,1,0:T(2,128)(2,1)S(1)} reshape(bf16[8,64,256]{2,1,0:T(8,128)(2,1)} %get-tuple-element.11) | data formatting | bytes 524288 | tf_op jit(solution)/shard_map/reshape | solution.py:355
  83.4 0.0 copy-done.9
  83.4 1.9 %fusion.2 = bf16[31,1,64,2,1,128]{5,2,3,0,4,1:T(8,128)(2,1)S(1)} fusion(bf16[1,31,64,512]{3,2,1,0:T(8,128)(2,1)S(1)} %copy-done.9, bf16[31,1,64,2,1,128]{5,3,4,2,1,0:T(2,128)(2,1)} %param.14, bf16[512,2,128]{2,1,0:T(2,128)(2,1)S(1)} %reshape.53), kind=kOutput, calls=%fused_computation.3 | convolution fusion | flops 521617408 | bytes 4325376 | tf_op jit(solution)/shard_map/dot_general | solution.py:409
  85.3 0.0 copy-start.3
  85.3 0.0 copy-start.5
  85.3 2.0 %copy.20 = bf16[31,1,64,2,1,128]{5,3,4,2,1,0:T(2,128)(2,1)} copy(bf16[31,1,64,2,1,128]{5,2,3,0,4,1:T(8,128)(2,1)S(1)} %fusion.2) | data formatting | bytes 2031616
  87.3 0.7 copy.48
  88.0 0.0 copy-done
  88.0 0.0 copy-done.3
  88.0 0.0 copy-done.5
  88.0 1.1 %fusion.17 = f32[512,512]{1,0:T(8,128)S(1)} fusion(f32[512,512]{1,0:T(8,128)S(1)} %copy-done, f32[512,512]{1,0:T(8,128)S(1)} %copy-done.3, bf16[512,512]{1,0:T(8,128)(2,1)S(1)} %bitcast.71), kind=kOutput, calls=%fused_computation.21 | convolution fusion | flops 806354944 | bytes 3670016 | tf_op jit(solution)/shard_map/dot_general | solution.py:21
  89.1 1.3 %copy.19 = f32[512,512]{0,1:T(8,128)} copy(f32[512,512]{1,0:T(8,128)S(1)} %fusion.17) | data formatting | bytes 2097152 | tf_op jit(solution)/shard_map/dot_general | solution.py:21
  90.4 0.0 copy-done.1
  90.4 2.3 %fusion.11 = f32[512,512]{1,0:T(8,128)S(1)} fusion(f32[512,512]{1,0:T(8,128)S(1)} %copy-done.1, f32[512,512]{1,0:T(8,128)S(1)} %fusion.17, f32[512,512]{0,1:T(8,128)} %copy.19), kind=kOutput, calls=%fused_computation.16 | convolution fusion | flops 808976384 | bytes 4194304 | tf_op jit(solution)/shard_map/dot_general | solution.py:30
  92.7 0.0 copy-start.7
  92.8 1.0 %fusion.40 = f32[512,512]{1,0:T(8,128)S(1)} fusion(f32[512,512]{1,0:T(8,128)S(1)} %fusion.11, f32[512,512]{1,0:T(8,128)S(1)} %copy-done.1), kind=kOutput, calls=%fused_computation.50 | convolution fusion | flops 805306368 | bytes 3145728 | tf_op jit(solution)/shard_map/dot_general | solution.py:31
  93.8 0.0 copy-start.2
  93.9 0.2 fusion.6
  94.0 0.7 reshape.57
  94.7 0.0 copy-done.2
  (7 shorter events, 0.0 us)
Async XLA Ops:
  0.6 87.4 %copy-start = (f32[512,512]{1,0:T(8,128)S(1)}, f32[512,512]{1,0:T(8,128)}, u32[]{:S(2)}) copy-start(f32[512,512]{1,0:T(8,128)} %param.12) | copy-start | bytes 3145732
  50.1 3.5 %copy-start.8 = (bf16[64,2,1,128]{3,1,2,0:T(2,128)(2,1)S(1)}, bf16[64,2,1,128]{3,1,2,0:T(2,128)(2,1)}, u32[]{:S(2)}) copy-start(bf16[64,2,1,128]{3,1,2,0:T(2,128)(2,1)} %param.11) | copy-start | bytes 98308
  50.1 33.2 %copy-start.9 = (bf16[1,31,64,512]{3,2,1,0:T(8,128)(2,1)S(1)}, bf16[1,31,64,512]{3,2,1,0:T(8,128)(2,1)}, u32[]{:S(2)}) copy-start(bf16[1,31,64,512]{3,2,1,0:T(8,128)(2,1)} %get-tuple-element.9) | copy-start | bytes 6094852
  85.3 2.7 %copy-start.3 = (f32[512,512]{1,0:T(8,128)S(1)}, f32[512,512]{1,0:T(8,128)}, u32[]{:S(2)}) copy-start(f32[512,512]{1,0:T(8,128)} %param.17) | copy-start | bytes 3145732
  85.3 2.7 %copy-start.5 = (bf16[32,16,512]{2,1,0:T(8,128)(2,1)S(1)}, bf16[32,16,512]{2,1,0:T(8,128)(2,1)}, u32[]{:S(2)}) copy-start(bf16[32,16,512]{2,1,0:T(8,128)(2,1)} %get-tuple-element.13) | copy-start | bytes 1572868
  88.0 2.4 %copy-start.1 = (f32[512,512]{1,0:T(8,128)S(1)}, f32[512,512]{1,0:T(8,128)}, u32[]{:S(2)}) copy-start(f32[512,512]{1,0:T(8,128)} %param.13) | copy-start | bytes 3145732
  92.7 1.1 %copy-start.7 = (bf16[64,2,1,128]{3,1,2,0:T(2,128)(2,1)S(1)}, bf16[64,2,1,128]{3,1,2,0:T(2,128)(2,1)}, u32[]{:S(2)}) copy-start(bf16[64,2,1,128]{3,1,2,0:T(2,128)(2,1)} %param.16) | copy-start | bytes 98308
  92.7 1.1 %copy-start.4 = (bf16[8,64,256]{2,1,0:T(8,128)(2,1)S(1)}, bf16[8,64,256]{2,1,0:T(8,128)(2,1)}, u32[]{:S(2)}) copy-start(bf16[8,64,256]{2,1,0:T(8,128)(2,1)} %get-tuple-element.11) | copy-start | bytes 786436
  92.7 1.1 %copy-start.6 = (f32[64,256]{1,0:T(8,128)S(1)}, f32[64,256]{1,0:T(8,128)}, u32[]{:S(2)}) copy-start(f32[64,256]{1,0:T(8,128)} %get-tuple-element.12) | copy-start | bytes 196612
  93.8 1.0 %copy-start.2 = (f32[512,512]{1,0:T(8,128)}, f32[512,512]{1,0:T(8,128)S(1)}, u32[]{:S(2)}) copy-start(f32[512,512]{1,0:T(8,128)S(1)} %fusion.40) | copy-start | bytes 3145732

commit v14 on v13

--- a/solution.py
+++ b/solution.py
@@ -39,7 +39,8 @@
             action(128 * (j + 1))
 
 
-def gather_kernel(n, line, x_ref, p_ref, out_ref, psum_ref, precv, psems, sems, local_sem):
+def gather_kernel(n, line, n_gr, x_ref, p_ref, out_ref, cross_out, precv, recv_piece, cross_slots,
+                  psems, sems, local_sem):
     me = lax.axis_index("gc")
     row = lax.axis_index("gr")
     rows = x_ref.shape[2]
@@ -56,14 +57,21 @@
 
     part_rows, part_width = p_ref.shape[1], p_ref.shape[2]
     precv[...] = jnp.zeros(precv.shape, precv.dtype)
+    recv_piece[...] = jnp.zeros(recv_piece.shape, recv_piece.dtype)
+    cross_slots[...] = jnp.zeros(cross_slots.shape, cross_slots.dtype)
     barrier = pltpu.get_barrier_semaphore()
 
     def greet(k, carry):
         pl.semaphore_signal(barrier, inc=1, device_id=(row, lax.rem(me + k, n)), device_id_type=MESH_ID)
         return carry
 
+    def greet_gr(k, carry):
+        pl.semaphore_signal(barrier, inc=1, device_id=(lax.rem(row + k, n_gr), me), device_id_type=MESH_ID)
+        return carry
+
     lax.fori_loop(1, n, greet, 0)
-    pl.semaphore_wait(barrier, n - 1)
+    lax.fori_loop(1, n_gr, greet_gr, 0)
+    pl.semaphore_wait(barrier, n + n_gr - 2)
 
     def part_copy(k, sender, cols):
         peer = lax.rem(me + k, n)
@@ -144,6 +152,68 @@
 
     lax.fori_loop(1, line, relay, 0)
 
+    precv[me] = p_ref[me]
+
+    def wait_parts(k, carry):
+        sender = lax.rem(me + n - k, n)
+        by_width(lax.rem(me + k, n), part_rows, part_width, lambda cols: part_copy(k, me, cols).wait_send())
+        by_width(me, part_rows, part_width, lambda cols: part_copy(k, sender, cols).wait_recv())
+        return carry
+
+    lax.fori_loop(1, n, wait_parts, 0)
+
+    def add_part(j, total):
+        return total + precv[j].astype(jnp.float32)
+
+    piece = lax.fori_loop(0, n, add_part, jnp.zeros(recv_piece.shape[1:], jnp.float32))
+    recv_piece[row] = piece
+
+    def piece_copy(k, sender, cols):
+        return pltpu.make_async_remote_copy(
+            src_ref=recv_piece.at[row, :, pl.ds(0, cols)],
+            dst_ref=recv_piece.at[sender, :, pl.ds(0, cols)],
+            send_sem=psems.at[2, k],
+            recv_sem=psems.at[3, sender],
+            device_id=(lax.rem(row + k, n_gr), me),
+            device_id_type=MESH_ID,
+        )
+
+    def send_piece(k, carry):
+        by_width(me, part_rows, part_width, lambda cols: piece_copy(k, row, cols).start())
+        return carry
+
+    lax.fori_loop(1, n_gr, send_piece, 0)
+
+    def wait_piece(k, carry):
+        sender = lax.rem(row + n_gr - k, n_gr)
+        by_width(me, part_rows, part_width, lambda cols: piece_copy(k, row, cols).wait_send())
+        by_width(me, part_rows, part_width, lambda cols: piece_copy(k, sender, cols).wait_recv())
+        return carry
+
+    lax.fori_loop(1, n_gr, wait_piece, 0)
+
+    def add_piece(j, total):
+        return total + recv_piece[j]
+
+    summed = lax.fori_loop(0, n_gr, add_piece, jnp.zeros(recv_piece.shape[1:], jnp.float32))
+    cross_slots[me] = summed.astype(cross_slots.dtype)
+
+    def cross_copy(k, sender, cols):
+        return pltpu.make_async_remote_copy(
+            src_ref=cross_slots.at[me, :, pl.ds(0, cols)],
+            dst_ref=cross_slots.at[sender, :, pl.ds(0, cols)],
+            send_sem=psems.at[4, k],
+            recv_sem=psems.at[5, sender],
+            device_id=(row, lax.rem(me + k, n)),
+            device_id_type=MESH_ID,
+        )
+
+    def send_cross(k, carry):
+        by_width(me, part_rows, part_width, lambda cols: cross_copy(k, me, cols).start())
+        return carry
+
+    lax.fori_loop(1, n, send_cross, 0)
+
     def wait_first(k, carry):
         first(k, pos).wait_send()
         return carry
@@ -165,36 +235,32 @@
 
     lax.fori_loop(1, lines, wait_lines, 0)
 
-    precv[me] = p_ref[me]
-
-    def wait_parts(k, carry):
+    def wait_cross(k, carry):
         sender = lax.rem(me + n - k, n)
-        by_width(lax.rem(me + k, n), part_rows, part_width, lambda cols: part_copy(k, me, cols).wait_send())
-        by_width(me, part_rows, part_width, lambda cols: part_copy(k, sender, cols).wait_recv())
-        return carry
-
-    lax.fori_loop(1, n, wait_parts, 0)
-
-    def add_part(j, total):
-        return total + precv[j].astype(jnp.float32)
-
-    psum_ref[...] = lax.fori_loop(0, n, add_part, jnp.zeros(psum_ref.shape, jnp.float32))
-
-
-def gather_gc(block, part, n, line):
+        by_width(me, part_rows, part_width, lambda cols: cross_copy(k, me, cols).wait_send())
+        by_width(sender, part_rows, part_width, lambda cols: cross_copy(k, sender, cols).wait_recv())
+        return carry
+
+    lax.fori_loop(1, n, wait_cross, 0)
+    cross_out[...] = cross_slots[...]
+
+
+def gather_gc(block, part, n, line, n_gr):
     count, tiles, rows, width = block.shape
     vmem = pl.BlockSpec(memory_space=pltpu.VMEM)
     return pl.pallas_call(
-        functools.partial(gather_kernel, n, line),
+        functools.partial(gather_kernel, n, line, n_gr),
         out_shape=(
             jax.ShapeDtypeStruct((count, tiles, rows * n, width), block.dtype),
-            jax.ShapeDtypeStruct(part.shape[1:], jnp.float32),
+            jax.ShapeDtypeStruct(part.shape, jnp.bfloat16),
         ),
         in_specs=[pl.BlockSpec(memory_space=pl.ANY), vmem],
         out_specs=(pl.BlockSpec(memory_space=pl.ANY), vmem),
         scratch_shapes=[
             pltpu.VMEM(part.shape, part.dtype),
-            pltpu.SemaphoreType.DMA((2, n)),
+            pltpu.VMEM((n_gr,) + part.shape[1:], jnp.float32),
+            pltpu.VMEM(part.shape, jnp.bfloat16),
+            pltpu.SemaphoreType.DMA((6, max(n, n_gr))),
             pltpu.SemaphoreType.DMA((2 + line, line + n // line)),
             pltpu.SemaphoreType.DMA,
         ],
@@ -202,14 +268,10 @@
     )(block, part)
 
 
-def reduce_kernel(n, n_gc, crossing_ref, piece_ref, prior_ref, cross_out, prior_out, crossing_out,
-                  recv_crossing, recv_piece, prior_slots, cross_slots, sems):
+def reduce_kernel(n, crossing_ref, prior_ref, prior_out, crossing_out, recv_crossing, prior_slots, sems):
     me = lax.axis_index("gr")
     col = lax.axis_index("gc")
     rows = prior_ref.shape[0]
-    piece_rows, piece_width = piece_ref.shape
-    cross_slots[...] = jnp.zeros(cross_slots.shape, cross_slots.dtype)
-    recv_piece[...] = jnp.zeros(recv_piece.shape, recv_piece.dtype)
 
     barrier = pltpu.get_barrier_semaphore()
 
@@ -217,13 +279,8 @@
         pl.semaphore_signal(barrier, inc=1, device_id=(lax.rem(me + k, n), col), device_id_type=MESH_ID)
         return carry
 
-    def greet_gc(k, carry):
-        pl.semaphore_signal(barrier, inc=1, device_id=(me, lax.rem(col + k, n_gc)), device_id_type=MESH_ID)
-        return carry
-
     lax.fori_loop(1, n, greet_gr, 0)
-    lax.fori_loop(1, n_gc, greet_gc, 0)
-    pl.semaphore_wait(barrier, n + n_gc - 2)
+    pl.semaphore_wait(barrier, n - 1)
 
     def gr_copy(k, sender, src, dst, index):
         return pltpu.make_async_remote_copy(
@@ -240,115 +297,53 @@
         src = crossing_ref.at[pl.ds(pl.multiple_of(peer * rows, rows), rows), :]
         return gr_copy(k, sender, src, recv_crossing, 0)
 
-    def piece_copy(k, sender, cols):
-        return pltpu.make_async_remote_copy(
-            src_ref=piece_ref.at[:, pl.ds(0, cols)],
-            dst_ref=recv_piece.at[sender, :, pl.ds(0, cols)],
-            send_sem=sems.at[2, k],
-            recv_sem=sems.at[3, sender],
-            device_id=(lax.rem(me + k, n), col),
-            device_id_type=MESH_ID,
-        )
-
     def prior_copy(k, sender):
-        return gr_copy(k, sender, prior_ref, prior_slots, 4)
-
-    def cross_copy(k, sender, cols):
-        return pltpu.make_async_remote_copy(
-            src_ref=cross_slots.at[col, :, pl.ds(0, cols)],
-            dst_ref=cross_slots.at[sender, :, pl.ds(0, cols)],
-            send_sem=sems.at[6, k],
-            recv_sem=sems.at[7, sender],
-            device_id=(me, lax.rem(col + k, n_gc)),
-            device_id_type=MESH_ID,
-        )
-
-    def send_first(k, carry):
-        by_width(col, piece_rows, piece_width, lambda cols: piece_copy(k, me, cols).start())
-        return carry
-
-    def send_rest(k, carry):
+        return gr_copy(k, sender, prior_ref, prior_slots, 2)
+
+    def send(k, carry):
         crossing_copy(k, me).start()
         prior_copy(k, me).start()
         return carry
 
-    lax.fori_loop(1, n, send_first, 0)
+    lax.fori_loop(1, n, send, 0)
     prior_slots[me] = prior_ref[...]
-    recv_piece[me] = piece_ref[...]
     recv_crossing[me] = crossing_ref[pl.ds(pl.multiple_of(me * rows, rows), rows), :]
 
-    def wait_first(k, carry):
+    def wait(k, carry):
         sender = lax.rem(me + n - k, n)
-        by_width(col, piece_rows, piece_width, lambda cols: piece_copy(k, me, cols).wait_send())
-        by_width(col, piece_rows, piece_width, lambda cols: piece_copy(k, sender, cols).wait_recv())
-        return carry
-
-    lax.fori_loop(1, n, wait_first, 0)
-
-    def add_piece(j, total):
-        return total + recv_piece[j]
-
-    piece = lax.fori_loop(0, n, add_piece, jnp.zeros(piece_ref.shape, jnp.float32))
-    cross_slots[col] = piece.astype(cross_slots.dtype)
-
-    def send_second(k, carry):
-        by_width(col, piece_rows, piece_width, lambda cols: cross_copy(k, col, cols).start())
-        return carry
-
-    lax.fori_loop(1, n_gc, send_second, 0)
-    lax.fori_loop(1, n, send_rest, 0)
-
-    def wait_crossing(k, carry):
         crossing_copy(k, me).wait_send()
-        crossing_copy(k, lax.rem(me + n - k, n)).wait_recv()
-        return carry
-
-    lax.fori_loop(1, n, wait_crossing, 0)
+        crossing_copy(k, sender).wait_recv()
+        prior_copy(k, me).wait_send()
+        prior_copy(k, sender).wait_recv()
+        return carry
+
+    lax.fori_loop(1, n, wait, 0)
 
     def add_crossing(j, total):
         return total + recv_crossing[j].astype(jnp.float32)
 
     crossing_out[...] = lax.fori_loop(0, n, add_crossing, jnp.zeros(crossing_out.shape, jnp.float32))
-
-    def wait_second(k, carry):
-        sender = lax.rem(col + n_gc - k, n_gc)
-        by_width(col, piece_rows, piece_width, lambda cols: cross_copy(k, col, cols).wait_send())
-        by_width(sender, piece_rows, piece_width, lambda cols: cross_copy(k, sender, cols).wait_recv())
-        return carry
-
-    lax.fori_loop(1, n_gc, wait_second, 0)
-
-    def wait_prior(k, carry):
-        prior_copy(k, me).wait_send()
-        prior_copy(k, lax.rem(me + n - k, n)).wait_recv()
-        return carry
-
-    lax.fori_loop(1, n, wait_prior, 0)
-    cross_out[...] = cross_slots[...]
     prior_out[...] = prior_slots[...]
 
 
-def reduce_gr(crossing_part, piece, prior_rows, n, n_gc):
+def reduce_gr(crossing_part, prior_rows, n):
     rows, cols = prior_rows.shape
     vmem = pl.BlockSpec(memory_space=pltpu.VMEM)
     return pl.pallas_call(
-        functools.partial(reduce_kernel, n, n_gc),
+        functools.partial(reduce_kernel, n),
         out_shape=(
-            jax.ShapeDtypeStruct((n_gc,) + piece.shape, jnp.bfloat16),
             jax.ShapeDtypeStruct((n, rows, cols), prior_rows.dtype),
             jax.ShapeDtypeStruct((rows, cols), jnp.float32),
         ),
-        in_specs=[vmem, vmem, vmem],
-        out_specs=(vmem, vmem, vmem),
+        in_specs=[vmem, vmem],
+        out_specs=(vmem, vmem),
         scratch_shapes=[
             pltpu.VMEM((n, rows, cols), crossing_part.dtype),
-            pltpu.VMEM((n,) + piece.shape, jnp.float32),
             pltpu.VMEM((n, rows, cols), prior_rows.dtype),
-            pltpu.VMEM((n_gc,) + piece.shape, jnp.bfloat16),
-            pltpu.SemaphoreType.DMA((8, max(n, n_gc))),
+            pltpu.SemaphoreType.DMA((4, n)),
         ],
         compiler_params=pltpu.CompilerParams(collective_id=1, has_side_effects=True),
-    )(crossing_part, piece, prior_rows)
+    )(crossing_part, prior_rows)
 
 
 def prior_factor_rows(prior_rows, below_shape):
@@ -392,16 +387,17 @@
         (((0, 1), (0, 1)), ((), ())),
         preferred_element_type=jnp.float32,
     ).astype(jnp.bfloat16)
-    whole, piece = gather_gc(
+    whole, cross_rows = gather_gc(
         own_grad.reshape(1, tile_count, own_rows, width),
         own_part.reshape(n_gc, width // n_gc, width),
         n_gc,
         line,
+        n_gr,
     )
     grad_rows = whole[0].reshape(local_rows, width)
     prior_here = prior_factor.reshape(prior_local, local_cols)
     crossing_part = row_product(grad_rows, below_mat).astype(jnp.bfloat16)
-    cross_rows, prior_rows, crossing = reduce_gr(crossing_part, piece, prior_here, n_gr, n_gc)
+    prior_rows, crossing = reduce_gr(crossing_part, prior_here, n_gr)
     summed = cross_rows.reshape(width, width).astype(jnp.float32)
     prior_whole = prior_rows.reshape(width, local_cols)
     diag_reduced = jnp.tril(diag_adjoint - summed)

time: 95.1 us -> 90.7 us (0.954)
  the two profiles are of different devices: /device:TPU:6 before, /device:TPU:7 now
where the time goes in v14:
time: 90.7 us; the launch traced here: 90.4 us
  Pallas kernels  68.9 us (76%)
  matrix products  13.4 us (15%)
  local copies, waits for them, and re-layouts  7.17 us (8%)
    pallas_call x1, Pallas kernels, gather_gc(): pl.pallas_call(functools.partial(gather_kernel, n, line, n_gr), out_shape...  56.9 us
    pallas_call x1, Pallas kernels, reduce_gr(): pl.pallas_call(functools.partial(reduce_kernel, n), out_shape=(jax.ShapeD...  12.1 us
    unnamed x25, local copies, waits for them, and re-layouts  4.14 us
    dot_general x1, matrix products, row_product(): lax.dot_general(left_rows, right_rows, (((0,), (0,)), ((), ())), preferre...  3.43 us
    dot_general x1, matrix products, diag_solve(): left_side = jnp.dot(diag_inverse.T, symmetric, precision=highest)  2.33 us
    dot_general x1, matrix products, local(): lax.dot_general(own_grad, panel_factor.reshape(tile_count, own_rows, widt...  1.95 us
    dot_general x1, matrix products, local(): lax.dot_general(grad_rows.reshape(tile_count, tile_rows, width), prior_fa...  1.91 us

profile of v14, /device:TPU:7, one launch (start us, length us, event | category | flops | bytes accessed | tf_op | source)
XLA Modules:
  0.0 90.4 jit_solution(8912441925423217752)
XLA Ops:
  0.6 0.0 copy-start
  0.6 1.6 %convolution_convert_fusion.1 = bf16[31,2,512]{2,0,1:T(8,128)(2,1)S(1)} fusion(f32[512,512]{1,0:T(8,128)} %param.13, bf16[31,2,512]{2,1,0:T(2,128)(2,1)} %bitcast.74), kind=kOutput, calls=%fused_computation.9 | convolution fusion | flops 32799744 | bytes 1175552 | tf_op jit(solution)/shard_map/dot_general | solution.py:377
  2.2 0.7 copy.49
  2.9 0.1 copy.27
  3.0 1.9 %fusion.5 = bf16[512,512]{1,0:T(8,128)(2,1)} fusion(bf16[31,2,512]{2,1,0:T(2,128)(2,1)} %bitcast.75, bf16[31,2,512]{2,1,0:T(2,128)(2,1)S(1)} %copy.27), kind=kOutput, calls=%fused_computation.7 | convolution fusion | flops 32768000 | bytes 651264 | tf_op jit(solution)/shard_map/dot_general | solution.py:384
  4.9 56.9 %shard_map.120 = (bf16[1,31,64,512]{3,2,1,0:T(8,128)(2,1)}, bf16[32,16,512]{2,1,0:T(8,128)(2,1)}) custom-call(bf16[1,31,2,512]{3,2,1,0:T(2,128)(2,1)} %bitcast.72, bf16[32,16,512]{2,1,0:T(8,128)(2,1)} %bitcast.69), custom_call_target="tpu_custom_call" | custom-call | tf_op jit(solution)/shard_map/pallas_call | solution.py:251
  61.8 0.0 copy-start.8
  61.8 0.0 copy-start.9
  61.8 3.4 %convolution_convert_fusion.crossing_ref = bf16[512,256]{1,0:T(8,128)(2,1)} fusion(bf16[1984,512]{1,0:T(8,128)(2,1)} %bitcast.80, bf16[248,8,2,128]{3,2,1,0:T(2,128)(2,1)} %bitcast.81), kind=kOutput, calls=%fused_computation.8 | convolution fusion | flops 520224768 | bytes 3309568 | tf_op jit(solution)/shard_map/dot_general | solution.py:14
  65.2 0.0 copy-done.8
  65.2 0.6 copy.47
  65.9 12.1 %shard_map.121 = (bf16[8,64,256]{2,1,0:T(8,128)(2,1)}, f32[64,256]{1,0:T(8,128)}) custom-call(bf16[512,256]{1,0:T(8,128)(2,1)} %convolution_convert_fusion.crossing_ref, bf16[64,256]{1,0:T(8,128)(2,1)} %bitcast.73), custom_call_target="tpu_custom_call" | custom-call | tf_op jit(solution)/shard_map/pallas_call | solution.py:332
  77.9 1.0 %reshape.53 = bf16[512,2,128]{2,1,0:T(2,128)(2,1)S(1)} reshape(bf16[8,64,256]{2,1,0:T(8,128)(2,1)} %get-tuple-element.9) | data formatting | bytes 524288 | tf_op jit(solution)/shard_map/reshape | solution.py:350
  79.0 0.0 copy-done.9
  79.0 1.9 %fusion.2 = bf16[31,1,64,2,1,128]{5,2,3,0,4,1:T(8,128)(2,1)S(1)} fusion(bf16[1,31,64,512]{3,2,1,0:T(8,128)(2,1)S(1)} %copy-done.9, bf16[31,1,64,2,1,128]{5,3,4,2,1,0:T(2,128)(2,1)} %param.14, bf16[512,2,128]{2,1,0:T(2,128)(2,1)S(1)} %reshape.53), kind=kOutput, calls=%fused_computation.3 | convolution fusion | flops 521617408 | bytes 4325376 | tf_op jit(solution)/shard_map/dot_general | solution.py:405
  80.9 0.0 copy-start.3
  80.9 0.0 copy-start.5
  80.9 2.0 %copy.20 = bf16[31,1,64,2,1,128]{5,3,4,2,1,0:T(2,128)(2,1)} copy(bf16[31,1,64,2,1,128]{5,2,3,0,4,1:T(8,128)(2,1)S(1)} %fusion.2) | data formatting | bytes 2031616
  82.9 0.7 copy.48
  83.6 0.0 copy-done
  83.6 0.0 copy-done.3
  83.6 0.0 copy-done.5
  83.6 1.1 %fusion.17 = f32[512,512]{1,0:T(8,128)S(1)} fusion(f32[512,512]{1,0:T(8,128)S(1)} %copy-done, f32[512,512]{1,0:T(8,128)S(1)} %copy-done.3, bf16[512,512]{1,0:T(8,128)(2,1)S(1)} %bitcast.71), kind=kOutput, calls=%fused_computation.21 | convolution fusion | flops 806354944 | bytes 3670016 | tf_op jit(solution)/shard_map/dot_general | solution.py:21
  84.7 1.3 %copy.19 = f32[512,512]{0,1:T(8,128)} copy(f32[512,512]{1,0:T(8,128)S(1)} %fusion.17) | data formatting | bytes 2097152 | tf_op jit(solution)/shard_map/dot_general | solution.py:21
  86.0 2.3 %fusion.11 = f32[512,512]{1,0:T(8,128)S(1)} fusion(f32[512,512]{1,0:T(8,128)S(1)} %copy-done.1, f32[512,512]{1,0:T(8,128)S(1)} %fusion.17, f32[512,512]{0,1:T(8,128)} %copy.19), kind=kOutput, calls=%fused_computation.16 | convolution fusion | flops 808976384 | bytes 4194304 | tf_op jit(solution)/shard_map/dot_general | solution.py:30
  88.3 0.0 copy-start.7
  88.4 1.0 %fusion.40 = f32[512,512]{1,0:T(8,128)S(1)} fusion(f32[512,512]{1,0:T(8,128)S(1)} %fusion.11, f32[512,512]{1,0:T(8,128)S(1)} %copy-done.1), kind=kOutput, calls=%fused_computation.50 | convolution fusion | flops 805306368 | bytes 3145728 | tf_op jit(solution)/shard_map/dot_general | solution.py:31
  89.4 0.0 copy-start.2
  89.4 0.0 copy-done.7
  89.5 0.2 fusion.6
  89.7 0.7 reshape.57
  90.4 0.0 copy-done.2
  (7 shorter events, 0.0 us)
Async XLA Ops:
  0.6 83.0 %copy-start = (f32[512,512]{1,0:T(8,128)S(1)}, f32[512,512]{1,0:T(8,128)}, u32[]{:S(2)}) copy-start(f32[512,512]{1,0:T(8,128)} %param.12) | copy-start | bytes 3145732
  61.8 3.5 %copy-start.8 = (bf16[64,2,1,128]{3,1,2,0:T(2,128)(2,1)S(1)}, bf16[64,2,1,128]{3,1,2,0:T(2,128)(2,1)}, u32[]{:S(2)}) copy-start(bf16[64,2,1,128]{3,1,2,0:T(2,128)(2,1)} %param.11) | copy-start | bytes 98308
  61.8 17.2 %copy-start.9 = (bf16[1,31,64,512]{3,2,1,0:T(8,128)(2,1)S(1)}, bf16[1,31,64,512]{3,2,1,0:T(8,128)(2,1)}, u32[]{:S(2)}) copy-start(bf16[1,31,64,512]{3,2,1,0:T(8,128)(2,1)} %get-tuple-element.8) | copy-start | bytes 6094852
  80.9 2.7 %copy-start.3 = (f32[512,512]{1,0:T(8,128)S(1)}, f32[512,512]{1,0:T(8,128)}, u32[]{:S(2)}) copy-start(f32[512,512]{1,0:T(8,128)} %param.17) | copy-start | bytes 3145732
  80.9 2.7 %copy-start.5 = (bf16[32,16,512]{2,1,0:T(8,128)(2,1)S(1)}, bf16[32,16,512]{2,1,0:T(8,128)(2,1)}, u32[]{:S(2)}) copy-start(bf16[32,16,512]{2,1,0:T(8,128)(2,1)} %get-tuple-element.11) | copy-start | bytes 1572868
  83.6 2.4 %copy-start.1 = (f32[512,512]{1,0:T(8,128)S(1)}, f32[512,512]{1,0:T(8,128)}, u32[]{:S(2)}) copy-start(f32[512,512]{1,0:T(8,128)} %param.13) | copy-start | bytes 3145732
  88.3 1.1 %copy-start.7 = (bf16[64,2,1,128]{3,1,2,0:T(2,128)(2,1)S(1)}, bf16[64,2,1,128]{3,1,2,0:T(2,128)(2,1)}, u32[]{:S(2)}) copy-start(bf16[64,2,1,128]{3,1,2,0:T(2,128)(2,1)} %param.16) | copy-start | bytes 98308
  88.4 1.1 %copy-start.4 = (bf16[8,64,256]{2,1,0:T(8,128)(2,1)S(1)}, bf16[8,64,256]{2,1,0:T(8,128)(2,1)}, u32[]{:S(2)}) copy-start(bf16[8,64,256]{2,1,0:T(8,128)(2,1)} %get-tuple-element.9) | copy-start | bytes 786436
  88.4 1.1 %copy-start.6 = (f32[64,256]{1,0:T(8,128)S(1)}, f32[64,256]{1,0:T(8,128)}, u32[]{:S(2)}) copy-start(f32[64,256]{1,0:T(8,128)} %get-tuple-element.10) | copy-start | bytes 196612
  89.4 1.0 %copy-start.2 = (f32[512,512]{1,0:T(8,128)}, f32[512,512]{1,0:T(8,128)S(1)}, u32[]{:S(2)}) copy-start(f32[512,512]{1,0:T(8,128)S(1)} %fusion.40) | copy-start | bytes 3145732

commit v15 on v14

--- a/solution.py
+++ b/solution.py
@@ -84,6 +84,12 @@
             device_id_type=MESH_ID,
         )
 
+    def send_parts(k, carry):
+        by_width(lax.rem(me + k, n), part_rows, part_width, lambda cols: part_copy(k, me, cols).start())
+        return carry
+
+    lax.fori_loop(1, n, send_parts, 0)
+
     own = pltpu.make_async_copy(x_ref, out_ref.at[:, :, pl.ds(me * rows, rows), :], local_sem)
     own.start()
 
@@ -103,11 +109,6 @@
 
     lax.fori_loop(1, line, send_first, 0)
 
-    def send_parts(k, carry):
-        by_width(lax.rem(me + k, n), part_rows, part_width, lambda cols: part_copy(k, me, cols).start())
-        return carry
-
-    lax.fori_loop(1, n, send_parts, 0)
 
     span = line * rows
 
@@ -140,17 +141,6 @@
 
     lax.fori_loop(1, lines, send_own, 0)
 
-    def relay(k, carry):
-        sender_pos = lax.rem(pos + line - k, line)
-        first(k, sender_pos).wait_recv()
-
-        def out(j, inner):
-            forward(j, sender_pos, grp).start()
-            return inner
-
-        return lax.fori_loop(1, lines, out, carry)
-
-    lax.fori_loop(1, line, relay, 0)
 
     precv[me] = p_ref[me]
 
@@ -183,6 +173,18 @@
         return carry
 
     lax.fori_loop(1, n_gr, send_piece, 0)
+
+    def relay(k, carry):
+        sender_pos = lax.rem(pos + line - k, line)
+        first(k, sender_pos).wait_recv()
+
+        def out(j, inner):
+            forward(j, sender_pos, grp).start()
+            return inner
+
+        return lax.fori_loop(1, lines, out, carry)
+
+    lax.fori_loop(1, line, relay, 0)
 
     def wait_piece(k, carry):
         sender = lax.rem(row + n_gr - k, n_gr)

time: 90.7 us -> 88.9 us (0.980)
  the two profiles are of different devices: /device:TPU:7 before, /device:TPU:1 now
where the time goes in v15:
time: 88.9 us; the launch traced here: 88.5 us
  Pallas kernels  67.1 us (75%)
  matrix products  13.4 us (15%)
  local copies, waits for them, and re-layouts  7.17 us (8%)
    pallas_call x1, Pallas kernels, gather_gc(): pl.pallas_call(functools.partial(gather_kernel, n, line, n_gr), out_shape...  52.3 us
    pallas_call x1, Pallas kernels, reduce_gr(): pl.pallas_call(functools.partial(reduce_kernel, n), out_shape=(jax.ShapeD...  14.8 us
    unnamed x25, local copies, waits for them, and re-layouts  4.14 us
    dot_general x1, matrix products, row_product(): lax.dot_general(left_rows, right_rows, (((0,), (0,)), ((), ())), preferre...  3.43 us
    dot_general x1, matrix products, diag_solve(): left_side = jnp.dot(diag_inverse.T, symmetric, precision=highest)  2.33 us
    dot_general x1, matrix products, local(): lax.dot_general(own_grad, panel_factor.reshape(tile_count, own_rows, widt...  1.95 us
    dot_general x1, matrix products, local(): lax.dot_general(grad_rows.reshape(tile_count, tile_rows, width), prior_fa...  1.91 us

profile of v15, /device:TPU:1, one launch (start us, length us, event | category | flops | bytes accessed | tf_op | source)
XLA Modules:
  0.0 88.5 jit_solution(16021197262162808196)
XLA Ops:
  0.6 0.0 copy-start
  0.6 1.6 %convolution_convert_fusion.1 = bf16[31,2,512]{2,0,1:T(8,128)(2,1)S(1)} fusion(f32[512,512]{1,0:T(8,128)} %param.13, bf16[31,2,512]{2,1,0:T(2,128)(2,1)} %bitcast.74), kind=kOutput, calls=%fused_computation.9 | convolution fusion | flops 32799744 | bytes 1175552 | tf_op jit(solution)/shard_map/dot_general | solution.py:379
  2.2 0.7 copy.49
  2.9 0.1 copy.27
  3.0 1.9 %fusion.5 = bf16[512,512]{1,0:T(8,128)(2,1)} fusion(bf16[31,2,512]{2,1,0:T(2,128)(2,1)} %bitcast.75, bf16[31,2,512]{2,1,0:T(2,128)(2,1)S(1)} %copy.27), kind=kOutput, calls=%fused_computation.7 | convolution fusion | flops 32768000 | bytes 651264 | tf_op jit(solution)/shard_map/dot_general | solution.py:386
  4.9 52.3 %shard_map.120 = (bf16[1,31,64,512]{3,2,1,0:T(8,128)(2,1)}, bf16[32,16,512]{2,1,0:T(8,128)(2,1)}) custom-call(bf16[1,31,2,512]{3,2,1,0:T(2,128)(2,1)} %bitcast.72, bf16[32,16,512]{2,1,0:T(8,128)(2,1)} %bitcast.69), custom_call_target="tpu_custom_call" | custom-call | tf_op jit(solution)/shard_map/pallas_call | solution.py:253
  57.2 0.0 copy-start.8
  57.2 0.0 copy-start.9
  57.2 3.4 %convolution_convert_fusion.crossing_ref = bf16[512,256]{1,0:T(8,128)(2,1)} fusion(bf16[1984,512]{1,0:T(8,128)(2,1)} %bitcast.80, bf16[248,8,2,128]{3,2,1,0:T(2,128)(2,1)} %bitcast.81), kind=kOutput, calls=%fused_computation.8 | convolution fusion | flops 520224768 | bytes 3309568 | tf_op jit(solution)/shard_map/dot_general | solution.py:14
  60.6 0.0 copy-done.8
  60.6 0.6 copy.47
  61.3 14.8 %shard_map.121 = (bf16[8,64,256]{2,1,0:T(8,128)(2,1)}, f32[64,256]{1,0:T(8,128)}) custom-call(bf16[512,256]{1,0:T(8,128)(2,1)} %convolution_convert_fusion.crossing_ref, bf16[64,256]{1,0:T(8,128)(2,1)} %bitcast.73), custom_call_target="tpu_custom_call" | custom-call | tf_op jit(solution)/shard_map/pallas_call | solution.py:334
  76.1 1.0 %reshape.53 = bf16[512,2,128]{2,1,0:T(2,128)(2,1)S(1)} reshape(bf16[8,64,256]{2,1,0:T(8,128)(2,1)} %get-tuple-element.9) | data formatting | bytes 524288 | tf_op jit(solution)/shard_map/reshape | solution.py:352
  77.1 0.0 copy-done.9
  77.1 1.9 %fusion.2 = bf16[31,1,64,2,1,128]{5,2,3,0,4,1:T(8,128)(2,1)S(1)} fusion(bf16[1,31,64,512]{3,2,1,0:T(8,128)(2,1)S(1)} %copy-done.9, bf16[31,1,64,2,1,128]{5,3,4,2,1,0:T(2,128)(2,1)} %param.14, bf16[512,2,128]{2,1,0:T(2,128)(2,1)S(1)} %reshape.53), kind=kOutput, calls=%fused_computation.3 | convolution fusion | flops 521617408 | bytes 4325376 | tf_op jit(solution)/shard_map/dot_general | solution.py:407
  79.1 0.0 copy-start.3
  79.1 0.0 copy-start.5
  79.1 2.0 %copy.20 = bf16[31,1,64,2,1,128]{5,3,4,2,1,0:T(2,128)(2,1)} copy(bf16[31,1,64,2,1,128]{5,2,3,0,4,1:T(8,128)(2,1)S(1)} %fusion.2) | data formatting | bytes 2031616
  81.1 0.7 copy.48
  81.8 0.0 copy-done
  81.8 0.0 copy-done.3
  81.8 0.0 copy-done.5
  81.8 1.1 %fusion.17 = f32[512,512]{1,0:T(8,128)S(1)} fusion(f32[512,512]{1,0:T(8,128)S(1)} %copy-done, f32[512,512]{1,0:T(8,128)S(1)} %copy-done.3, bf16[512,512]{1,0:T(8,128)(2,1)S(1)} %bitcast.71), kind=kOutput, calls=%fused_computation.21 | convolution fusion | flops 806354944 | bytes 3670016 | tf_op jit(solution)/shard_map/dot_general | solution.py:21
  82.9 1.3 %copy.19 = f32[512,512]{0,1:T(8,128)} copy(f32[512,512]{1,0:T(8,128)S(1)} %fusion.17) | data formatting | bytes 2097152 | tf_op jit(solution)/shard_map/dot_general | solution.py:21
  84.2 0.0 copy-done.1
  84.2 2.3 %fusion.11 = f32[512,512]{1,0:T(8,128)S(1)} fusion(f32[512,512]{1,0:T(8,128)S(1)} %copy-done.1, f32[512,512]{1,0:T(8,128)S(1)} %fusion.17, f32[512,512]{0,1:T(8,128)} %copy.19), kind=kOutput, calls=%fused_computation.16 | convolution fusion | flops 808976384 | bytes 4194304 | tf_op jit(solution)/shard_map/dot_general | solution.py:30
  86.5 0.0 copy-start.7
  86.5 1.0 %fusion.40 = f32[512,512]{1,0:T(8,128)S(1)} fusion(f32[512,512]{1,0:T(8,128)S(1)} %fusion.11, f32[512,512]{1,0:T(8,128)S(1)} %copy-done.1), kind=kOutput, calls=%fused_computation.50 | convolution fusion | flops 805306368 | bytes 3145728 | tf_op jit(solution)/shard_map/dot_general | solution.py:31
  87.6 0.0 copy-start.2
  87.6 0.2 fusion.6
  87.8 0.7 reshape.57
  88.5 0.0 copy-done.2
  (7 shorter events, 0.0 us)
Async XLA Ops:
  0.6 81.1 %copy-start = (f32[512,512]{1,0:T(8,128)S(1)}, f32[512,512]{1,0:T(8,128)}, u32[]{:S(2)}) copy-start(f32[512,512]{1,0:T(8,128)} %param.12) | copy-start | bytes 3145732
  57.2 3.5 %copy-start.8 = (bf16[64,2,1,128]{3,1,2,0:T(2,128)(2,1)S(1)}, bf16[64,2,1,128]{3,1,2,0:T(2,128)(2,1)}, u32[]{:S(2)}) copy-start(bf16[64,2,1,128]{3,1,2,0:T(2,128)(2,1)} %param.11) | copy-start | bytes 98308
  57.2 19.9 %copy-start.9 = (bf16[1,31,64,512]{3,2,1,0:T(8,128)(2,1)S(1)}, bf16[1,31,64,512]{3,2,1,0:T(8,128)(2,1)}, u32[]{:S(2)}) copy-start(bf16[1,31,64,512]{3,2,1,0:T(8,128)(2,1)} %get-tuple-element.8) | copy-start | bytes 6094852
  79.1 2.7 %copy-start.3 = (f32[512,512]{1,0:T(8,128)S(1)}, f32[512,512]{1,0:T(8,128)}, u32[]{:S(2)}) copy-start(f32[512,512]{1,0:T(8,128)} %param.17) | copy-start | bytes 3145732
  79.1 2.7 %copy-start.5 = (bf16[32,16,512]{2,1,0:T(8,128)(2,1)S(1)}, bf16[32,16,512]{2,1,0:T(8,128)(2,1)}, u32[]{:S(2)}) copy-start(bf16[32,16,512]{2,1,0:T(8,128)(2,1)} %get-tuple-element.11) | copy-start | bytes 1572868
  81.8 2.4 %copy-start.1 = (f32[512,512]{1,0:T(8,128)S(1)}, f32[512,512]{1,0:T(8,128)}, u32[]{:S(2)}) copy-start(f32[512,512]{1,0:T(8,128)} %param.13) | copy-start | bytes 3145732
  86.5 1.1 %copy-start.7 = (bf16[64,2,1,128]{3,1,2,0:T(2,128)(2,1)S(1)}, bf16[64,2,1,128]{3,1,2,0:T(2,128)(2,1)}, u32[]{:S(2)}) copy-start(bf16[64,2,1,128]{3,1,2,0:T(2,128)(2,1)} %param.16) | copy-start | bytes 98308
  86.5 1.1 %copy-start.4 = (bf16[8,64,256]{2,1,0:T(8,128)(2,1)S(1)}, bf16[8,64,256]{2,1,0:T(8,128)(2,1)}, u32[]{:S(2)}) copy-start(bf16[8,64,256]{2,1,0:T(8,128)(2,1)} %get-tuple-element.9) | copy-start | bytes 786436
  86.5 1.1 %copy-start.6 = (f32[64,256]{1,0:T(8,128)S(1)}, f32[64,256]{1,0:T(8,128)}, u32[]{:S(2)}) copy-start(f32[64,256]{1,0:T(8,128)} %get-tuple-element.10) | copy-start | bytes 196612
  87.6 1.0 %copy-start.2 = (f32[512,512]{1,0:T(8,128)}, f32[512,512]{1,0:T(8,128)S(1)}, u32[]{:S(2)}) copy-start(f32[512,512]{1,0:T(8,128)S(1)} %fusion.40) | copy-start | bytes 3145732

commit v16 on v15

--- a/solution.py
+++ b/solution.py
@@ -39,8 +39,8 @@
             action(128 * (j + 1))
 
 
-def gather_kernel(n, line, n_gr, x_ref, p_ref, out_ref, cross_out, precv, recv_piece, cross_slots,
-                  psems, sems, local_sem):
+def gather_kernel(n, line, n_gr, x_ref, p_ref, prior_ref, out_ref, cross_out, prior_out, precv, recv_piece,
+                  cross_slots, prior_slots, psems, sems, local_sem):
     me = lax.axis_index("gc")
     row = lax.axis_index("gr")
     rows = x_ref.shape[2]
@@ -216,6 +216,23 @@
 
     lax.fori_loop(1, n, send_cross, 0)
 
+    def prior_copy(k, sender):
+        return pltpu.make_async_remote_copy(
+            src_ref=prior_ref,
+            dst_ref=prior_slots.at[sender],
+            send_sem=psems.at[6, k],
+            recv_sem=psems.at[7, sender],
+            device_id=(lax.rem(row + k, n_gr), me),
+            device_id_type=MESH_ID,
+        )
+
+    def send_prior(k, carry):
+        prior_copy(k, row).start()
+        return carry
+
+    lax.fori_loop(1, n_gr, send_prior, 0)
+    prior_slots[row] = prior_ref[...]
+
     def wait_first(k, carry):
         first(k, pos).wait_send()
         return carry
@@ -246,8 +263,16 @@
     lax.fori_loop(1, n, wait_cross, 0)
     cross_out[...] = cross_slots[...]
 
-
-def gather_gc(block, part, n, line, n_gr):
+    def wait_prior(k, carry):
+        prior_copy(k, row).wait_send()
+        prior_copy(k, lax.rem(row + n_gr - k, n_gr)).wait_recv()
+        return carry
+
+    lax.fori_loop(1, n_gr, wait_prior, 0)
+    prior_out[...] = prior_slots[...]
+
+
+def gather_gc(block, part, prior_rows, n, line, n_gr):
     count, tiles, rows, width = block.shape
     vmem = pl.BlockSpec(memory_space=pltpu.VMEM)
     return pl.pallas_call(
@@ -255,25 +280,27 @@
         out_shape=(
             jax.ShapeDtypeStruct((count, tiles, rows * n, width), block.dtype),
             jax.ShapeDtypeStruct(part.shape, jnp.bfloat16),
+            jax.ShapeDtypeStruct((n_gr,) + prior_rows.shape, prior_rows.dtype),
         ),
-        in_specs=[pl.BlockSpec(memory_space=pl.ANY), vmem],
-        out_specs=(pl.BlockSpec(memory_space=pl.ANY), vmem),
+        in_specs=[pl.BlockSpec(memory_space=pl.ANY), vmem, vmem],
+        out_specs=(pl.BlockSpec(memory_space=pl.ANY), vmem, vmem),
         scratch_shapes=[
             pltpu.VMEM(part.shape, part.dtype),
             pltpu.VMEM((n_gr,) + part.shape[1:], jnp.float32),
             pltpu.VMEM(part.shape, jnp.bfloat16),
-            pltpu.SemaphoreType.DMA((6, max(n, n_gr))),
+            pltpu.VMEM((n_gr,) + prior_rows.shape, prior_rows.dtype),
+            pltpu.SemaphoreType.DMA((8, max(n, n_gr))),
             pltpu.SemaphoreType.DMA((2 + line, line + n // line)),
             pltpu.SemaphoreType.DMA,
         ],
         compiler_params=pltpu.CompilerParams(collective_id=0, has_side_effects=True),
-    )(block, part)
-
-
-def reduce_kernel(n, crossing_ref, prior_ref, prior_out, crossing_out, recv_crossing, prior_slots, sems):
+    )(block, part, prior_rows)
+
+
+def reduce_kernel(n, crossing_ref, crossing_out, recv_crossing, sems):
     me = lax.axis_index("gr")
     col = lax.axis_index("gc")
-    rows = prior_ref.shape[0]
+    rows = crossing_out.shape[0]
 
     barrier = pltpu.get_barrier_semaphore()
 
@@ -299,24 +326,17 @@
         src = crossing_ref.at[pl.ds(pl.multiple_of(peer * rows, rows), rows), :]
         return gr_copy(k, sender, src, recv_crossing, 0)
 
-    def prior_copy(k, sender):
-        return gr_copy(k, sender, prior_ref, prior_slots, 2)
-
     def send(k, carry):
         crossing_copy(k, me).start()
-        prior_copy(k, me).start()
         return carry
 
     lax.fori_loop(1, n, send, 0)
-    prior_slots[me] = prior_ref[...]
     recv_crossing[me] = crossing_ref[pl.ds(pl.multiple_of(me * rows, rows), rows), :]
 
     def wait(k, carry):
         sender = lax.rem(me + n - k, n)
         crossing_copy(k, me).wait_send()
         crossing_copy(k, sender).wait_recv()
-        prior_copy(k, me).wait_send()
-        prior_copy(k, sender).wait_recv()
         return carry
 
     lax.fori_loop(1, n, wait, 0)
@@ -325,27 +345,23 @@
         return total + recv_crossing[j].astype(jnp.float32)
 
     crossing_out[...] = lax.fori_loop(0, n, add_crossing, jnp.zeros(crossing_out.shape, jnp.float32))
-    prior_out[...] = prior_slots[...]
-
-
-def reduce_gr(crossing_part, prior_rows, n):
-    rows, cols = prior_rows.shape
+
+
+def reduce_gr(crossing_part, n):
+    rows = crossing_part.shape[0] // n
+    cols = crossing_part.shape[1]
     vmem = pl.BlockSpec(memory_space=pltpu.VMEM)
     return pl.pallas_call(
         functools.partial(reduce_kernel, n),
-        out_shape=(
-            jax.ShapeDtypeStruct((n, rows, cols), prior_rows.dtype),
-            jax.ShapeDtypeStruct((rows, cols), jnp.float32),
-        ),
-        in_specs=[vmem, vmem],
-        out_specs=(vmem, vmem),
+        out_shape=jax.ShapeDtypeStruct((rows, cols), jnp.float32),
+        in_specs=[vmem],
+        out_specs=vmem,
         scratch_shapes=[
             pltpu.VMEM((n, rows, cols), crossing_part.dtype),
-            pltpu.VMEM((n, rows, cols), prior_rows.dtype),
-            pltpu.SemaphoreType.DMA((4, n)),
+            pltpu.SemaphoreType.DMA((2, n)),
         ],
         compiler_params=pltpu.CompilerParams(collective_id=1, has_side_effects=True),
-    )(crossing_part, prior_rows)
+    )(crossing_part)
 
 
 def prior_factor_rows(prior_rows, below_shape):
@@ -389,17 +405,18 @@
         (((0, 1), (0, 1)), ((), ())),
         preferred_element_type=jnp.float32,
     ).astype(jnp.bfloat16)
-    whole, cross_rows = gather_gc(
+    prior_here = prior_factor.reshape(prior_local, local_cols)
+    whole, cross_rows, prior_rows = gather_gc(
         own_grad.reshape(1, tile_count, own_rows, width),
         own_part.reshape(n_gc, width // n_gc, width),
+        prior_here,
         n_gc,
         line,
         n_gr,
     )
     grad_rows = whole[0].reshape(local_rows, width)
-    prior_here = prior_factor.reshape(prior_local, local_cols)
     crossing_part = row_product(grad_rows, below_mat).astype(jnp.bfloat16)
-    prior_rows, crossing = reduce_gr(crossing_part, prior_here, n_gr)
+    crossing = reduce_gr(crossing_part, n_gr)
     summed = cross_rows.reshape(width, width).astype(jnp.float32)
     prior_whole = prior_rows.reshape(width, local_cols)
     diag_reduced = jnp.tril(diag_adjoint - summed)

time: 88.9 us -> 87.3 us (0.982)
  Pallas kernels: 67.1 us -> 64.7 us
    pallas_call x1, Pallas kernels: 14.8 us -> 11.7 us  [reduce_gr(): pl.pallas_call(functools.partial(reduce_kernel, n), out_shape=jax.ShapeDt...]
    reshape x1, local copies, waits for them, and re-layouts: 1.02 us -> 0.07 us  [prior_factor_rows(): return prior_rows.reshape(-1, below_shape[3], below_shape[5])]
    unnamed x25 -> x23, local copies, waits for them, and re-layouts: 4.14 us -> 5.03 us
where the time goes in v16:
time: 87.3 us; the launch traced here: 86.9 us
  Pallas kernels  64.7 us (74%)
  matrix products  13.4 us (15%)
  local copies, waits for them, and re-layouts  7.18 us (8%)
    pallas_call x1, Pallas kernels, gather_gc(): pl.pallas_call(functools.partial(gather_kernel, n, line, n_gr), out_shape...  53 us
    pallas_call x1, Pallas kernels, reduce_gr(): pl.pallas_call(functools.partial(reduce_kernel, n), out_shape=jax.ShapeDt...  11.7 us
    unnamed x23, local copies, waits for them, and re-layouts  5.03 us
    dot_general x1, matrix products, row_product(): lax.dot_general(left_rows, right_rows, (((0,), (0,)), ((), ())), preferre...  3.13 us
    dot_general x1, matrix products, diag_solve(): left_side = jnp.dot(diag_inverse.T, symmetric, precision=highest)  2.33 us
    dot_general x1, matrix products, local(): lax.dot_general(grad_rows.reshape(tile_count, tile_rows, width), prior_fa...  2.26 us
    dot_general x1, matrix products, local(): lax.dot_general(own_grad, panel_factor.reshape(tile_count, own_rows, widt...  1.95 us

profile of v16, /device:TPU:1, one launch (start us, length us, event | category | flops | bytes accessed | tf_op | source)
XLA Modules:
  0.0 86.9 jit_solution(13190910175779985760)
XLA Ops:
  0.6 0.0 copy-start
  0.6 0.0 copy-start.7
  0.7 1.5 %copy.47 = bf16[8,8,2,128]{3,1,2,0:T(8,128)(2,1)} copy(bf16[8,8,2,128]{3,2,1,0:T(2,128)(2,1)} %bitcast.78) | data formatting | bytes 65536
  2.2 1.5 %convolution_convert_fusion.1 = bf16[31,2,512]{2,0,1:T(8,128)(2,1)S(1)} fusion(f32[512,512]{1,0:T(8,128)} %param.13, bf16[31,2,512]{2,1,0:T(2,128)(2,1)} %bitcast.74), kind=kOutput, calls=%fused_computation.9 | convolution fusion | flops 32799744 | bytes 1175552 | tf_op jit(solution)/shard_map/dot_general | solution.py:395
  3.7 0.7 copy.49
  4.4 0.7 copy.48
  5.0 0.1 copy.27
  5.1 0.8 convert.7
  5.9 2.0 %fusion.5 = bf16[512,512]{1,0:T(8,128)(2,1)} fusion(bf16[31,2,512]{2,1,0:T(2,128)(2,1)} %bitcast.75, bf16[31,2,512]{2,1,0:T(2,128)(2,1)S(1)} %copy.27), kind=kOutput, calls=%fused_computation.7 | convolution fusion | flops 32768000 | bytes 651264 | tf_op jit(solution)/shard_map/dot_general | solution.py:402
  7.9 53.0 %shard_map.120 = (bf16[1,31,64,512]{3,2,1,0:T(8,128)(2,1)}, bf16[32,16,512]{2,1,0:T(8,128)(2,1)}, bf16[8,64,256]{2,1,0:T(8,128)(2,1)}) custom-call(bf16[1,31,2,512]{3,2,1,0:T(2,128)(2,1)} %bitcast.72, bf16[32,16,512]{2,1,0:T(8,128)(2,1)} %bitcast.69, bf16[64,256]{1,0:T(8,128)(2,1)} %bitcast.73), custom_call_target="tpu_custom_call" | custom-call | tf_op jit(solution)/shard_map/pallas_call | solution.py:278
  60.9 0.0 copy-done.7
  60.9 0.0 copy-start.4
  60.9 0.0 copy-start.8
  60.9 3.1 %convolution_convert_fusion.crossing_ref = bf16[512,256]{1,0:T(8,128)(2,1)} fusion(bf16[1984,512]{1,0:T(8,128)(2,1)} %bitcast.80, bf16[248,8,2,128]{3,2,1,0:T(2,128)(2,1)S(1)} %bitcast.81), kind=kOutput, calls=%fused_computation.8 | convolution fusion | flops 520224768 | bytes 3309568 | tf_op jit(solution)/shard_map/dot_general | solution.py:14
  64.0 11.7 %shard_map.121 = f32[64,256]{1,0:T(8,128)} custom-call(bf16[512,256]{1,0:T(8,128)(2,1)} %convolution_convert_fusion.crossing_ref), custom_call_target="tpu_custom_call" | custom-call | tf_op jit(solution)/shard_map/pallas_call | solution.py:354
  75.7 0.0 copy-done.4
  75.8 0.1 reshape.52
  75.8 0.0 copy-done.8
  75.8 2.3 %fusion.2 = bf16[31,1,64,2,1,128]{5,2,3,0,4,1:T(8,128)(2,1)S(1)} fusion(bf16[1,31,64,512]{3,2,1,0:T(8,128)(2,1)} %get-tuple-element.7, bf16[31,1,64,2,1,128]{5,3,4,2,1,0:T(2,128)(2,1)S(1)} %copy-done.8, bf16[512,2,128]{2,1,0:T(2,128)(2,1)S(1)} %reshape.52), kind=kOutput, calls=%fused_computation.3 | convolution fusion | flops 521617408 | bytes 4325376 | tf_op jit(solution)/shard_map/dot_general | solution.py:424
  78.1 0.0 copy-start.3
  78.1 2.0 %copy.20 = bf16[31,1,64,2,1,128]{5,3,4,2,1,0:T(2,128)(2,1)} copy(bf16[31,1,64,2,1,128]{5,2,3,0,4,1:T(8,128)(2,1)S(1)} %fusion.2) | data formatting | bytes 2031616
  80.1 0.0 copy-done
  80.1 1.1 %fusion.17 = f32[512,512]{1,0:T(8,128)S(1)} fusion(f32[512,512]{1,0:T(8,128)S(1)} %copy-done, f32[512,512]{1,0:T(8,128)S(1)} %copy-done.3, bf16[512,512]{1,0:T(8,128)(2,1)S(1)} %bitcast.71), kind=kOutput, calls=%fused_computation.21 | convolution fusion | flops 806354944 | bytes 3670016 | tf_op jit(solution)/shard_map/dot_general | solution.py:21
  81.2 1.3 %copy.19 = f32[512,512]{0,1:T(8,128)} copy(f32[512,512]{1,0:T(8,128)S(1)} %fusion.17) | data formatting | bytes 2097152 | tf_op jit(solution)/shard_map/dot_general | solution.py:21
  82.5 2.3 %fusion.11 = f32[512,512]{1,0:T(8,128)S(1)} fusion(f32[512,512]{1,0:T(8,128)S(1)} %copy-done.1, f32[512,512]{1,0:T(8,128)S(1)} %fusion.17, f32[512,512]{0,1:T(8,128)} %copy.19), kind=kOutput, calls=%fused_computation.16 | convolution fusion | flops 808976384 | bytes 4194304 | tf_op jit(solution)/shard_map/dot_general | solution.py:30
  84.9 0.0 copy-start.6
  84.9 1.0 %fusion.40 = f32[512,512]{1,0:T(8,128)S(1)} fusion(f32[512,512]{1,0:T(8,128)S(1)} %fusion.11, f32[512,512]{1,0:T(8,128)S(1)} %copy-done.1), kind=kOutput, calls=%fused_computation.50 | convolution fusion | flops 805306368 | bytes 3145728 | tf_op jit(solution)/shard_map/dot_general | solution.py:31
  85.9 0.0 copy-done.6
  85.9 0.0 copy-start.2
  85.9 0.2 fusion.6
  86.1 0.8 reshape.57
  86.9 0.0 copy-done.2
  (5 shorter events, 0.0 us)
Async XLA Ops:
  0.6 79.5 %copy-start = (f32[512,512]{1,0:T(8,128)S(1)}, f32[512,512]{1,0:T(8,128)}, u32[]{:S(2)}) copy-start(f32[512,512]{1,0:T(8,128)} %param.12) | copy-start | bytes 3145732
  0.6 60.2 %copy-start.7 = (bf16[31,1,64,2,1,128]{5,3,4,2,1,0:T(2,128)(2,1)S(1)}, bf16[31,1,64,2,1,128]{5,3,4,2,1,0:T(2,128)(2,1)}, u32[]{:S(2)}) copy-start(bf16[31,1,64,2,1,128]{5,3,4,2,1,0:T(2,128)(2,1)} %param.9) | copy-start | bytes 3047428
  60.9 14.9 %copy-start.4 = (bf16[8,64,256]{2,1,0:T(8,128)(2,1)S(1)}, bf16[8,64,256]{2,1,0:T(8,128)(2,1)}, u32[]{:S(2)}) copy-start(bf16[8,64,256]{2,1,0:T(8,128)(2,1)} %get-tuple-element.8) | copy-start | bytes 786436
  60.9 15.0 %copy-start.8 = (bf16[31,1,64,2,1,128]{5,3,4,2,1,0:T(2,128)(2,1)S(1)}, bf16[31,1,64,2,1,128]{5,3,4,2,1,0:T(2,128)(2,1)}, u32[]{:S(2)}) copy-start(bf16[31,1,64,2,1,128]{5,3,4,2,1,0:T(2,128)(2,1)} %param.14) | copy-start | bytes 3047428
  78.1 2.0 %copy-start.3 = (f32[512,512]{1,0:T(8,128)S(1)}, f32[512,512]{1,0:T(8,128)}, u32[]{:S(2)}) copy-start(f32[512,512]{1,0:T(8,128)} %param.17) | copy-start | bytes 3145732
  78.1 2.0 %copy-start.5 = (bf16[32,16,512]{2,1,0:T(8,128)(2,1)S(1)}, bf16[32,16,512]{2,1,0:T(8,128)(2,1)}, u32[]{:S(2)}) copy-start(bf16[32,16,512]{2,1,0:T(8,128)(2,1)} %get-tuple-element.9) | copy-start | bytes 1572868
  80.1 2.4 %copy-start.1 = (f32[512,512]{1,0:T(8,128)S(1)}, f32[512,512]{1,0:T(8,128)}, u32[]{:S(2)}) copy-start(f32[512,512]{1,0:T(8,128)} %param.13) | copy-start | bytes 3145732
  84.9 1.0 %copy-start.6 = (f32[64,256]{1,0:T(8,128)S(1)}, f32[64,256]{1,0:T(8,128)}, u32[]{:S(2)}) copy-start(f32[64,256]{1,0:T(8,128)} %shard_map.121) | copy-start | bytes 196612
  85.9 1.0 %copy-start.2 = (f32[512,512]{1,0:T(8,128)}, f32[512,512]{1,0:T(8,128)S(1)}, u32[]{:S(2)}) copy-start(f32[512,512]{1,0:T(8,128)S(1)} %fusion.40) | copy-start | bytes 3145732

commit v17 on v16

--- a/solution.py
+++ b/solution.py
@@ -415,7 +415,12 @@
         n_gr,
     )
     grad_rows = whole[0].reshape(local_rows, width)
-    crossing_part = row_product(grad_rows, below_mat).astype(jnp.bfloat16)
+    crossing_part = lax.dot_general(
+        grad_rows.reshape(tile_count, tile_rows, width),
+        below_factor.reshape(tile_count, tile_rows, local_cols),
+        (((0, 1), (0, 1)), ((), ())),
+        preferred_element_type=jnp.float32,
+    ).astype(jnp.bfloat16)
     crossing = reduce_gr(crossing_part, n_gr)
     summed = cross_rows.reshape(width, width).astype(jnp.float32)
     prior_whole = prior_rows.reshape(width, local_cols)

time: 87.3 us -> 88 us (level)
  no operation moved by 1% of the time
where the time goes in v17:
time: 88 us; the launch traced here: 87.7 us
  Pallas kernels  64.9 us (74%)
  matrix products  13.4 us (15%)
  local copies, waits for them, and re-layouts  7.83 us (9%)
    pallas_call x1, Pallas kernels, gather_gc(): pl.pallas_call(functools.partial(gather_kernel, n, line, n_gr), out_shape...  53.1 us
    pallas_call x1, Pallas kernels, reduce_gr(): pl.pallas_call(functools.partial(reduce_kernel, n), out_shape=jax.ShapeDt...  11.7 us
    unnamed x23, local copies, waits for them, and re-layouts  5.03 us
    dot_general x1, matrix products, local(): lax.dot_general(grad_rows.reshape(tile_count, tile_rows, width), below_fa...  3.13 us
    dot_general x1, matrix products, diag_solve(): left_side = jnp.dot(diag_inverse.T, symmetric, precision=highest)  2.33 us
    dot_general x1, matrix products, local(): lax.dot_general(grad_rows.reshape(tile_count, tile_rows, width), prior_fa...  2.26 us
    dot_general x1, matrix products, local(): lax.dot_general(own_grad, panel_factor.reshape(tile_count, own_rows, widt...  1.95 us

profile of v17, /device:TPU:1, one launch (start us, length us, event | category | flops | bytes accessed | tf_op | source)
XLA Modules:
  0.0 87.7 jit_solution(14673628717904516819)
XLA Ops:
  0.6 0.0 copy-start
  0.6 0.0 copy-start.5
  0.7 1.5 %copy.42 = bf16[8,8,2,128]{3,1,2,0:T(8,128)(2,1)} copy(bf16[8,8,2,128]{3,2,1,0:T(2,128)(2,1)} %bitcast.83) | data formatting | bytes 65536
  2.2 1.5 %convolution_convert_fusion = bf16[31,2,512]{2,0,1:T(8,128)(2,1)S(1)} fusion(f32[512,512]{1,0:T(8,128)} %param.13, bf16[31,2,512]{2,1,0:T(2,128)(2,1)} %bitcast.79), kind=kOutput, calls=%fused_computation.12 | convolution fusion | flops 32799744 | bytes 1175552 | tf_op jit(solution)/shard_map/dot_general | solution.py:395
  3.7 0.7 copy.44
  4.4 0.7 copy.43
  5.0 0.1 copy.26
  5.1 0.8 convert.7
  5.9 2.0 %fusion.7 = bf16[512,512]{1,0:T(8,128)(2,1)} fusion(bf16[31,2,512]{2,1,0:T(2,128)(2,1)} %bitcast.80, bf16[31,2,512]{2,1,0:T(2,128)(2,1)S(1)} %copy.26), kind=kOutput, calls=%fused_computation.9 | convolution fusion | flops 32768000 | bytes 651264 | tf_op jit(solution)/shard_map/dot_general | solution.py:402
  7.9 0.0 copy-done.5
  7.9 0.6 reshape.55
  8.5 53.1 %shard_map.120 = (bf16[1,31,64,512]{3,2,1,0:T(8,128)(2,1)}, bf16[32,16,512]{2,1,0:T(8,128)(2,1)}, bf16[8,64,256]{2,1,0:T(8,128)(2,1)}) custom-call(bf16[1,31,2,512]{3,2,1,0:T(2,128)(2,1)} %bitcast.77, bf16[32,16,512]{2,1,0:T(8,128)(2,1)} %bitcast.74, bf16[64,256]{1,0:T(8,128)(2,1)} %bitcast.78), custom_call_target="tpu_custom_call" | custom-call | tf_op jit(solution)/shard_map/pallas_call | solution.py:278
  61.6 0.0 copy-start.4
  61.7 0.0 copy-start.8
  61.7 3.1 %fusion.11.crossing_ref = bf16[512,256]{1,0:T(8,128)(2,1)} fusion(bf16[31,64,256]{2,1,0:T(8,128)(2,1)S(1)} %reshape.55, bf16[1,31,64,512]{3,2,1,0:T(8,128)(2,1)} %get-tuple-element.7), kind=kOutput, calls=%fused_computation.11 | convolution fusion | flops 520224768 | bytes 3309568 | tf_op jit(solution)/shard_map/dot_general | solution.py:418
  64.8 11.7 %shard_map.121 = f32[64,256]{1,0:T(8,128)} custom-call(bf16[512,256]{1,0:T(8,128)(2,1)} %fusion.11.crossing_ref), custom_call_target="tpu_custom_call" | custom-call | tf_op jit(solution)/shard_map/pallas_call | solution.py:354
  76.5 0.0 copy-done.4
  76.5 0.1 reshape.52
  76.6 0.0 copy-done.8
  76.6 2.3 %fusion.2 = bf16[31,1,64,2,1,128]{5,2,3,0,4,1:T(8,128)(2,1)S(1)} fusion(bf16[1,31,64,512]{3,2,1,0:T(8,128)(2,1)} %get-tuple-element.7, bf16[31,1,64,2,1,128]{5,3,4,2,1,0:T(2,128)(2,1)S(1)} %copy-done.8, bf16[512,2,128]{2,1,0:T(2,128)(2,1)S(1)} %reshape.52), kind=kOutput, calls=%fused_computation.3 | convolution fusion | flops 521617408 | bytes 4325376 | tf_op jit(solution)/shard_map/dot_general | solution.py:429
  78.9 0.0 copy-start.3
  78.9 2.0 %copy.20 = bf16[31,1,64,2,1,128]{5,3,4,2,1,0:T(2,128)(2,1)} copy(bf16[31,1,64,2,1,128]{5,2,3,0,4,1:T(8,128)(2,1)S(1)} %fusion.2) | data formatting | bytes 2031616
  80.9 1.1 %fusion.25 = f32[512,512]{1,0:T(8,128)S(1)} fusion(f32[512,512]{1,0:T(8,128)S(1)} %copy-done, f32[512,512]{1,0:T(8,128)S(1)} %copy-done.3, bf16[512,512]{1,0:T(8,128)(2,1)S(1)} %bitcast.76), kind=kOutput, calls=%fused_computation.24 | convolution fusion | flops 806354944 | bytes 3670016 | tf_op jit(solution)/shard_map/dot_general | solution.py:21
  82.0 1.3 %copy.19 = f32[512,512]{0,1:T(8,128)} copy(f32[512,512]{1,0:T(8,128)S(1)} %fusion.25) | data formatting | bytes 2097152 | tf_op jit(solution)/shard_map/dot_general | solution.py:21
  83.3 2.3 %fusion.19 = f32[512,512]{1,0:T(8,128)S(1)} fusion(f32[512,512]{1,0:T(8,128)S(1)} %copy-done.1, f32[512,512]{1,0:T(8,128)S(1)} %fusion.25, f32[512,512]{0,1:T(8,128)} %copy.19), kind=kOutput, calls=%fused_computation.19 | convolution fusion | flops 808976384 | bytes 4194304 | tf_op jit(solution)/shard_map/dot_general | solution.py:30
  85.6 0.0 copy-start.7
  85.7 1.0 %fusion.46 = f32[512,512]{1,0:T(8,128)S(1)} fusion(f32[512,512]{1,0:T(8,128)S(1)} %fusion.19, f32[512,512]{1,0:T(8,128)S(1)} %copy-done.1), kind=kOutput, calls=%fused_computation.51 | convolution fusion | flops 805306368 | bytes 3145728 | tf_op jit(solution)/shard_map/dot_general | solution.py:31
  86.7 0.0 copy-done.7
  86.7 0.0 copy-start.2
  86.7 0.2 fusion.14
  86.9 0.8 reshape.57
  87.7 0.0 copy-done.2
  (6 shorter events, 0.0 us)
Async XLA Ops:
  0.6 80.3 %copy-start = (f32[512,512]{1,0:T(8,128)S(1)}, f32[512,512]{1,0:T(8,128)}, u32[]{:S(2)}) copy-start(f32[512,512]{1,0:T(8,128)} %param.12) | copy-start | bytes 3145732
  0.6 7.2 %copy-start.5 = (bf16[31,1,64,2,1,128]{5,3,4,2,1,0:T(2,128)(2,1)S(1)}, bf16[31,1,64,2,1,128]{5,3,4,2,1,0:T(2,128)(2,1)}, u32[]{:S(2)}) copy-start(bf16[31,1,64,2,1,128]{5,3,4,2,1,0:T(2,128)(2,1)} %param.9) | copy-start | bytes 3047428
  61.6 14.9 %copy-start.4 = (bf16[8,64,256]{2,1,0:T(8,128)(2,1)S(1)}, bf16[8,64,256]{2,1,0:T(8,128)(2,1)}, u32[]{:S(2)}) copy-start(bf16[8,64,256]{2,1,0:T(8,128)(2,1)} %get-tuple-element.8) | copy-start | bytes 786436
  61.7 15.0 %copy-start.8 = (bf16[31,1,64,2,1,128]{5,3,4,2,1,0:T(2,128)(2,1)S(1)}, bf16[31,1,64,2,1,128]{5,3,4,2,1,0:T(2,128)(2,1)}, u32[]{:S(2)}) copy-start(bf16[31,1,64,2,1,128]{5,3,4,2,1,0:T(2,128)(2,1)} %param.14) | copy-start | bytes 3047428
  78.9 2.0 %copy-start.3 = (f32[512,512]{1,0:T(8,128)S(1)}, f32[512,512]{1,0:T(8,128)}, u32[]{:S(2)}) copy-start(f32[512,512]{1,0:T(8,128)} %param.17) | copy-start | bytes 3145732
  78.9 2.0 %copy-start.6 = (bf16[32,16,512]{2,1,0:T(8,128)(2,1)S(1)}, bf16[32,16,512]{2,1,0:T(8,128)(2,1)}, u32[]{:S(2)}) copy-start(bf16[32,16,512]{2,1,0:T(8,128)(2,1)} %get-tuple-element.9) | copy-start | bytes 1572868
  80.9 2.4 %copy-start.1 = (f32[512,512]{1,0:T(8,128)S(1)}, f32[512,512]{1,0:T(8,128)}, u32[]{:S(2)}) copy-start(f32[512,512]{1,0:T(8,128)} %param.13) | copy-start | bytes 3145732
  85.6 1.0 %copy-start.7 = (f32[64,256]{1,0:T(8,128)S(1)}, f32[64,256]{1,0:T(8,128)}, u32[]{:S(2)}) copy-start(f32[64,256]{1,0:T(8,128)} %shard_map.121) | copy-start | bytes 196612
  86.7 1.0 %copy-start.2 = (f32[512,512]{1,0:T(8,128)}, f32[512,512]{1,0:T(8,128)S(1)}, u32[]{:S(2)}) copy-start(f32[512,512]{1,0:T(8,128)S(1)} %fusion.46) | copy-start | bytes 3145732

commit v18 on v16

--- a/solution.py
+++ b/solution.py
@@ -156,7 +156,7 @@
         return total + precv[j].astype(jnp.float32)
 
     piece = lax.fori_loop(0, n, add_part, jnp.zeros(recv_piece.shape[1:], jnp.float32))
-    recv_piece[row] = piece
+    recv_piece[row] = piece.astype(recv_piece.dtype)
 
     def piece_copy(k, sender, cols):
         return pltpu.make_async_remote_copy(
@@ -195,7 +195,7 @@
     lax.fori_loop(1, n_gr, wait_piece, 0)
 
     def add_piece(j, total):
-        return total + recv_piece[j]
+        return total + recv_piece[j].astype(jnp.float32)
 
     summed = lax.fori_loop(0, n_gr, add_piece, jnp.zeros(recv_piece.shape[1:], jnp.float32))
     cross_slots[me] = summed.astype(cross_slots.dtype)
@@ -286,7 +286,7 @@
         out_specs=(pl.BlockSpec(memory_space=pl.ANY), vmem, vmem),
         scratch_shapes=[
             pltpu.VMEM(part.shape, part.dtype),
-            pltpu.VMEM((n_gr,) + part.shape[1:], jnp.float32),
+            pltpu.VMEM((n_gr,) + part.shape[1:], jnp.bfloat16),
             pltpu.VMEM(part.shape, jnp.bfloat16),
             pltpu.VMEM((n_gr,) + prior_rows.shape, prior_rows.dtype),
             pltpu.SemaphoreType.DMA((8, max(n, n_gr))),

time: 87.3 us -> 87.3 us (level)
  no operation moved by 1% of the time
where the time goes in v18:
time: 87.3 us; the launch traced here: 86.9 us
  Pallas kernels  64.7 us (74%)
  matrix products  13.4 us (15%)
  local copies, waits for them, and re-layouts  7.18 us (8%)
    pallas_call x1, Pallas kernels, gather_gc(): pl.pallas_call(functools.partial(gather_kernel, n, line, n_gr), out_shape...  53 us
    pallas_call x1, Pallas kernels, reduce_gr(): pl.pallas_call(functools.partial(reduce_kernel, n), out_shape=jax.ShapeDt...  11.7 us
    unnamed x23, local copies, waits for them, and re-layouts  5.03 us
    dot_general x1, matrix products, row_product(): lax.dot_general(left_rows, right_rows, (((0,), (0,)), ((), ())), preferre...  3.13 us
    dot_general x1, matrix products, diag_solve(): left_side = jnp.dot(diag_inverse.T, symmetric, precision=highest)  2.33 us
    dot_general x1, matrix products, local(): lax.dot_general(grad_rows.reshape(tile_count, tile_rows, width), prior_fa...  2.26 us
    dot_general x1, matrix products, local(): lax.dot_general(own_grad, panel_factor.reshape(tile_count, own_rows, widt...  1.95 us

profile of v18, /device:TPU:1, one launch (start us, length us, event | category | flops | bytes accessed | tf_op | source)
XLA Modules:
  0.0 86.9 jit_solution(9551140671425815017)
XLA Ops:
  0.6 0.0 copy-start
  0.6 0.0 copy-start.7
  0.7 1.5 %copy.47 = bf16[8,8,2,128]{3,1,2,0:T(8,128)(2,1)} copy(bf16[8,8,2,128]{3,2,1,0:T(2,128)(2,1)} %bitcast.78) | data formatting | bytes 65536
  2.2 1.5 %convolution_convert_fusion.1 = bf16[31,2,512]{2,0,1:T(8,128)(2,1)S(1)} fusion(f32[512,512]{1,0:T(8,128)} %param.13, bf16[31,2,512]{2,1,0:T(2,128)(2,1)} %bitcast.74), kind=kOutput, calls=%fused_computation.9 | convolution fusion | flops 32799744 | bytes 1175552 | tf_op jit(solution)/shard_map/dot_general | solution.py:395
  3.7 0.7 copy.49
  4.4 0.7 copy.48
  5.0 0.1 copy.27
  5.1 0.8 convert.7
  5.9 2.0 %fusion.5 = bf16[512,512]{1,0:T(8,128)(2,1)} fusion(bf16[31,2,512]{2,1,0:T(2,128)(2,1)} %bitcast.75, bf16[31,2,512]{2,1,0:T(2,128)(2,1)S(1)} %copy.27), kind=kOutput, calls=%fused_computation.7 | convolution fusion | flops 32768000 | bytes 651264 | tf_op jit(solution)/shard_map/dot_general | solution.py:402
  7.9 53.0 %shard_map.120 = (bf16[1,31,64,512]{3,2,1,0:T(8,128)(2,1)}, bf16[32,16,512]{2,1,0:T(8,128)(2,1)}, bf16[8,64,256]{2,1,0:T(8,128)(2,1)}) custom-call(bf16[1,31,2,512]{3,2,1,0:T(2,128)(2,1)} %bitcast.72, bf16[32,16,512]{2,1,0:T(8,128)(2,1)} %bitcast.69, bf16[64,256]{1,0:T(8,128)(2,1)} %bitcast.73), custom_call_target="tpu_custom_call" | custom-call | tf_op jit(solution)/shard_map/pallas_call | solution.py:278
  60.8 0.0 copy-done.7
  60.9 0.0 copy-start.4
  60.9 0.0 copy-start.8
  60.9 3.1 %convolution_convert_fusion.crossing_ref = bf16[512,256]{1,0:T(8,128)(2,1)} fusion(bf16[1984,512]{1,0:T(8,128)(2,1)} %bitcast.80, bf16[248,8,2,128]{3,2,1,0:T(2,128)(2,1)S(1)} %bitcast.81), kind=kOutput, calls=%fused_computation.8 | convolution fusion | flops 520224768 | bytes 3309568 | tf_op jit(solution)/shard_map/dot_general | solution.py:14
  64.0 11.7 %shard_map.121 = f32[64,256]{1,0:T(8,128)} custom-call(bf16[512,256]{1,0:T(8,128)(2,1)} %convolution_convert_fusion.crossing_ref), custom_call_target="tpu_custom_call" | custom-call | tf_op jit(solution)/shard_map/pallas_call | solution.py:354
  75.7 0.0 copy-done.4
  75.7 0.1 reshape.52
  75.8 0.0 copy-done.8
  75.8 2.3 %fusion.2 = bf16[31,1,64,2,1,128]{5,2,3,0,4,1:T(8,128)(2,1)S(1)} fusion(bf16[1,31,64,512]{3,2,1,0:T(8,128)(2,1)} %get-tuple-element.7, bf16[31,1,64,2,1,128]{5,3,4,2,1,0:T(2,128)(2,1)S(1)} %copy-done.8, bf16[512,2,128]{2,1,0:T(2,128)(2,1)S(1)} %reshape.52), kind=kOutput, calls=%fused_computation.3 | convolution fusion | flops 521617408 | bytes 4325376 | tf_op jit(solution)/shard_map/dot_general | solution.py:424
  78.1 0.0 copy-start.3
  78.1 2.0 %copy.20 = bf16[31,1,64,2,1,128]{5,3,4,2,1,0:T(2,128)(2,1)} copy(bf16[31,1,64,2,1,128]{5,2,3,0,4,1:T(8,128)(2,1)S(1)} %fusion.2) | data formatting | bytes 2031616
  80.1 0.0 copy-done
  80.1 1.1 %fusion.17 = f32[512,512]{1,0:T(8,128)S(1)} fusion(f32[512,512]{1,0:T(8,128)S(1)} %copy-done, f32[512,512]{1,0:T(8,128)S(1)} %copy-done.3, bf16[512,512]{1,0:T(8,128)(2,1)S(1)} %bitcast.71), kind=kOutput, calls=%fused_computation.21 | convolution fusion | flops 806354944 | bytes 3670016 | tf_op jit(solution)/shard_map/dot_general | solution.py:21
  81.2 1.3 %copy.19 = f32[512,512]{0,1:T(8,128)} copy(f32[512,512]{1,0:T(8,128)S(1)} %fusion.17) | data formatting | bytes 2097152 | tf_op jit(solution)/shard_map/dot_general | solution.py:21
  82.5 2.3 %fusion.11 = f32[512,512]{1,0:T(8,128)S(1)} fusion(f32[512,512]{1,0:T(8,128)S(1)} %copy-done.1, f32[512,512]{1,0:T(8,128)S(1)} %fusion.17, f32[512,512]{0,1:T(8,128)} %copy.19), kind=kOutput, calls=%fused_computation.16 | convolution fusion | flops 808976384 | bytes 4194304 | tf_op jit(solution)/shard_map/dot_general | solution.py:30
  84.9 0.0 copy-start.6
  84.9 1.0 %fusion.40 = f32[512,512]{1,0:T(8,128)S(1)} fusion(f32[512,512]{1,0:T(8,128)S(1)} %fusion.11, f32[512,512]{1,0:T(8,128)S(1)} %copy-done.1), kind=kOutput, calls=%fused_computation.50 | convolution fusion | flops 805306368 | bytes 3145728 | tf_op jit(solution)/shard_map/dot_general | solution.py:31
  85.9 0.0 copy-done.6
  85.9 0.0 copy-start.2
  85.9 0.2 fusion.6
  86.1 0.8 reshape.57
  86.9 0.0 copy-done.2
  (5 shorter events, 0.0 us)
Async XLA Ops:
  0.6 79.5 %copy-start = (f32[512,512]{1,0:T(8,128)S(1)}, f32[512,512]{1,0:T(8,128)}, u32[]{:S(2)}) copy-start(f32[512,512]{1,0:T(8,128)} %param.12) | copy-start | bytes 3145732
  0.6 60.2 %copy-start.7 = (bf16[31,1,64,2,1,128]{5,3,4,2,1,0:T(2,128)(2,1)S(1)}, bf16[31,1,64,2,1,128]{5,3,4,2,1,0:T(2,128)(2,1)}, u32[]{:S(2)}) copy-start(bf16[31,1,64,2,1,128]{5,3,4,2,1,0:T(2,128)(2,1)} %param.9) | copy-start | bytes 3047428
  60.9 14.9 %copy-start.4 = (bf16[8,64,256]{2,1,0:T(8,128)(2,1)S(1)}, bf16[8,64,256]{2,1,0:T(8,128)(2,1)}, u32[]{:S(2)}) copy-start(bf16[8,64,256]{2,1,0:T(8,128)(2,1)} %get-tuple-element.8) | copy-start | bytes 786436
  60.9 15.0 %copy-start.8 = (bf16[31,1,64,2,1,128]{5,3,4,2,1,0:T(2,128)(2,1)S(1)}, bf16[31,1,64,2,1,128]{5,3,4,2,1,0:T(2,128)(2,1)}, u32[]{:S(2)}) copy-start(bf16[31,1,64,2,1,128]{5,3,4,2,1,0:T(2,128)(2,1)} %param.14) | copy-start | bytes 3047428
  78.1 2.0 %copy-start.3 = (f32[512,512]{1,0:T(8,128)S(1)}, f32[512,512]{1,0:T(8,128)}, u32[]{:S(2)}) copy-start(f32[512,512]{1,0:T(8,128)} %param.17) | copy-start | bytes 3145732
  78.1 2.0 %copy-start.5 = (bf16[32,16,512]{2,1,0:T(8,128)(2,1)S(1)}, bf16[32,16,512]{2,1,0:T(8,128)(2,1)}, u32[]{:S(2)}) copy-start(bf16[32,16,512]{2,1,0:T(8,128)(2,1)} %get-tuple-element.9) | copy-start | bytes 1572868
  80.1 2.4 %copy-start.1 = (f32[512,512]{1,0:T(8,128)S(1)}, f32[512,512]{1,0:T(8,128)}, u32[]{:S(2)}) copy-start(f32[512,512]{1,0:T(8,128)} %param.13) | copy-start | bytes 3145732
  84.9 1.0 %copy-start.6 = (f32[64,256]{1,0:T(8,128)S(1)}, f32[64,256]{1,0:T(8,128)}, u32[]{:S(2)}) copy-start(f32[64,256]{1,0:T(8,128)} %shard_map.121) | copy-start | bytes 196612
  85.9 1.0 %copy-start.2 = (f32[512,512]{1,0:T(8,128)}, f32[512,512]{1,0:T(8,128)S(1)}, u32[]{:S(2)}) copy-start(f32[512,512]{1,0:T(8,128)S(1)} %fusion.40) | copy-start | bytes 3145732

commit v19 on v16

--- a/solution.py
+++ b/solution.py
@@ -273,12 +273,12 @@
 
 
 def gather_gc(block, part, prior_rows, n, line, n_gr):
-    count, tiles, rows, width = block.shape
+    tiles, count, rows, width = block.shape
     vmem = pl.BlockSpec(memory_space=pltpu.VMEM)
     return pl.pallas_call(
         functools.partial(gather_kernel, n, line, n_gr),
         out_shape=(
-            jax.ShapeDtypeStruct((count, tiles, rows * n, width), block.dtype),
+            jax.ShapeDtypeStruct((tiles, count, rows * n, width), block.dtype),
             jax.ShapeDtypeStruct(part.shape, jnp.bfloat16),
             jax.ShapeDtypeStruct((n_gr,) + prior_rows.shape, prior_rows.dtype),
         ),
@@ -407,14 +407,14 @@
     ).astype(jnp.bfloat16)
     prior_here = prior_factor.reshape(prior_local, local_cols)
     whole, cross_rows, prior_rows = gather_gc(
-        own_grad.reshape(1, tile_count, own_rows, width),
+        panel_grad,
         own_part.reshape(n_gc, width // n_gc, width),
         prior_here,
         n_gc,
         line,
         n_gr,
     )
-    grad_rows = whole[0].reshape(local_rows, width)
+    grad_rows = whole.reshape(local_rows, width)
     crossing_part = row_product(grad_rows, below_mat).astype(jnp.bfloat16)
     crossing = reduce_gr(crossing_part, n_gr)
     summed = cross_rows.reshape(width, width).astype(jnp.float32)

time: 87.3 us -> 86.6 us (level)
    unnamed x23 -> x22, local copies, waits for them, and re-layouts: 5.03 us -> 4.34 us
where the time goes in v19:
time: 86.6 us; the launch traced here: 86.2 us
  Pallas kernels  64.7 us (75%)
  matrix products  13.4 us (15%)
  local copies, waits for them, and re-layouts  6.49 us (7%)
    pallas_call x1, Pallas kernels, gather_gc(): pl.pallas_call(functools.partial(gather_kernel, n, line, n_gr), out_shape...  53 us
    pallas_call x1, Pallas kernels, reduce_gr(): pl.pallas_call(functools.partial(reduce_kernel, n), out_shape=jax.ShapeDt...  11.7 us
    unnamed x22, local copies, waits for them, and re-layouts  4.34 us
    dot_general x1, matrix products, row_product(): lax.dot_general(left_rows, right_rows, (((0,), (0,)), ((), ())), preferre...  3.13 us
    dot_general x1, matrix products, diag_solve(): left_side = jnp.dot(diag_inverse.T, symmetric, precision=highest)  2.33 us
    dot_general x1, matrix products, local(): lax.dot_general(grad_rows.reshape(tile_count, tile_rows, width), prior_fa...  2.25 us
    dot_general x1, matrix products, local(): lax.dot_general(own_grad, panel_factor.reshape(tile_count, own_rows, widt...  1.95 us

profile of v19, /device:TPU:1, one launch (start us, length us, event | category | flops | bytes accessed | tf_op | source)
XLA Modules:
  0.0 86.2 jit_solution(18367553010848149600)
XLA Ops:
  0.6 0.0 copy-start
  0.6 0.0 copy-start.7
  0.7 1.5 %copy.45 = bf16[8,8,2,128]{3,1,2,0:T(8,128)(2,1)} copy(bf16[8,8,2,128]{3,2,1,0:T(2,128)(2,1)} %bitcast.73) | data formatting | bytes 65536
  2.2 1.5 %convolution_convert_fusion.1 = bf16[31,2,512]{2,0,1:T(8,128)(2,1)S(1)} fusion(f32[512,512]{1,0:T(8,128)} %param.13, bf16[31,2,512]{2,1,0:T(2,128)(2,1)} %bitcast.70), kind=kOutput, calls=%fused_computation.9 | convolution fusion | flops 32799744 | bytes 1175552 | tf_op jit(solution)/shard_map/dot_general | solution.py:395
  3.7 0.7 copy.46
  4.4 0.1 copy.26
  4.4 0.8 convert.7
  5.2 2.0 %fusion.5 = bf16[512,512]{1,0:T(8,128)(2,1)} fusion(bf16[31,2,512]{2,1,0:T(2,128)(2,1)} %bitcast.71, bf16[31,2,512]{2,1,0:T(2,128)(2,1)S(1)} %copy.26), kind=kOutput, calls=%fused_computation.7 | convolution fusion | flops 32768000 | bytes 651264 | tf_op jit(solution)/shard_map/dot_general | solution.py:402
  7.2 53.0 %shard_map.120 = (bf16[31,1,64,512]{3,2,1,0:T(8,128)(2,1)}, bf16[32,16,512]{2,1,0:T(8,128)(2,1)}, bf16[8,64,256]{2,1,0:T(8,128)(2,1)}) custom-call(bf16[31,1,2,512]{3,2,1,0:T(2,128)(2,1)} %bitcast.67, bf16[32,16,512]{2,1,0:T(8,128)(2,1)} %bitcast.64, bf16[64,256]{1,0:T(8,128)(2,1)} %bitcast.69), custom_call_target="tpu_custom_call" | custom-call | tf_op jit(solution)/shard_map/pallas_call | solution.py:278
  60.2 0.0 copy-done.7
  60.2 0.0 copy-start.4
  60.2 0.0 copy-start.8
  60.2 3.1 %convolution_convert_fusion.crossing_ref = bf16[512,256]{1,0:T(8,128)(2,1)} fusion(bf16[1984,512]{1,0:T(8,128)(2,1)} %bitcast.75, bf16[248,8,2,128]{3,2,1,0:T(2,128)(2,1)S(1)} %bitcast.76), kind=kOutput, calls=%fused_computation.8 | convolution fusion | flops 520224768 | bytes 3309568 | tf_op jit(solution)/shard_map/dot_general | solution.py:14
  63.3 11.7 %shard_map.121 = f32[64,256]{1,0:T(8,128)} custom-call(bf16[512,256]{1,0:T(8,128)(2,1)} %convolution_convert_fusion.crossing_ref), custom_call_target="tpu_custom_call" | custom-call | tf_op jit(solution)/shard_map/pallas_call | solution.py:354
  75.1 0.0 copy-done.4
  75.1 0.1 reshape.52
  75.1 0.0 copy-done.8
  75.1 2.3 %fusion.2 = bf16[31,1,64,2,1,128]{5,2,3,0,4,1:T(8,128)(2,1)S(1)} fusion(bf16[31,1,64,512]{3,2,1,0:T(8,128)(2,1)} %get-tuple-element.7, bf16[31,1,64,2,1,128]{5,3,4,2,1,0:T(2,128)(2,1)S(1)} %copy-done.8, bf16[512,2,128]{2,1,0:T(2,128)(2,1)S(1)} %reshape.52), kind=kOutput, calls=%fused_computation.3 | convolution fusion | flops 521617408 | bytes 4325376 | tf_op jit(solution)/shard_map/dot_general | solution.py:424
  77.4 0.0 copy-start.3
  77.4 0.0 copy-start.5
  77.4 2.0 %copy.20 = bf16[31,1,64,2,1,128]{5,3,4,2,1,0:T(2,128)(2,1)} copy(bf16[31,1,64,2,1,128]{5,2,3,0,4,1:T(8,128)(2,1)S(1)} %fusion.2) | data formatting | bytes 2031616
  79.4 0.0 copy-done
  79.4 0.0 copy-done.3
  79.4 0.0 copy-done.5
  79.5 1.1 %fusion.17 = f32[512,512]{1,0:T(8,128)S(1)} fusion(f32[512,512]{1,0:T(8,128)S(1)} %copy-done, f32[512,512]{1,0:T(8,128)S(1)} %copy-done.3, bf16[512,512]{1,0:T(8,128)(2,1)S(1)} %bitcast.66), kind=kOutput, calls=%fused_computation.21 | convolution fusion | flops 806354944 | bytes 3670016 | tf_op jit(solution)/shard_map/dot_general | solution.py:21
  80.5 1.3 %copy.19 = f32[512,512]{0,1:T(8,128)} copy(f32[512,512]{1,0:T(8,128)S(1)} %fusion.17) | data formatting | bytes 2097152 | tf_op jit(solution)/shard_map/dot_general | solution.py:21
  81.8 2.3 %fusion.11 = f32[512,512]{1,0:T(8,128)S(1)} fusion(f32[512,512]{1,0:T(8,128)S(1)} %copy-done.1, f32[512,512]{1,0:T(8,128)S(1)} %fusion.17, f32[512,512]{0,1:T(8,128)} %copy.19), kind=kOutput, calls=%fused_computation.16 | convolution fusion | flops 808976384 | bytes 4194304 | tf_op jit(solution)/shard_map/dot_general | solution.py:30
  84.2 1.0 %fusion.40 = f32[512,512]{1,0:T(8,128)S(1)} fusion(f32[512,512]{1,0:T(8,128)S(1)} %fusion.11, f32[512,512]{1,0:T(8,128)S(1)} %copy-done.1), kind=kOutput, calls=%fused_computation.50 | convolution fusion | flops 805306368 | bytes 3145728 | tf_op jit(solution)/shard_map/dot_general | solution.py:31
  85.2 0.0 copy-start.2
  85.2 0.2 fusion.6
  85.4 0.8 reshape.57
  86.2 0.0 copy-done.2
  (4 shorter events, 0.0 us)
Async XLA Ops:
  0.6 78.8 %copy-start = (f32[512,512]{1,0:T(8,128)S(1)}, f32[512,512]{1,0:T(8,128)}, u32[]{:S(2)}) copy-start(f32[512,512]{1,0:T(8,128)} %param.12) | copy-start | bytes 3145732
  0.6 59.5 %copy-start.7 = (bf16[31,1,64,2,1,128]{5,3,4,2,1,0:T(2,128)(2,1)S(1)}, bf16[31,1,64,2,1,128]{5,3,4,2,1,0:T(2,128)(2,1)}, u32[]{:S(2)}) copy-start(bf16[31,1,64,2,1,128]{5,3,4,2,1,0:T(2,128)(2,1)} %param.9) | copy-start | bytes 3047428
  60.2 14.9 %copy-start.4 = (bf16[8,64,256]{2,1,0:T(8,128)(2,1)S(1)}, bf16[8,64,256]{2,1,0:T(8,128)(2,1)}, u32[]{:S(2)}) copy-start(bf16[8,64,256]{2,1,0:T(8,128)(2,1)} %get-tuple-element.8) | copy-start | bytes 786436
  60.2 14.9 %copy-start.8 = (bf16[31,1,64,2,1,128]{5,3,4,2,1,0:T(2,128)(2,1)S(1)}, bf16[31,1,64,2,1,128]{5,3,4,2,1,0:T(2,128)(2,1)}, u32[]{:S(2)}) copy-start(bf16[31,1,64,2,1,128]{5,3,4,2,1,0:T(2,128)(2,1)} %param.14) | copy-start | bytes 3047428
  77.4 2.0 %copy-start.3 = (f32[512,512]{1,0:T(8,128)S(1)}, f32[512,512]{1,0:T(8,128)}, u32[]{:S(2)}) copy-start(f32[512,512]{1,0:T(8,128)} %param.17) | copy-start | bytes 3145732
  77.4 2.0 %copy-start.5 = (bf16[32,16,512]{2,1,0:T(8,128)(2,1)S(1)}, bf16[32,16,512]{2,1,0:T(8,128)(2,1)}, u32[]{:S(2)}) copy-start(bf16[32,16,512]{2,1,0:T(8,128)(2,1)} %get-tuple-element.9) | copy-start | bytes 1572868
  79.4 2.4 %copy-start.1 = (f32[512,512]{1,0:T(8,128)S(1)}, f32[512,512]{1,0:T(8,128)}, u32[]{:S(2)}) copy-start(f32[512,512]{1,0:T(8,128)} %param.13) | copy-start | bytes 3145732
  84.2 1.0 %copy-start.6 = (f32[64,256]{1,0:T(8,128)S(1)}, f32[64,256]{1,0:T(8,128)}, u32[]{:S(2)}) copy-start(f32[64,256]{1,0:T(8,128)} %shard_map.121) | copy-start | bytes 196612
  85.2 1.0 %copy-start.2 = (f32[512,512]{1,0:T(8,128)}, f32[512,512]{1,0:T(8,128)S(1)}, u32[]{:S(2)}) copy-start(f32[512,512]{1,0:T(8,128)S(1)} %fusion.40) | copy-start | bytes 3145732

commit v20 on v19

--- a/solution.py
+++ b/solution.py
@@ -40,7 +40,7 @@
 
 
 def gather_kernel(n, line, n_gr, x_ref, p_ref, prior_ref, out_ref, cross_out, prior_out, precv, recv_piece,
-                  cross_slots, prior_slots, psems, sems, local_sem):
+                  cross_slots, psems, sems, local_sem):
     me = lax.axis_index("gc")
     row = lax.axis_index("gr")
     rows = x_ref.shape[2]
@@ -219,7 +219,7 @@
     def prior_copy(k, sender):
         return pltpu.make_async_remote_copy(
             src_ref=prior_ref,
-            dst_ref=prior_slots.at[sender],
+            dst_ref=prior_out.at[sender],
             send_sem=psems.at[6, k],
             recv_sem=psems.at[7, sender],
             device_id=(lax.rem(row + k, n_gr), me),
@@ -231,7 +231,8 @@
         return carry
 
     lax.fori_loop(1, n_gr, send_prior, 0)
-    prior_slots[row] = prior_ref[...]
+    own_prior = pltpu.make_async_copy(prior_ref, prior_out.at[row], psems.at[6, 0])
+    own_prior.start()
 
     def wait_first(k, carry):
         first(k, pos).wait_send()
@@ -269,7 +270,7 @@
         return carry
 
     lax.fori_loop(1, n_gr, wait_prior, 0)
-    prior_out[...] = prior_slots[...]
+    own_prior.wait()
 
 
 def gather_gc(block, part, prior_rows, n, line, n_gr):
@@ -282,13 +283,12 @@
             jax.ShapeDtypeStruct(part.shape, jnp.bfloat16),
             jax.ShapeDtypeStruct((n_gr,) + prior_rows.shape, prior_rows.dtype),
         ),
-        in_specs=[pl.BlockSpec(memory_space=pl.ANY), vmem, vmem],
-        out_specs=(pl.BlockSpec(memory_space=pl.ANY), vmem, vmem),
+        in_specs=[pl.BlockSpec(memory_space=pl.ANY), vmem, pl.BlockSpec(memory_space=pl.ANY)],
+        out_specs=(pl.BlockSpec(memory_space=pl.ANY), vmem, pl.BlockSpec(memory_space=pl.ANY)),
         scratch_shapes=[
             pltpu.VMEM(part.shape, part.dtype),
             pltpu.VMEM((n_gr,) + part.shape[1:], jnp.float32),
             pltpu.VMEM(part.shape, jnp.bfloat16),
-            pltpu.VMEM((n_gr,) + prior_rows.shape, prior_rows.dtype),
             pltpu.SemaphoreType.DMA((8, max(n, n_gr))),
             pltpu.SemaphoreType.DMA((2 + line, line + n // line)),
             pltpu.SemaphoreType.DMA,
@@ -405,7 +405,7 @@
         (((0, 1), (0, 1)), ((), ())),
         preferred_element_type=jnp.float32,
     ).astype(jnp.bfloat16)
-    prior_here = prior_factor.reshape(prior_local, local_cols)
+    prior_here = prior_factor.reshape(prior_local, below_factor.shape[3], below_factor.shape[5])
     whole, cross_rows, prior_rows = gather_gc(
         panel_grad,
         own_part.reshape(n_gc, width // n_gc, width),

time: 86.6 us -> 84.7 us (0.978)
  local copies, waits for them, and re-layouts: 6.49 us -> 4.9 us
    dot_general x1, matrix products: 2.25 us -> 0.69 us  [local(): lax.dot_general(grad_rows.reshape(tile_count, tile_rows, width), prior_fa...]
    unnamed x22 -> x21, local copies, waits for them, and re-layouts: 4.34 us -> 2.82 us
    dot_general x1, matrix products: 1.06 us -> 2.24 us  [diag_solve(): chol_proj = jnp.dot(diag_factor.T, diag_reduced, precision=highest)]
where the time goes in v20:
time: 84.7 us; the launch traced here: 84.3 us
  Pallas kernels  64.7 us (76%)
  matrix products  13.1 us (15%)
  local copies, waits for them, and re-layouts  4.9 us (6%)
    pallas_call x1, Pallas kernels, gather_gc(): pl.pallas_call(functools.partial(gather_kernel, n, line, n_gr), out_shape...  52.9 us
    pallas_call x1, Pallas kernels, reduce_gr(): pl.pallas_call(functools.partial(reduce_kernel, n), out_shape=jax.ShapeDt...  11.7 us
    dot_general x1, matrix products, row_product(): lax.dot_general(left_rows, right_rows, (((0,), (0,)), ((), ())), preferre...  3.12 us
    unnamed x21, local copies, waits for them, and re-layouts  2.82 us
    dot_general x1, matrix products, diag_solve(): left_side = jnp.dot(diag_inverse.T, symmetric, precision=highest)  2.33 us
    dot_general x1, matrix products, diag_solve(): chol_proj = jnp.dot(diag_factor.T, diag_reduced, precision=highest)  2.24 us
    dot_general x1, matrix products, local(): lax.dot_general(own_grad, panel_factor.reshape(tile_count, own_rows, widt...  1.95 us

profile of v20, /device:TPU:1, one launch (start us, length us, event | category | flops | bytes accessed | tf_op | source)
XLA Modules:
  0.0 84.3 jit_solution(9218212186545916442)
XLA Ops:
  0.6 0.0 copy-start
  0.6 0.0 copy-start.7
  0.7 1.6 %convolution_convert_fusion.1 = bf16[31,2,512]{2,0,1:T(8,128)(2,1)S(1)} fusion(f32[512,512]{1,0:T(8,128)} %param.13, bf16[31,2,512]{2,1,0:T(2,128)(2,1)} %bitcast.69), kind=kOutput, calls=%fused_computation.9 | convolution fusion | flops 32799744 | bytes 1175552 | tf_op jit(solution)/shard_map/dot_general | solution.py:395
  2.3 0.7 copy.48
  3.0 0.1 copy.26
  3.0 0.8 convert.7
  3.8 1.9 %fusion.5 = bf16[512,512]{1,0:T(8,128)(2,1)} fusion(bf16[31,2,512]{2,1,0:T(2,128)(2,1)} %bitcast.70, bf16[31,2,512]{2,1,0:T(2,128)(2,1)S(1)} %copy.26), kind=kOutput, calls=%fused_computation.7 | convolution fusion | flops 32768000 | bytes 651264 | tf_op jit(solution)/shard_map/dot_general | solution.py:402
  5.8 52.9 %shard_map.120 = (bf16[31,1,64,512]{3,2,1,0:T(8,128)(2,1)}, bf16[32,16,512]{2,1,0:T(8,128)(2,1)}, bf16[8,64,2,128]{3,2,1,0:T(2,128)(2,1)}) custom-call(bf16[31,1,2,512]{3,2,1,0:T(2,128)(2,1)} %bitcast.67, bf16[32,16,512]{2,1,0:T(8,128)(2,1)} %bitcast.63, bf16[64,2,128]{2,1,0:T(2,128)(2,1)} %bitcast.72), custom_call_target="tpu_custom_call" | custom-call | tf_op jit(solution)/shard_map/pallas_call | solution.py:279
  58.7 0.0 copy-done.7
  58.7 0.0 copy-start.3
  58.7 3.1 %convolution_convert_fusion.crossing_ref = bf16[512,256]{1,0:T(8,128)(2,1)} fusion(bf16[1984,512]{1,0:T(8,128)(2,1)} %bitcast.74, bf16[248,8,2,128]{3,2,1,0:T(2,128)(2,1)S(1)} %bitcast.75), kind=kOutput, calls=%fused_computation.8 | convolution fusion | flops 520224768 | bytes 3309568 | tf_op jit(solution)/shard_map/dot_general | solution.py:14
  61.9 11.7 %shard_map.121 = f32[64,256]{1,0:T(8,128)} custom-call(bf16[512,256]{1,0:T(8,128)(2,1)} %convolution_convert_fusion.crossing_ref), custom_call_target="tpu_custom_call" | custom-call | tf_op jit(solution)/shard_map/pallas_call | solution.py:354
  73.6 0.0 copy-done
  73.6 0.0 copy-done.3
  73.6 0.0 copy-start.6
  73.6 0.0 copy-start.8
  73.6 2.2 %fusion.17 = f32[512,512]{1,0:T(8,128)S(1)} fusion(f32[512,512]{1,0:T(8,128)S(1)} %copy-done, f32[512,512]{1,0:T(8,128)S(1)} %copy-done.3, bf16[512,512]{1,0:T(8,128)(2,1)} %bitcast.64), kind=kOutput, calls=%fused_computation.21 | convolution fusion | flops 806354944 | bytes 3670016 | tf_op jit(solution)/shard_map/dot_general | solution.py:21
  75.9 0.0 copy-done.5
  75.9 0.0 copy-done.6
  75.9 0.0 copy-done.8
  75.9 0.7 fusion.2
  76.6 0.0 copy-start.1
  76.6 2.0 %copy.20 = bf16[31,1,64,2,1,128]{5,3,4,2,1,0:T(2,128)(2,1)} copy(bf16[31,1,64,2,1,128]{5,2,3,0,4,1:T(8,128)(2,1)S(1)} %fusion.2) | data formatting | bytes 2031616
  78.6 1.3 %copy.19 = f32[512,512]{0,1:T(8,128)} copy(f32[512,512]{1,0:T(8,128)S(1)} %fusion.17) | data formatting | bytes 2097152 | tf_op jit(solution)/shard_map/dot_general | solution.py:21
  79.9 0.0 copy-done.1
  80.0 2.3 %fusion.11 = f32[512,512]{1,0:T(8,128)S(1)} fusion(f32[512,512]{1,0:T(8,128)S(1)} %copy-done.1, f32[512,512]{1,0:T(8,128)S(1)} %fusion.17, f32[512,512]{0,1:T(8,128)} %copy.19), kind=kOutput, calls=%fused_computation.16 | convolution fusion | flops 808976384 | bytes 4194304 | tf_op jit(solution)/shard_map/dot_general | solution.py:30
  82.3 0.0 copy-start.4
  82.3 1.0 %fusion.42 = f32[512,512]{1,0:T(8,128)S(1)} fusion(f32[512,512]{1,0:T(8,128)S(1)} %fusion.11, f32[512,512]{1,0:T(8,128)S(1)} %copy-done.1), kind=kOutput, calls=%fused_computation.51 | convolution fusion | flops 805306368 | bytes 3145728 | tf_op jit(solution)/shard_map/dot_general | solution.py:31
  83.3 0.0 copy-start.2
  83.4 0.2 fusion.6
  83.5 0.8 reshape.57
  84.3 0.0 copy-done.2
  (2 shorter events, 0.0 us)
Async XLA Ops:
  0.6 73.0 %copy-start = (f32[512,512]{1,0:T(8,128)S(1)}, f32[512,512]{1,0:T(8,128)}, u32[]{:S(2)}) copy-start(f32[512,512]{1,0:T(8,128)} %param.12) | copy-start | bytes 3145732
  0.6 58.1 %copy-start.7 = (bf16[31,1,64,2,1,128]{5,3,4,2,1,0:T(2,128)(2,1)S(1)}, bf16[31,1,64,2,1,128]{5,3,4,2,1,0:T(2,128)(2,1)}, u32[]{:S(2)}) copy-start(bf16[31,1,64,2,1,128]{5,3,4,2,1,0:T(2,128)(2,1)} %param.9) | copy-start | bytes 3047428
  58.7 14.9 %copy-start.3 = (f32[512,512]{1,0:T(8,128)S(1)}, f32[512,512]{1,0:T(8,128)}, u32[]{:S(2)}) copy-start(f32[512,512]{1,0:T(8,128)} %param.17) | copy-start | bytes 3145732
  61.9 14.0 %copy-start.5 = (bf16[8,64,2,128]{3,2,1,0:T(2,128)(2,1)S(1)}, bf16[8,64,2,128]{3,2,1,0:T(2,128)(2,1)}, u32[]{:S(2)}) copy-start(bf16[8,64,2,128]{3,2,1,0:T(2,128)(2,1)} %get-tuple-element.8) | copy-start | bytes 786436
  73.6 2.3 %copy-start.6 = (bf16[31,1,64,512]{3,2,1,0:T(8,128)(2,1)S(1)}, bf16[31,1,64,512]{3,2,1,0:T(8,128)(2,1)}, u32[]{:S(2)}) copy-start(bf16[31,1,64,512]{3,2,1,0:T(8,128)(2,1)} %get-tuple-element.7) | copy-start | bytes 6094852
  73.6 2.3 %copy-start.8 = (bf16[31,1,64,2,1,128]{5,3,4,2,1,0:T(2,128)(2,1)S(1)}, bf16[31,1,64,2,1,128]{5,3,4,2,1,0:T(2,128)(2,1)}, u32[]{:S(2)}) copy-start(bf16[31,1,64,2,1,128]{5,3,4,2,1,0:T(2,128)(2,1)} %param.14) | copy-start | bytes 3047428
  76.6 3.3 %copy-start.1 = (f32[512,512]{1,0:T(8,128)S(1)}, f32[512,512]{1,0:T(8,128)}, u32[]{:S(2)}) copy-start(f32[512,512]{1,0:T(8,128)} %param.13) | copy-start | bytes 3145732
  82.3 1.0 %copy-start.4 = (f32[64,256]{1,0:T(8,128)S(1)}, f32[64,256]{1,0:T(8,128)}, u32[]{:S(2)}) copy-start(f32[64,256]{1,0:T(8,128)} %shard_map.121) | copy-start | bytes 196612
  83.3 1.0 %copy-start.2 = (f32[512,512]{1,0:T(8,128)}, f32[512,512]{1,0:T(8,128)S(1)}, u32[]{:S(2)}) copy-start(f32[512,512]{1,0:T(8,128)S(1)} %fusion.42) | copy-start | bytes 3145732

commit v21 on v20

--- a/solution.py
+++ b/solution.py
@@ -56,9 +56,7 @@
         return lax.rem(grp + k, lines) * line + pos
 
     part_rows, part_width = p_ref.shape[1], p_ref.shape[2]
-    precv[...] = jnp.zeros(precv.shape, precv.dtype)
-    recv_piece[...] = jnp.zeros(recv_piece.shape, recv_piece.dtype)
-    cross_slots[...] = jnp.zeros(cross_slots.shape, cross_slots.dtype)
+    kept = lax.broadcasted_iota(jnp.int32, p_ref.shape[1:], 1) < 128 * ((p_ref.shape[1] * (me + 1) - 1) // 128 + 1)
     barrier = pltpu.get_barrier_semaphore()
 
     def greet(k, carry):
@@ -156,7 +154,7 @@
         return total + precv[j].astype(jnp.float32)
 
     piece = lax.fori_loop(0, n, add_part, jnp.zeros(recv_piece.shape[1:], jnp.float32))
-    recv_piece[row] = piece
+    recv_piece[row] = jnp.where(kept, piece, 0.0)
 
     def piece_copy(k, sender, cols):
         return pltpu.make_async_remote_copy(
@@ -198,7 +196,7 @@
         return total + recv_piece[j]
 
     summed = lax.fori_loop(0, n_gr, add_piece, jnp.zeros(recv_piece.shape[1:], jnp.float32))
-    cross_slots[me] = summed.astype(cross_slots.dtype)
+    cross_slots[me] = jnp.where(kept, summed, 0.0).astype(cross_slots.dtype)
 
     def cross_copy(k, sender, cols):
         return pltpu.make_async_remote_copy(

time: 84.7 us -> 84.3 us (level)
  no operation moved by 1% of the time
where the time goes in v21:
time: 84.3 us; the launch traced here: 84 us
  Pallas kernels  64.4 us (76%)
  matrix products  13.1 us (16%)
  local copies, waits for them, and re-layouts  4.9 us (6%)
    pallas_call x1, Pallas kernels, gather_gc(): pl.pallas_call(functools.partial(gather_kernel, n, line, n_gr), out_shape...  52.6 us
    pallas_call x1, Pallas kernels, reduce_gr(): pl.pallas_call(functools.partial(reduce_kernel, n), out_shape=jax.ShapeDt...  11.7 us
    dot_general x1, matrix products, row_product(): lax.dot_general(left_rows, right_rows, (((0,), (0,)), ((), ())), preferre...  3.12 us
    unnamed x21, local copies, waits for them, and re-layouts  2.82 us
    dot_general x1, matrix products, diag_solve(): left_side = jnp.dot(diag_inverse.T, symmetric, precision=highest)  2.33 us
    dot_general x1, matrix products, diag_solve(): chol_proj = jnp.dot(diag_factor.T, diag_reduced, precision=highest)  2.24 us
    dot_general x1, matrix products, local(): lax.dot_general(own_grad, panel_factor.reshape(tile_count, own_rows, widt...  1.95 us

profile of v21, /device:TPU:1, one launch (start us, length us, event | category | flops | bytes accessed | tf_op | source)
XLA Modules:
  0.0 84.0 jit_solution(8128331334616350065)
XLA Ops:
  0.6 0.0 copy-start
  0.6 0.0 copy-start.7
  0.7 1.6 %convolution_convert_fusion.1 = bf16[31,2,512]{2,0,1:T(8,128)(2,1)S(1)} fusion(f32[512,512]{1,0:T(8,128)} %param.13, bf16[31,2,512]{2,1,0:T(2,128)(2,1)} %bitcast.69), kind=kOutput, calls=%fused_computation.9 | convolution fusion | flops 32799744 | bytes 1175552 | tf_op jit(solution)/shard_map/dot_general | solution.py:393
  2.3 0.7 copy.48
  3.0 0.1 copy.26
  3.0 0.8 convert.7
  3.8 1.9 %fusion.5 = bf16[512,512]{1,0:T(8,128)(2,1)} fusion(bf16[31,2,512]{2,1,0:T(2,128)(2,1)} %bitcast.70, bf16[31,2,512]{2,1,0:T(2,128)(2,1)S(1)} %copy.26), kind=kOutput, calls=%fused_computation.7 | convolution fusion | flops 32768000 | bytes 651264 | tf_op jit(solution)/shard_map/dot_general | solution.py:400
  5.8 52.6 %shard_map.120 = (bf16[31,1,64,512]{3,2,1,0:T(8,128)(2,1)}, bf16[32,16,512]{2,1,0:T(8,128)(2,1)}, bf16[8,64,2,128]{3,2,1,0:T(2,128)(2,1)}) custom-call(bf16[31,1,2,512]{3,2,1,0:T(2,128)(2,1)} %bitcast.67, bf16[32,16,512]{2,1,0:T(8,128)(2,1)} %bitcast.63, bf16[64,2,128]{2,1,0:T(2,128)(2,1)} %bitcast.72), custom_call_target="tpu_custom_call" | custom-call | tf_op jit(solution)/shard_map/pallas_call | solution.py:277
  58.4 0.0 copy-done.7
  58.4 0.0 copy-start.3
  58.4 3.1 %convolution_convert_fusion.crossing_ref = bf16[512,256]{1,0:T(8,128)(2,1)} fusion(bf16[1984,512]{1,0:T(8,128)(2,1)} %bitcast.74, bf16[248,8,2,128]{3,2,1,0:T(2,128)(2,1)S(1)} %bitcast.75), kind=kOutput, calls=%fused_computation.8 | convolution fusion | flops 520224768 | bytes 3309568 | tf_op jit(solution)/shard_map/dot_general | solution.py:14
  61.6 11.7 %shard_map.121 = f32[64,256]{1,0:T(8,128)} custom-call(bf16[512,256]{1,0:T(8,128)(2,1)} %convolution_convert_fusion.crossing_ref), custom_call_target="tpu_custom_call" | custom-call | tf_op jit(solution)/shard_map/pallas_call | solution.py:352
  73.3 0.0 copy-done
  73.3 0.0 copy-done.3
  73.3 0.0 copy-start.6
  73.3 0.0 copy-start.8
  73.3 2.2 %fusion.17 = f32[512,512]{1,0:T(8,128)S(1)} fusion(f32[512,512]{1,0:T(8,128)S(1)} %copy-done, f32[512,512]{1,0:T(8,128)S(1)} %copy-done.3, bf16[512,512]{1,0:T(8,128)(2,1)} %bitcast.64), kind=kOutput, calls=%fused_computation.21 | convolution fusion | flops 806354944 | bytes 3670016 | tf_op jit(solution)/shard_map/dot_general | solution.py:21
  75.6 0.0 copy-done.5
  75.6 0.0 copy-done.6
  75.6 0.0 copy-done.8
  75.6 0.7 fusion.2
  76.3 0.0 copy-start.1
  76.3 2.0 %copy.20 = bf16[31,1,64,2,1,128]{5,3,4,2,1,0:T(2,128)(2,1)} copy(bf16[31,1,64,2,1,128]{5,2,3,0,4,1:T(8,128)(2,1)S(1)} %fusion.2) | data formatting | bytes 2031616
  78.3 1.3 %copy.19 = f32[512,512]{0,1:T(8,128)} copy(f32[512,512]{1,0:T(8,128)S(1)} %fusion.17) | data formatting | bytes 2097152 | tf_op jit(solution)/shard_map/dot_general | solution.py:21
  79.6 0.0 copy-done.1
  79.6 2.3 %fusion.11 = f32[512,512]{1,0:T(8,128)S(1)} fusion(f32[512,512]{1,0:T(8,128)S(1)} %copy-done.1, f32[512,512]{1,0:T(8,128)S(1)} %fusion.17, f32[512,512]{0,1:T(8,128)} %copy.19), kind=kOutput, calls=%fused_computation.16 | convolution fusion | flops 808976384 | bytes 4194304 | tf_op jit(solution)/shard_map/dot_general | solution.py:30
  82.0 0.0 copy-start.4
  82.0 1.0 %fusion.42 = f32[512,512]{1,0:T(8,128)S(1)} fusion(f32[512,512]{1,0:T(8,128)S(1)} %fusion.11, f32[512,512]{1,0:T(8,128)S(1)} %copy-done.1), kind=kOutput, calls=%fused_computation.51 | convolution fusion | flops 805306368 | bytes 3145728 | tf_op jit(solution)/shard_map/dot_general | solution.py:31
  83.0 0.0 copy-start.2
  83.0 0.2 fusion.6
  83.2 0.8 reshape.57
  84.0 0.0 copy-done.2
  (2 shorter events, 0.0 us)
Async XLA Ops:
  0.6 72.7 %copy-start = (f32[512,512]{1,0:T(8,128)S(1)}, f32[512,512]{1,0:T(8,128)}, u32[]{:S(2)}) copy-start(f32[512,512]{1,0:T(8,128)} %param.12) | copy-start | bytes 3145732
  0.6 57.8 %copy-start.7 = (bf16[31,1,64,2,1,128]{5,3,4,2,1,0:T(2,128)(2,1)S(1)}, bf16[31,1,64,2,1,128]{5,3,4,2,1,0:T(2,128)(2,1)}, u32[]{:S(2)}) copy-start(bf16[31,1,64,2,1,128]{5,3,4,2,1,0:T(2,128)(2,1)} %param.9) | copy-start | bytes 3047428
  58.4 14.9 %copy-start.3 = (f32[512,512]{1,0:T(8,128)S(1)}, f32[512,512]{1,0:T(8,128)}, u32[]{:S(2)}) copy-start(f32[512,512]{1,0:T(8,128)} %param.17) | copy-start | bytes 3145732
  61.6 14.0 %copy-start.5 = (bf16[8,64,2,128]{3,2,1,0:T(2,128)(2,1)S(1)}, bf16[8,64,2,128]{3,2,1,0:T(2,128)(2,1)}, u32[]{:S(2)}) copy-start(bf16[8,64,2,128]{3,2,1,0:T(2,128)(2,1)} %get-tuple-element.8) | copy-start | bytes 786436
  73.3 2.3 %copy-start.6 = (bf16[31,1,64,512]{3,2,1,0:T(8,128)(2,1)S(1)}, bf16[31,1,64,512]{3,2,1,0:T(8,128)(2,1)}, u32[]{:S(2)}) copy-start(bf16[31,1,64,512]{3,2,1,0:T(8,128)(2,1)} %get-tuple-element.7) | copy-start | bytes 6094852
  73.3 2.3 %copy-start.8 = (bf16[31,1,64,2,1,128]{5,3,4,2,1,0:T(2,128)(2,1)S(1)}, bf16[31,1,64,2,1,128]{5,3,4,2,1,0:T(2,128)(2,1)}, u32[]{:S(2)}) copy-start(bf16[31,1,64,2,1,128]{5,3,4,2,1,0:T(2,128)(2,1)} %param.14) | copy-start | bytes 3047428
  76.3 3.3 %copy-start.1 = (f32[512,512]{1,0:T(8,128)S(1)}, f32[512,512]{1,0:T(8,128)}, u32[]{:S(2)}) copy-start(f32[512,512]{1,0:T(8,128)} %param.13) | copy-start | bytes 3145732
  82.0 1.0 %copy-start.4 = (f32[64,256]{1,0:T(8,128)S(1)}, f32[64,256]{1,0:T(8,128)}, u32[]{:S(2)}) copy-start(f32[64,256]{1,0:T(8,128)} %shard_map.121) | copy-start | bytes 196612
  83.0 1.0 %copy-start.2 = (f32[512,512]{1,0:T(8,128)}, f32[512,512]{1,0:T(8,128)S(1)}, u32[]{:S(2)}) copy-start(f32[512,512]{1,0:T(8,128)S(1)} %fusion.42) | copy-start | bytes 3145732

commit v22 on v21

--- a/solution.py
+++ b/solution.py
@@ -88,6 +88,24 @@
 
     lax.fori_loop(1, n, send_parts, 0)
 
+    def prior_copy(k, sender):
+        return pltpu.make_async_remote_copy(
+            src_ref=prior_ref,
+            dst_ref=prior_out.at[sender],
+            send_sem=psems.at[6, k],
+            recv_sem=psems.at[7, sender],
+            device_id=(lax.rem(row + k, n_gr), me),
+            device_id_type=MESH_ID,
+        )
+
+    def send_prior(k, carry):
+        prior_copy(k, row).start()
+        return carry
+
+    lax.fori_loop(1, n_gr, send_prior, 0)
+    own_prior = pltpu.make_async_copy(prior_ref, prior_out.at[row], psems.at[6, 0])
+    own_prior.start()
+
     own = pltpu.make_async_copy(x_ref, out_ref.at[:, :, pl.ds(me * rows, rows), :], local_sem)
     own.start()
 
@@ -214,23 +232,6 @@
 
     lax.fori_loop(1, n, send_cross, 0)
 
-    def prior_copy(k, sender):
-        return pltpu.make_async_remote_copy(
-            src_ref=prior_ref,
-            dst_ref=prior_out.at[sender],
-            send_sem=psems.at[6, k],
-            recv_sem=psems.at[7, sender],
-            device_id=(lax.rem(row + k, n_gr), me),
-            device_id_type=MESH_ID,
-        )
-
-    def send_prior(k, carry):
-        prior_copy(k, row).start()
-        return carry
-
-    lax.fori_loop(1, n_gr, send_prior, 0)
-    own_prior = pltpu.make_async_copy(prior_ref, prior_out.at[row], psems.at[6, 0])
-    own_prior.start()
 
     def wait_first(k, carry):
         first(k, pos).wait_send()

time: 84.3 us -> 84.3 us (level)
  no operation moved by 1% of the time
where the time goes in v22:
time: 84.3 us; the launch traced here: 84 us
  Pallas kernels  64.3 us (76%)
  matrix products  13.1 us (16%)
  local copies, waits for them, and re-layouts  4.9 us (6%)
    pallas_call x1, Pallas kernels, gather_gc(): pl.pallas_call(functools.partial(gather_kernel, n, line, n_gr), out_shape...  52.6 us
    pallas_call x1, Pallas kernels, reduce_gr(): pl.pallas_call(functools.partial(reduce_kernel, n), out_shape=jax.ShapeDt...  11.7 us
    dot_general x1, matrix products, row_product(): lax.dot_general(left_rows, right_rows, (((0,), (0,)), ((), ())), preferre...  3.12 us
    unnamed x21, local copies, waits for them, and re-layouts  2.82 us
    dot_general x1, matrix products, diag_solve(): left_side = jnp.dot(diag_inverse.T, symmetric, precision=highest)  2.33 us
    dot_general x1, matrix products, diag_solve(): chol_proj = jnp.dot(diag_factor.T, diag_reduced, precision=highest)  2.24 us
    dot_general x1, matrix products, local(): lax.dot_general(own_grad, panel_factor.reshape(tile_count, own_rows, widt...  1.95 us

profile of v22, /device:TPU:1, one launch (start us, length us, event | category | flops | bytes accessed | tf_op | source)
XLA Modules:
  0.0 84.0 jit_solution(10332446724944161235)
XLA Ops:
  0.6 0.0 copy-start
  0.6 0.0 copy-start.7
  0.7 1.6 %convolution_convert_fusion.1 = bf16[31,2,512]{2,0,1:T(8,128)(2,1)S(1)} fusion(f32[512,512]{1,0:T(8,128)} %param.13, bf16[31,2,512]{2,1,0:T(2,128)(2,1)} %bitcast.69), kind=kOutput, calls=%fused_computation.9 | convolution fusion | flops 32799744 | bytes 1175552 | tf_op jit(solution)/shard_map/dot_general | solution.py:394
  2.3 0.7 copy.48
  3.0 0.1 copy.26
  3.0 0.8 convert.7
  3.8 1.9 %fusion.5 = bf16[512,512]{1,0:T(8,128)(2,1)} fusion(bf16[31,2,512]{2,1,0:T(2,128)(2,1)} %bitcast.70, bf16[31,2,512]{2,1,0:T(2,128)(2,1)S(1)} %copy.26), kind=kOutput, calls=%fused_computation.7 | convolution fusion | flops 32768000 | bytes 651264 | tf_op jit(solution)/shard_map/dot_general | solution.py:401
  5.8 52.6 %shard_map.120 = (bf16[31,1,64,512]{3,2,1,0:T(8,128)(2,1)}, bf16[32,16,512]{2,1,0:T(8,128)(2,1)}, bf16[8,64,2,128]{3,2,1,0:T(2,128)(2,1)}) custom-call(bf16[31,1,2,512]{3,2,1,0:T(2,128)(2,1)} %bitcast.67, bf16[32,16,512]{2,1,0:T(8,128)(2,1)} %bitcast.63, bf16[64,2,128]{2,1,0:T(2,128)(2,1)} %bitcast.72), custom_call_target="tpu_custom_call" | custom-call | tf_op jit(solution)/shard_map/pallas_call | solution.py:278
  58.4 0.0 copy-done.7
  58.4 0.0 copy-start.3
  58.4 3.1 %convolution_convert_fusion.crossing_ref = bf16[512,256]{1,0:T(8,128)(2,1)} fusion(bf16[1984,512]{1,0:T(8,128)(2,1)} %bitcast.74, bf16[248,8,2,128]{3,2,1,0:T(2,128)(2,1)S(1)} %bitcast.75), kind=kOutput, calls=%fused_computation.8 | convolution fusion | flops 520224768 | bytes 3309568 | tf_op jit(solution)/shard_map/dot_general | solution.py:14
  61.6 11.7 %shard_map.121 = f32[64,256]{1,0:T(8,128)} custom-call(bf16[512,256]{1,0:T(8,128)(2,1)} %convolution_convert_fusion.crossing_ref), custom_call_target="tpu_custom_call" | custom-call | tf_op jit(solution)/shard_map/pallas_call | solution.py:353
  73.3 0.0 copy-done
  73.3 0.0 copy-done.3
  73.3 0.0 copy-start.6
  73.3 0.0 copy-start.8
  73.3 2.2 %fusion.17 = f32[512,512]{1,0:T(8,128)S(1)} fusion(f32[512,512]{1,0:T(8,128)S(1)} %copy-done, f32[512,512]{1,0:T(8,128)S(1)} %copy-done.3, bf16[512,512]{1,0:T(8,128)(2,1)} %bitcast.64), kind=kOutput, calls=%fused_computation.21 | convolution fusion | flops 806354944 | bytes 3670016 | tf_op jit(solution)/shard_map/dot_general | solution.py:21
  75.6 0.0 copy-done.5
  75.6 0.0 copy-done.6
  75.6 0.0 copy-done.8
  75.6 0.7 fusion.2
  76.3 0.0 copy-start.1
  76.3 2.0 %copy.20 = bf16[31,1,64,2,1,128]{5,3,4,2,1,0:T(2,128)(2,1)} copy(bf16[31,1,64,2,1,128]{5,2,3,0,4,1:T(8,128)(2,1)S(1)} %fusion.2) | data formatting | bytes 2031616
  78.3 1.3 %copy.19 = f32[512,512]{0,1:T(8,128)} copy(f32[512,512]{1,0:T(8,128)S(1)} %fusion.17) | data formatting | bytes 2097152 | tf_op jit(solution)/shard_map/dot_general | solution.py:21
  79.6 0.0 copy-done.1
  79.6 2.3 %fusion.11 = f32[512,512]{1,0:T(8,128)S(1)} fusion(f32[512,512]{1,0:T(8,128)S(1)} %copy-done.1, f32[512,512]{1,0:T(8,128)S(1)} %fusion.17, f32[512,512]{0,1:T(8,128)} %copy.19), kind=kOutput, calls=%fused_computation.16 | convolution fusion | flops 808976384 | bytes 4194304 | tf_op jit(solution)/shard_map/dot_general | solution.py:30
  82.0 1.0 %fusion.42 = f32[512,512]{1,0:T(8,128)S(1)} fusion(f32[512,512]{1,0:T(8,128)S(1)} %fusion.11, f32[512,512]{1,0:T(8,128)S(1)} %copy-done.1), kind=kOutput, calls=%fused_computation.51 | convolution fusion | flops 805306368 | bytes 3145728 | tf_op jit(solution)/shard_map/dot_general | solution.py:31
  83.0 0.0 copy-done.4
  83.0 0.0 copy-start.2
  83.0 0.2 fusion.6
  83.2 0.8 reshape.57
  84.0 0.0 copy-done.2
  (2 shorter events, 0.0 us)
Async XLA Ops:
  0.6 72.6 %copy-start = (f32[512,512]{1,0:T(8,128)S(1)}, f32[512,512]{1,0:T(8,128)}, u32[]{:S(2)}) copy-start(f32[512,512]{1,0:T(8,128)} %param.12) | copy-start | bytes 3145732
  0.6 57.8 %copy-start.7 = (bf16[31,1,64,2,1,128]{5,3,4,2,1,0:T(2,128)(2,1)S(1)}, bf16[31,1,64,2,1,128]{5,3,4,2,1,0:T(2,128)(2,1)}, u32[]{:S(2)}) copy-start(bf16[31,1,64,2,1,128]{5,3,4,2,1,0:T(2,128)(2,1)} %param.9) | copy-start | bytes 3047428
  58.4 14.9 %copy-start.3 = (f32[512,512]{1,0:T(8,128)S(1)}, f32[512,512]{1,0:T(8,128)}, u32[]{:S(2)}) copy-start(f32[512,512]{1,0:T(8,128)} %param.17) | copy-start | bytes 3145732
  61.6 14.0 %copy-start.5 = (bf16[8,64,2,128]{3,2,1,0:T(2,128)(2,1)S(1)}, bf16[8,64,2,128]{3,2,1,0:T(2,128)(2,1)}, u32[]{:S(2)}) copy-start(bf16[8,64,2,128]{3,2,1,0:T(2,128)(2,1)} %get-tuple-element.8) | copy-start | bytes 786436
  73.3 2.3 %copy-start.6 = (bf16[31,1,64,512]{3,2,1,0:T(8,128)(2,1)S(1)}, bf16[31,1,64,512]{3,2,1,0:T(8,128)(2,1)}, u32[]{:S(2)}) copy-start(bf16[31,1,64,512]{3,2,1,0:T(8,128)(2,1)} %get-tuple-element.7) | copy-start | bytes 6094852
  73.3 2.3 %copy-start.8 = (bf16[31,1,64,2,1,128]{5,3,4,2,1,0:T(2,128)(2,1)S(1)}, bf16[31,1,64,2,1,128]{5,3,4,2,1,0:T(2,128)(2,1)}, u32[]{:S(2)}) copy-start(bf16[31,1,64,2,1,128]{5,3,4,2,1,0:T(2,128)(2,1)} %param.14) | copy-start | bytes 3047428
  76.3 3.3 %copy-start.1 = (f32[512,512]{1,0:T(8,128)S(1)}, f32[512,512]{1,0:T(8,128)}, u32[]{:S(2)}) copy-start(f32[512,512]{1,0:T(8,128)} %param.13) | copy-start | bytes 3145732
  82.0 1.0 %copy-start.4 = (f32[64,256]{1,0:T(8,128)S(1)}, f32[64,256]{1,0:T(8,128)}, u32[]{:S(2)}) copy-start(f32[64,256]{1,0:T(8,128)} %shard_map.121) | copy-start | bytes 196612
  83.0 1.0 %copy-start.2 = (f32[512,512]{1,0:T(8,128)}, f32[512,512]{1,0:T(8,128)S(1)}, u32[]{:S(2)}) copy-start(f32[512,512]{1,0:T(8,128)S(1)} %fusion.42) | copy-start | bytes 3145732
